TPU v7x, 32 devices: a whole 2x2x4 slice. The times are simulated.
32 devices in a mesh: row: 4 (over y, core), col: 8 (over z, x).
Axes of the slice: x: 2, y: 2, z: 4, core: 2. Of those that a mesh axis runs over, the one named last changes fastest.
Arguments:
- tokens: bfloat16 [16384, 768], P(('row', 'col')), may hold values from -6 to 6
- parents: int32 [4, 16], P('row'), may hold values from -1 to 14, as said below
- w_qkv: bfloat16 [768, 2304], P('row', 'col'), may hold values from -0.21875 to 0.21875
- w_out: bfloat16 [768, 768], P('row', 'col'), may hold values from -0.875 to 0.875
- w_up: bfloat16 [768, 3072], P('row', 'col'), may hold values from -0.21875 to 0.21875
- w_down: bfloat16 [3072, 768], P('row', 'col'), may hold values from -0.109375 to 0.109375
- ln_gain: bfloat16 [2, 768], P(None, 'col'), may hold values from 0.099609375 to 1.8984375
- ln_bias: bfloat16 [2, 768], P(None, 'col'), may hold values from -3 to 3
- proj_bias: bfloat16 [4, 768], P(None, 'col'), may hold values from -3 to 3
- ff_bias: bfloat16 [3072], P('col'), may hold values from -3 to 3
- cotangent: bfloat16 [16384, 768], P(('row', 'col')), may hold values from -6 to 6
Outputs:
- output: bfloat16 [16384, 768], P(('row', 'col'))
- grad_tokens: bfloat16 [16384, 768], P(('row', 'col'))
- grad_w_qkv: float32 [768, 2304], P('row', 'col')
- grad_w_out: float32 [768, 768], P('row', 'col')
- grad_w_up: float32 [768, 3072], P('row', 'col')
- grad_w_down: float32 [3072, 768], P('row', 'col')
- grad_ln_gain: float32 [2, 768], P(None, 'col')
- grad_ln_bias: float32 [2, 768], P(None, 'col')
- grad_proj_bias: float32 [4, 768], P(None, 'col')
- grad_ff_bias: float32 [3072], P('col')
Inputs may be any that keep to these rules, and one draw needn't show every extreme that they name: `parents`: for each tree, segments 0 to 3 are the trunk: segment 0 has parent -1 and each other trunk segment continues the one before. The remaining segments are 4 branches that continue segment 4 - 1 and, for each branch, 2 leaves that continue it; segment 16 - 2 is a branch and segment 16 - 1 one of its leaves, the others come in any order.
All inputs are finite; a program needn't handle non-finite values.
Results may differ from a plain program's by a relative error of at most 0.017.
Values may be sent and summed in bfloat16 or wider, within the bound.
No kernel may reach another device: no remote copies, remote signals or barrier semaphores. Data moves between devices by JAX's collectives and lax.ppermute only.
A program may use at most 192 MiB of HBM per device.

v0:
```python
import jax
import jax.numpy as jnp
from jax import lax
from jax.sharding import PartitionSpec as P

D = 768
HEADS = 12
HEAD_DIM = 64
SEG = 256
SEGS = 16
TREE_TOKENS = 4096


EPSILON = 1e-12
NEGATIVE = -1e30


def layer_norm(values, scaling, shifting):
    centre = values - jnp.mean(values, axis=-1, keepdims=True)
    spread = jnp.mean(centre * centre, axis=-1, keepdims=True)
    return centre * lax.rsqrt(spread + EPSILON) * scaling + shifting


def exact_gelu(values):
    return jax.nn.gelu(values, approximate=False)


def ancestry(parents):
    segment_count = parents.shape[0]
    labels = jnp.arange(segment_count, dtype=jnp.int32)
    closure = jnp.eye(segment_count, dtype=jnp.float32) + (
        parents[:, None] == labels[None, :]
    ).astype(jnp.float32)
    for repeat in range(segment_count.bit_length()):
        closure = jnp.minimum(jnp.dot(closure, closure, precision=lax.Precision.HIGHEST), 1.0)
    return closure


def allowed(query_pos, key_pos, closure):
    labels = jnp.arange(closure.shape[0], dtype=jnp.int32)
    query_seg = query_pos // SEG
    key_seg = key_pos // SEG
    query_hot = (query_seg[:, None] == labels[None, :]).astype(jnp.float32)
    key_hot = (key_seg[:, None] == labels[None, :]).astype(jnp.float32)
    reach = jnp.dot(
        jnp.dot(query_hot, closure, precision=lax.Precision.HIGHEST),
        key_hot.T,
        precision=lax.Precision.HIGHEST,
    )
    causal = (query_seg[:, None] != key_seg[None, :]) | (key_pos[None, :] <= query_pos[:, None])
    return (reach > 0.5) & causal


def body(
    tokens, parents, w_qkv, w_out, w_up, w_down, ln_gain, ln_bias, proj_bias, ff_bias, cotangent
):
    local_rows = tokens.shape[0]
    score_scale = HEAD_DIM ** (-0.5)
    head_shape = (local_rows, HEADS, HEAD_DIM)
    block_rows = 2 * SEG
    block_count = SEGS // 2
    cols_qkv, cols_out, cols_up, cols_down, norm_gains, shifts, biases, ff_shift = (
        lax.all_gather(w_qkv, "col", axis=1, tiled=True),
        lax.all_gather(w_out, "col", axis=1, tiled=True),
        lax.all_gather(w_up, "col", axis=1, tiled=True),
        lax.all_gather(w_down, "col", axis=1, tiled=True),
        lax.all_gather(ln_gain, "col", axis=1, tiled=True),
        lax.all_gather(ln_bias, "col", axis=1, tiled=True),
        lax.all_gather(proj_bias, "col", axis=1, tiled=True),
        lax.all_gather(ff_bias, "col", axis=0, tiled=True),
    )
    full_qkv, full_out, full_up, full_down = (
        lax.all_gather(cols_qkv, "row", axis=0, tiled=True),
        lax.all_gather(cols_out, "row", axis=0, tiled=True),
        lax.all_gather(cols_up, "row", axis=0, tiled=True),
        lax.all_gather(cols_down, "row", axis=0, tiled=True),
    )
    norm_gains = norm_gains.astype(jnp.float32)
    shifts = shifts.astype(jnp.float32)
    biases = biases.astype(jnp.float32)
    ff_shift = ff_shift.astype(jnp.float32)
    inputs = tokens.astype(jnp.float32)
    normed_low = layer_norm(inputs, norm_gains[0], shifts[0]).astype(jnp.bfloat16)
    projected = jnp.dot(normed_low, full_qkv, preferred_element_type=jnp.float32)
    queries = (projected[:, :D] + biases[0]).astype(jnp.bfloat16).reshape(head_shape)
    keys_own = projected[:, D : 2 * D].astype(jnp.bfloat16).reshape(head_shape)
    values_own = (projected[:, 2 * D :] + biases[1]).astype(jnp.bfloat16).reshape(head_shape)
    keys_all, values_all = (
        lax.all_gather(keys_own, "col", axis=0, tiled=True),
        lax.all_gather(values_own, "col", axis=0, tiled=True),
    )
    key_blocks = keys_all.reshape(block_count, block_rows, HEADS, HEAD_DIM)
    value_blocks = values_all.reshape(block_count, block_rows, HEADS, HEAD_DIM)
    block_starts = jnp.arange(block_count, dtype=jnp.int32) * block_rows
    within = jnp.arange(block_rows, dtype=jnp.int32)
    query_pos = lax.axis_index("col") * local_rows + jnp.arange(local_rows, dtype=jnp.int32)
    closure = ancestry(parents[0])

    def scores_of(query_block, key_block, query_positions, key_positions):
        products = jnp.einsum(
            "qhd,khd->hqk", query_block, key_block, preferred_element_type=jnp.float32
        )
        return (products * score_scale, allowed(query_positions, key_positions, closure)[None])

    def probabilities(query_block, key_block, query_positions, key_positions, log_block):
        scores, visible = scores_of(query_block, key_block, query_positions, key_positions)
        return jnp.where(visible, jnp.exp(scores - log_block[..., None]), 0.0)

    def extent(running, pieces):
        highest_score, mass_total = running
        key_block, first_pos = pieces
        scores, visible = scores_of(queries, key_block, query_pos, first_pos + within)
        masked = jnp.where(visible, scores, NEGATIVE)
        new_highest = jnp.maximum(highest_score, jnp.max(masked, axis=-1))
        exp_terms = jnp.where(visible, jnp.exp(masked - new_highest[..., None]), 0.0)
        new_total = mass_total * jnp.exp(highest_score - new_highest) + jnp.sum(exp_terms, axis=-1)
        return ((new_highest, new_total), None)

    start_state = (
        jnp.full((HEADS, local_rows), NEGATIVE, jnp.float32),
        jnp.zeros((HEADS, local_rows), jnp.float32),
    )
    (highest_score, mass_total), unused = lax.scan(extent, start_state, (key_blocks, block_starts))
    log_total = highest_score + jnp.log(mass_total)

    def attend(running, pieces):
        key_block, value_block, first_pos = pieces
        chances = probabilities(
            queries, key_block, query_pos, first_pos + within, log_total
        ).astype(jnp.bfloat16)
        return (
            running
            + jnp.einsum("hqk,khd->qhd", chances, value_block, preferred_element_type=jnp.float32),
            None,
        )

    attended, unused = lax.scan(
        attend, jnp.zeros(head_shape, jnp.float32), (key_blocks, value_blocks, block_starts)
    )
    attended_low = attended.reshape(local_rows, D).astype(jnp.bfloat16)
    mixed_rows = (
        inputs + jnp.dot(attended_low, full_out, preferred_element_type=jnp.float32) + biases[2]
    )
    second_low = layer_norm(mixed_rows, norm_gains[1], shifts[1]).astype(jnp.bfloat16)
    hidden_pre = jnp.dot(second_low, full_up, preferred_element_type=jnp.float32) + ff_shift
    activated_low = exact_gelu(hidden_pre).astype(jnp.bfloat16)
    output = (
        mixed_rows
        + jnp.dot(activated_low, full_down, preferred_element_type=jnp.float32)
        + biases[3]
    )
    upstream = cotangent.astype(jnp.float32)
    grad_down = jnp.einsum(
        "tf,td->fd", activated_low, cotangent, preferred_element_type=jnp.float32
    )
    grad_act = jnp.einsum("td,fd->tf", cotangent, full_down, preferred_element_type=jnp.float32)
    unused, gelu_back = jax.vjp(exact_gelu, hidden_pre)
    grad_pre = gelu_back(grad_act)[0]
    grad_pre_low = grad_pre.astype(jnp.bfloat16)
    grad_up = jnp.einsum("td,tf->df", second_low, grad_pre_low, preferred_element_type=jnp.float32)
    grad_second = jnp.einsum("tf,df->td", grad_pre_low, full_up, preferred_element_type=jnp.float32)
    unused, second_back = jax.vjp(layer_norm, mixed_rows, norm_gains[1], shifts[1])
    grad_mixed_norm, grad_gain_two, grad_shift_two = second_back(grad_second)
    grad_mixed = upstream + grad_mixed_norm
    grad_mixed_low = grad_mixed.astype(jnp.bfloat16)
    grad_out = jnp.einsum(
        "td,te->de", attended_low, grad_mixed_low, preferred_element_type=jnp.float32
    )
    grad_att_low = (
        jnp.einsum("te,de->td", grad_mixed_low, full_out, preferred_element_type=jnp.float32)
        .astype(jnp.bfloat16)
        .reshape(head_shape)
    )
    deltas = jnp.einsum("qhd,qhd->hq", grad_att_low.astype(jnp.float32), attended)

    def score_grads(
        query_block,
        key_block,
        value_block,
        grad_block,
        query_positions,
        key_positions,
        log_block,
        delta_block,
    ):
        chances = probabilities(query_block, key_block, query_positions, key_positions, log_block)
        grad_chances = jnp.einsum(
            "qhd,khd->hqk", grad_block, value_block, preferred_element_type=jnp.float32
        )
        grad_scores = (chances * (grad_chances - delta_block[..., None]) * score_scale).astype(
            jnp.bfloat16
        )
        return (chances.astype(jnp.bfloat16), grad_scores)

    def backward_block(running, pieces):
        key_block, value_block, first_pos = pieces
        chances_low, grad_scores = score_grads(
            queries,
            key_block,
            value_block,
            grad_att_low,
            query_pos,
            first_pos + within,
            log_total,
            deltas,
        )
        running = running + jnp.einsum(
            "hqk,khd->qhd", grad_scores, key_block, preferred_element_type=jnp.float32
        )
        key_term = jnp.einsum(
            "hqk,qhd->khd", grad_scores, queries, preferred_element_type=jnp.float32
        )
        value_term = jnp.einsum(
            "hqk,qhd->khd", chances_low, grad_att_low, preferred_element_type=jnp.float32
        )
        return (running, (key_term, value_term))

    grad_queries, (key_terms, value_terms) = lax.scan(
        backward_block, jnp.zeros(head_shape, jnp.float32), (key_blocks, value_blocks, block_starts)
    )
    grad_keys, grad_values = (
        lax.psum_scatter(
            key_terms.reshape(TREE_TOKENS, D).astype(jnp.bfloat16),
            "col",
            scatter_dimension=0,
            tiled=True,
        ).astype(jnp.float32),
        lax.psum_scatter(
            value_terms.reshape(TREE_TOKENS, D).astype(jnp.bfloat16),
            "col",
            scatter_dimension=0,
            tiled=True,
        ).astype(jnp.float32),
    )
    grad_queries = grad_queries.reshape(local_rows, D)
    grad_projected_low = jnp.concatenate([grad_queries, grad_keys, grad_values], axis=1).astype(
        jnp.bfloat16
    )
    grad_qkv = jnp.einsum(
        "td,te->de", normed_low, grad_projected_low, preferred_element_type=jnp.float32
    )
    grad_normed = jnp.einsum(
        "te,de->td", grad_projected_low, full_qkv, preferred_element_type=jnp.float32
    )
    unused, first_back = jax.vjp(layer_norm, inputs, norm_gains[0], shifts[0])
    grad_input_norm, grad_gain_one, grad_shift_one = first_back(grad_normed)
    grad_tokens = (grad_mixed + grad_input_norm).astype(jnp.bfloat16)
    gain_terms = jnp.stack([grad_gain_one, grad_gain_two])
    shift_terms = jnp.stack([grad_shift_one, grad_shift_two])
    bias_terms = jnp.stack(
        [
            jnp.sum(grad_queries, axis=0),
            jnp.sum(grad_values, axis=0),
            jnp.sum(grad_mixed, axis=0),
            jnp.sum(upstream, axis=0),
        ]
    )
    ff_terms = jnp.sum(grad_pre, axis=0)
    part_qkv, part_out, part_up, part_down, part_gain, part_shift, part_bias, part_ff = (
        lax.psum_scatter(
            grad_qkv.astype(jnp.bfloat16), "col", scatter_dimension=1, tiled=True
        ).astype(jnp.float32),
        lax.psum_scatter(
            grad_out.astype(jnp.bfloat16), "col", scatter_dimension=1, tiled=True
        ).astype(jnp.float32),
        lax.psum_scatter(
            grad_up.astype(jnp.bfloat16), "col", scatter_dimension=1, tiled=True
        ).astype(jnp.float32),
        lax.psum_scatter(
            grad_down.astype(jnp.bfloat16), "col", scatter_dimension=1, tiled=True
        ).astype(jnp.float32),
        lax.psum_scatter(
            gain_terms.astype(jnp.bfloat16), "col", scatter_dimension=1, tiled=True
        ).astype(jnp.float32),
        lax.psum_scatter(
            shift_terms.astype(jnp.bfloat16), "col", scatter_dimension=1, tiled=True
        ).astype(jnp.float32),
        lax.psum_scatter(
            bias_terms.astype(jnp.bfloat16), "col", scatter_dimension=1, tiled=True
        ).astype(jnp.float32),
        lax.psum_scatter(
            ff_terms.astype(jnp.bfloat16), "col", scatter_dimension=0, tiled=True
        ).astype(jnp.float32),
    )
    grad_w_qkv, grad_w_out, grad_w_up, grad_w_down = (
        lax.psum_scatter(
            part_qkv.astype(jnp.bfloat16), "row", scatter_dimension=0, tiled=True
        ).astype(jnp.float32),
        lax.psum_scatter(
            part_out.astype(jnp.bfloat16), "row", scatter_dimension=0, tiled=True
        ).astype(jnp.float32),
        lax.psum_scatter(
            part_up.astype(jnp.bfloat16), "row", scatter_dimension=0, tiled=True
        ).astype(jnp.float32),
        lax.psum_scatter(
            part_down.astype(jnp.bfloat16), "row", scatter_dimension=0, tiled=True
        ).astype(jnp.float32),
    )
    grad_gain, grad_shift, grad_bias, grad_ff = lax.psum(
        (part_gain, part_shift, part_bias, part_ff), "row"
    )
    return (
        output.astype(jnp.bfloat16),
        grad_tokens,
        grad_w_qkv,
        grad_w_out,
        grad_w_up,
        grad_w_down,
        grad_gain,
        grad_shift,
        grad_bias,
        grad_ff,
    )


def solution(mesh):
    return jax.shard_map(
        body,
        mesh=mesh,
        in_specs=(
            P(("row", "col"), None),
            P("row", None),
            P("row", "col"),
            P("row", "col"),
            P("row", "col"),
            P("row", "col"),
            P(None, "col"),
            P(None, "col"),
            P(None, "col"),
            P("col"),
            P(("row", "col"), None),
        ),
        out_specs=(
            P(("row", "col"), None),
            P(("row", "col"), None),
            P("row", "col"),
            P("row", "col"),
            P("row", "col"),
            P("row", "col"),
            P(None, "col"),
            P(None, "col"),
            P(None, "col"),
            P("col"),
        ),
        check_vma=False,
    )
```

profile of v0, /device:TPU:0, one launch (start us, length us, event | category | flops | bytes accessed | tf_op | source)
XLA Modules:
  0.0 1622.3 jit_solution(980665624562013141)
XLA Ops:
  8.3 35.3 %all_gather.44 = bf16[192,2304]{0,1:T(8,128)(2,1)S(1)} all-gather(bf16[192,288]{0,1:T(8,128)(2,1)S(1)} %copy.107), channel_id=1, replica_groups=mesh['row'=4,'col'=8] {'col'}, dimensions={1}, use_global_device_ids=true | all-gather | bytes 995328 | tf_op jit(solution)/shard_map/all_gather | solution.py:63
  46.5 20.0 %all-gather = bf16[8,96,2]{1,2,0:T(2,128)(2,1)S(1)} all-gather(bf16[1,96,2]{1,2,0:T(2,128)(2,1)S(1)} %bitcast.281), channel_id=1, replica_groups=mesh['row'=4,'col'=8] {'col'}, dimensions={0}, use_global_device_ids=true | all-gather | bytes 3456 | tf_op jit(solution)/shard_map/all_gather | solution.py:67
  66.6 16.2 all-gather.1
  92.5 18.3 %all-gather.2 = bf16[8,96,4]{1,2,0:T(4,128)(2,1)S(1)} all-gather(bf16[1,96,4]{1,2,0:T(4,128)(2,1)S(1)} %bitcast.280), channel_id=1, replica_groups=mesh['row'=4,'col'=8] {'col'}, dimensions={0}, use_global_device_ids=true | all-gather | bytes 6912 | tf_op jit(solution)/shard_map/all_gather | solution.py:69
  115.8 31.4 %all_gather.49 = bf16[192,768]{0,1:T(8,128)(2,1)S(1)} all-gather(bf16[192,96]{0,1:T(8,128)(2,1)S(1)} %copy.116), channel_id=1, replica_groups=mesh['row'=4,'col'=8] {'col'}, dimensions={1}, use_global_device_ids=true | all-gather | bytes 331776 | tf_op jit(solution)/shard_map/all_gather | solution.py:64
  149.0 25.9 %all-gather.3 = bf16[8,1,384]{2,1,0:T(2,128)(2,1)S(1)} all-gather(bf16[1,1,384]{2,1,0:T(2,128)(2,1)S(1)} %reshape.404), channel_id=1, replica_groups=mesh['row'=4,'col'=8] {'col'}, dimensions={0}, use_global_device_ids=true | all-gather | bytes 6912 | tf_op jit(solution)/shard_map/all_gather | solution.py:70
  177.6 85.8 %all-gather.17.cloned.1.call-done = bf16[4096,12,64]{0,2,1:T(8,128)(2,1)} async-done(((bf16[512,12,64]{0,2,1:T(8,128)(2,1)}), bf16[4096,12,64]{0,2,1:T(8,128)(2,1)}) %all-gather.17.cloned.1.call-update) | async-done | bytes 6291472 | tf_op jit(solution)/shard_map/all_gather | solution.py:89
  263.4 6.3 copy.159
  269.7 68.4 %while.60 = (s32[]{:T(128)}, f32[12,512]{1,0:T(8,128)S(1)}, f32[12,512]{1,0:T(8,128)S(1)}, s32[8]{0:T(128)S(1)}, f32[512,16]{0,1:T(8,128)S(1)}, /*index=5*/bf16[...) while((s32[]{:T(128)}, f32[12,512]{1,0:T(8,128)S(1)}, ...), condition=%wide.region_5.6_spmd.clone.clone.clone, body=%wide.region_2.5_spmd.clone.clone.clone.sunk | while | flops 479517696 | bytes 27899032 | solution.py:123
  338.1 25.9 %all-gather.15.cloned.1.call-done = bf16[4096,12,64]{0,2,1:T(8,128)(2,1)} async-done(((bf16[512,12,64]{0,2,1:T(8,128)(2,1)}), bf16[4096,12,64]{0,2,1:T(8,128)(2,1)}) %all-gather.15.cloned.1.call-update) | async-done | bytes 6291472 | tf_op jit(solution)/shard_map/all_gather | solution.py:90
  364.0 6.4 copy.160
  370.4 65.0 %while.61 = (s32[]{:T(128)}, f32[512,12,64]{0,2,1:T(8,128)S(1)}, bf16[8,512,12,64]{1,3,2,0:T(8,128)(2,1)}, s32[8]{0:T(128)S(1)}, f32[512,16]{0,1:T(8,128)S(1)}, ...) while((s32[]{:T(128)}, f32[512,12,64]{0,2,1:T(8,128)S(1)}, ...), condition=%wide.region_7.8_spmd.clone.clone.clone, body=%wide.region_6.7_spmd.clone.clone.clone.sunk | while | flops 870343680 | bytes 6109850 | solution.py:137
  440.7 8.2 fusion.148
  448.9 11.0 all-gather.27.cloned.1.call-done
  459.9 20.7 %fusion.151 = (bf16[3072]{0:T(1024)(128)(2,1)}, bf16[512,3072]{1,0:T(8,128)(2,1)S(1)}, f32[512,3072]{1,0:T(8,128)}) fusion(f32[512,3072]{1,0:T(8,128)} %fusion.148, f32[3072]{0:T(1024)S(1)} %bitcast.272, bf16[512,768]{1,0:T(8,128)(2,1)S(1)} %copy-done.11, bf16[3072,768]{0,1:T(8,128)(2,1)} %all-gather.27.cloned.1.call-done), kind=kOutput, calls=%fused_computation.251 | convolution fusion | flops 2532307968 | bytes 21252096 | tf_op jit(solution)/shard_map/td,fd->tf/dot_general | solution.py:156
  490.8 236.6 %while.62 = (s32[]{:T(128)}, f32[512,12,64]{0,2,1:T(8,128)S(1)}, bf16[8,512,12,64]{1,3,2,0:T(8,128)(2,1)}, bf16[8,512,12,64]{1,3,2,0:T(8,128)(2,1)}, bf16[8,512,...) while((s32[]{:T(128)}, f32[512,12,64]{0,2,1:T(8,128)S(1)}, ...), condition=%wide.region_13.14_spmd.clone.clone.clone, body=%wide.region_12.13_spmd.clone.clone.clone.sunk | while | flops 2100323328 | bytes 69334224 | solution.py:218
  493.3 7.6 fusion.244
  500.9 7.6 fusion.247
  508.5 7.0 bitcast_dynamic-update-slice_fusion.5
  522.8 7.6 fusion.244
  530.4 7.6 fusion.247
  538.1 7.0 bitcast_dynamic-update-slice_fusion.5
  552.3 7.6 fusion.244
  559.9 7.6 fusion.247
  567.5 7.0 bitcast_dynamic-update-slice_fusion.5
  581.8 7.6 fusion.244
  589.4 7.6 fusion.247
  597.0 7.0 bitcast_dynamic-update-slice_fusion.5
  611.3 7.6 fusion.244
  618.9 7.6 fusion.247
  626.5 7.0 bitcast_dynamic-update-slice_fusion.5
  640.8 7.6 fusion.244
  648.4 7.6 fusion.247
  656.0 7.0 bitcast_dynamic-update-slice_fusion.5
  670.3 7.6 fusion.244
  677.9 7.6 fusion.247
  685.5 7.0 bitcast_dynamic-update-slice_fusion.5
  699.8 7.6 fusion.244
  707.4 7.6 fusion.247
  715.0 7.0 bitcast_dynamic-update-slice_fusion.5
  727.4 6.9 copy.122
  734.3 6.8 copy.153
  741.3 6.9 copy.121
  748.3 6.8 copy.152
  759.2 6.4 convolution_convert_fusion.2
  765.6 6.6 copy.141
  772.9 6.5 multiply_convert_fusion
  786.8 72.8 %reduce-scatter.28.cloned.1.call-done = bf16[512,768]{0,1:T(8,128)(2,1)} async-done(((bf16[4096,768]{0,1:T(8,128)(2,1)}), bf16[512,768]{0,1:T(8,128)(2,1)}) %reduce-scatter.28.cloned.1.call-update) | async-done | bytes 786448 | tf_op jit(solution)/shard_map/reduce_scatter | solution.py:228
  859.6 121.0 %reduce-scatter.26.cloned.1.call-done = bf16[512,768]{0,1:T(8,128)(2,1)} async-done(((bf16[4096,768]{0,1:T(8,128)(2,1)}), bf16[512,768]{0,1:T(8,128)(2,1)}) %reduce-scatter.26.cloned.1.call-update) | async-done | bytes 786448 | tf_op jit(solution)/shard_map/reduce_scatter | solution.py:222
  980.7 5.6 convolution_convert_fusion
  986.3 60.9 %reduce-scatter.32.cloned.1.call-done = bf16[768,96]{0,1:T(8,128)(2,1)} async-done(((bf16[768,768]{0,1:T(8,128)(2,1)}), bf16[768,96]{0,1:T(8,128)(2,1)}) %reduce-scatter.32.cloned.1.call-update) | async-done | bytes 147472 | tf_op jit(solution)/shard_map/reduce_scatter | solution.py:263
  1049.0 95.9 %reduce-scatter.44.cloned.1.call-done = bf16[384,768]{1,0:T(8,128)(2,1)} async-done(((bf16[3072,768]{1,0:T(8,128)(2,1)}), bf16[384,768]{1,0:T(8,128)(2,1)}) %reduce-scatter.44.cloned.1.call-update) | async-done | bytes 589840
  1147.5 96.2 %reduce-scatter.36.cloned.1.call-done = bf16[3072,96]{0,1:T(8,128)(2,1)} async-done(((bf16[3072,768]{0,1:T(8,128)(2,1)}), bf16[3072,96]{0,1:T(8,128)(2,1)}) %reduce-scatter.36.cloned.1.call-update) | async-done | bytes 589840 | tf_op jit(solution)/shard_map/reduce_scatter | solution.py:269
  1259.6 21.7 %all-reduce = bf16[3072]{0:T(1024)(128)(2,1)S(1)} all-reduce(bf16[3072]{0:T(1024)(128)(2,1)S(1)} %copy-done.27), channel_id=15, replica_groups=mesh['row'=4,'col'=8] {'col'}, use_global_device_ids=true, to_apply=%region_41.42.clone | all-reduce | flops 3072 | bytes 12288
  1281.3 45.6 %reduce-scatter.30.cloned.1.call-done = bf16[768,288]{0,1:T(8,128)(2,1)} async-done(((bf16[768,2304]{0,1:T(8,128)(2,1)}), bf16[768,288]{0,1:T(8,128)(2,1)}) %reduce-scatter.30.cloned.1.call-update) | async-done | bytes 442384 | tf_op jit(solution)/shard_map/reduce_scatter | solution.py:260
  1329.1 6.8 add_convert_fusion.1
  1335.9 13.2 reduce-scatter.42.cloned.1.call-done
  1350.7 22.8 %reduce-scatter.34.cloned.1.call-done = bf16[192,384]{1,0:T(8,128)(2,1)} async-done(((bf16[768,384]{1,0:T(8,128)(2,1)}), bf16[192,384]{1,0:T(8,128)(2,1)}) %reduce-scatter.34.cloned.1.call-update) | async-done | bytes 147472 | tf_op jit(solution)/shard_map/reduce_scatter | solution.py:292
  1375.2 22.8 %reduce-scatter.38.cloned.1.call-done = bf16[768,96]{0,1:T(8,128)(2,1)} async-done(((bf16[3072,96]{0,1:T(8,128)(2,1)}), bf16[768,96]{0,1:T(8,128)(2,1)}) %reduce-scatter.38.cloned.1.call-update) | async-done | bytes 147472 | tf_op jit(solution)/shard_map/reduce_scatter | solution.py:295
  1399.7 63.2 %reduce-scatter.46.cloned.1.call-done = bf16[96,2]{1,0:T(8,128)(2,1)} async-done(((bf16[768,2]{1,0:T(8,128)(2,1)}), bf16[96,2]{1,0:T(8,128)(2,1)}) %reduce-scatter.46.cloned.1.call-update) | async-done | bytes 400
  1463.6 62.6 %reduce-scatter.48.cloned.1.call-done = bf16[96,2]{1,0:T(8,128)(2,1)} async-done(((bf16[768,2]{1,0:T(8,128)(2,1)}), bf16[96,2]{1,0:T(8,128)(2,1)}) %reduce-scatter.48.cloned.1.call-update) | async-done | bytes 400
  1527.0 62.4 %reduce-scatter.50.cloned.1.call-done = bf16[96,4]{1,0:T(8,128)(2,1)} async-done(((bf16[768,4]{1,0:T(8,128)(2,1)}), bf16[96,4]{1,0:T(8,128)(2,1)}) %reduce-scatter.50.cloned.1.call-update) | async-done | bytes 784
  1590.2 6.3 all-reduce.1
  1596.6 16.5 %reduce-scatter.40.cloned.1.call-done = bf16[192,288]{1,0:T(8,128)(2,1)} async-done(((bf16[768,288]{1,0:T(8,128)(2,1)}), bf16[192,288]{1,0:T(8,128)(2,1)}) %reduce-scatter.40.cloned.1.call-update) | async-done | bytes 110608
  (432 shorter events, 272.0 us)
Async XLA Ops:
  7.2 39.3 %copy-start.37 = (bf16[2,96]{1,0:T(2,128)(2,1)S(1)}, bf16[2,96]{1,0:T(2,128)(2,1)}, u32[]{:S(2)}) copy-start(bf16[2,96]{1,0:T(2,128)(2,1)} %param.23) | copy-start | bytes 1156
  7.2 59.4 %copy-start.38 = (bf16[2,96]{1,0:T(2,128)(2,1)S(1)}, bf16[2,96]{1,0:T(2,128)(2,1)}, u32[]{:S(2)}) copy-start(bf16[2,96]{1,0:T(2,128)(2,1)} %param.24) | copy-start | bytes 1156
  7.2 75.7 %copy-start.1 = (bf16[512,768]{1,0:T(8,128)(2,1)S(1)}, bf16[512,768]{1,0:T(8,128)(2,1)}, u32[]{:S(2)}) copy-start(bf16[512,768]{1,0:T(8,128)(2,1)} %param.17) | copy-start | bytes 2359300
  7.2 76.9 %all-gather.13.cloned.1.call-start = ((), (), s32[]{:S(2)}) async-start(), calls=%async_computation.13 | async-start | bytes 4423680 | tf_op jit(solution)/shard_map/all_gather | solution.py:73
  45.0 103.2 %all-gather.21.cloned.1.call-start = ((), (), s32[]{:S(2)}) async-start(), calls=%async_computation.17 | async-start | bytes 1327104 | tf_op jit(solution)/shard_map/all_gather | solution.py:65
  45.7 130.4 %all-gather.25.cloned.1.call-start = ((), (), s32[]{:S(2)}) async-start(), calls=%async_computation.19 | async-start | bytes 1327104 | tf_op jit(solution)/shard_map/all_gather | solution.py:66
  46.5 216.9 %all-gather.17.cloned.1.call-start = ((), (), s32[]{:S(2)}) async-start(), calls=%async_computation.15 | async-start | bytes 7077888 | tf_op jit(solution)/shard_map/all_gather | solution.py:89
  82.9 1.2 copy-start.19
  82.9 1.2 copy-start.29
  82.9 357.7 %copy-start.31 = (f32[768]{0:T(1024)}, f32[768]{0:T(1024)S(1)}, u32[]{:S(2)}) copy-start(f32[768]{0:T(1024)S(1)} %get-tuple-element.1351) | copy-start | bytes 9220
  83.1 1.0 copy-start.21
  83.5 0.6 copy-start.23
  84.7 7.8 copy-start.35
  88.9 2.1 copy-start.10
  91.1 24.6 %copy-start.18 = (bf16[192,96]{1,0:T(8,128)(2,1)S(1)}, bf16[192,96]{1,0:T(8,128)(2,1)}, u32[]{:S(2)}) copy-start(bf16[192,96]{1,0:T(8,128)(2,1)} %param.20) | copy-start | bytes 110596
  92.4 271.7 %all-gather.15.cloned.1.call-start = ((), (), s32[]{:S(2)}) async-start(), calls=%async_computation.14 | async-start | bytes 7077888 | tf_op jit(solution)/shard_map/all_gather | solution.py:90
  111.4 37.5 %copy-start.36 = (bf16[384]{0:T(512)(128)(2,1)S(1)}, bf16[384]{0:T(512)(128)(2,1)}, u32[]{:S(2)}) copy-start(bf16[384]{0:T(512)(128)(2,1)} %param.26) | copy-start | bytes 2308
  111.4 63.6 %copy-start.41 = (s32[1,16]{1,0:T(1,128)S(1)}, s32[1,16]{1,0:T(1,128)}, u32[]{:S(2)}) copy-start(s32[1,16]{1,0:T(1,128)} %param.18) | copy-start | bytes 196
  115.7 320.9 %all-gather.19.cloned.1.call-start = ((), (), s32[]{:S(2)}) async-start(), calls=%async_computation.16 | async-start | bytes 1474560 | tf_op jit(solution)/shard_map/all_gather | solution.py:74
  148.1 292.5 %all-gather.23.cloned.1.call-start = ((), (), s32[]{:S(2)}) async-start(), calls=%async_computation.18 | async-start | bytes 5898240 | tf_op jit(solution)/shard_map/all_gather | solution.py:75
  148.9 311.0 %all-gather.27.cloned.1.call-start = ((), (), s32[]{:S(2)}) async-start(), calls=%async_computation.20 | async-start | bytes 5898240 | tf_op jit(solution)/shard_map/all_gather | solution.py:76
  175.0 284.9 %copy-start.16 = (f32[8,1,384]{2,1,0:T(1,128)}, f32[8,1,384]{2,1,0:T(1,128)S(1)}, u32[]{:S(2)}) copy-start(f32[8,1,384]{2,1,0:T(1,128)S(1)} %convert_element_type.203) | copy-start | bytes 36868
  176.1 683.5 %reduce-scatter.28.cloned.1.call-start = ((), (), s32[]{:S(2)}) async-start(), calls=%async_computation.22 | async-start | bytes 7077888 | tf_op jit(solution)/shard_map/reduce_scatter | solution.py:228
  435.4 13.5 copy-start.3
  439.0 1.3 copy-start.4
  440.6 19.2 %copy-start.11 = (bf16[512,768]{1,0:T(8,128)(2,1)S(1)}, bf16[512,768]{1,0:T(8,128)(2,1)}, u32[]{:S(2)}) copy-start(bf16[512,768]{1,0:T(8,128)(2,1)} %param.27) | copy-start | bytes 2359300
  459.9 20.7 %copy-start.5 = (f32[512,768]{1,0:T(8,128)S(1)}, f32[512,768]{1,0:T(8,128)}, u32[]{:S(2)}) copy-start(f32[512,768]{1,0:T(8,128)} %copy-done.4) | copy-start | bytes 4718596
  459.9 20.7 %copy-start.39 = (bf16[768,3072]{1,0:T(8,128)(2,1)S(1)}, bf16[768,3072]{1,0:T(8,128)(2,1)}, u32[]{:S(2)}) copy-start(bf16[768,3072]{1,0:T(8,128)(2,1)} %all-gather.23.cloned.1.call-done) | copy-start | bytes 14155780
  480.6 3.5 copy-start.43
  484.1 1.8 copy-start.40
  484.7 1.1 copy-start.8
  484.7 6.0 copy-start
  741.1 239.6 %reduce-scatter.26.cloned.1.call-start = ((), (), s32[]{:S(2)}) async-start(), calls=%async_computation.21 | async-start | bytes 7077888 | tf_op jit(solution)/shard_map/reduce_scatter | solution.py:222
  755.1 4.1 copy-start.6
  755.1 4.1 copy-start.32
  755.1 292.1 %reduce-scatter.32.cloned.1.call-start = ((), (), s32[]{:S(2)}) async-start(), calls=%async_computation.24 | async-start | bytes 1327104 | tf_op jit(solution)/shard_map/reduce_scatter | solution.py:263
  759.1 385.9 %reduce-scatter.44.cloned.1.call-start = ((), (), s32[]{:S(2)}) async-start(), calls=%async_computation.30 | async-start | bytes 5308416
  772.2 0.7 copy-start.17
  772.3 471.4 %reduce-scatter.36.cloned.1.call-start = ((), (), s32[]{:S(2)}) async-start(), calls=%async_computation.26 | async-start | bytes 5308416 | tf_op jit(solution)/shard_map/reduce_scatter | solution.py:269
  772.9 8.2 copy-start.12
  779.5 1.7 copy-start.14
  785.6 195.0 %copy-start.2 = (bf16[512,768]{1,0:T(8,128)(2,1)S(1)}, bf16[512,768]{1,0:T(8,128)(2,1)}, u32[]{:S(2)}) copy-start(bf16[512,768]{1,0:T(8,128)(2,1)} %param.17) | copy-start | bytes 2359300
  785.6 195.0 %copy-start.20 = (f32[768]{0:T(1024)S(1)}, f32[768]{0:T(1024)}, u32[]{:S(2)}) copy-start(f32[768]{0:T(1024)} %copy-done.19) | copy-start | bytes 9220
  785.6 195.0 %copy-start.22 = (f32[512]{0:T(512)S(1)}, f32[512]{0:T(512)}, u32[]{:S(2)}) copy-start(f32[512]{0:T(512)} %copy-done.21) | copy-start | bytes 6148
  785.6 195.0 %copy-start.26 = (f32[512]{0:T(512)S(1)}, f32[512]{0:T(512)}, u32[]{:S(2)}) copy-start(f32[512]{0:T(512)} %copy-done.25) | copy-start | bytes 6148
  785.6 195.0 %copy-start.30 = (f32[768]{0:T(1024)S(1)}, f32[768]{0:T(1024)}, u32[]{:S(2)}) copy-start(f32[768]{0:T(1024)} %copy-done.29) | copy-start | bytes 9220
  785.7 541.3 %reduce-scatter.30.cloned.1.call-start = ((), (), s32[]{:S(2)}) async-start(), calls=%async_computation.23 | async-start | bytes 3981312 | tf_op jit(solution)/shard_map/reduce_scatter | solution.py:260
  986.3 161.1 %copy-start.34 = (bf16[768]{0:T(1024)(128)(2,1)S(1)}, bf16[768]{0:T(1024)(128)(2,1)}, u32[]{:S(2)}) copy-start(bf16[768]{0:T(1024)(128)(2,1)} %get-tuple-element.1338) | copy-start | bytes 4612
  986.3 161.1 %copy-start.33 = (bf16[768]{0:T(1024)(128)(2,1)S(1)}, bf16[768]{0:T(1024)(128)(2,1)}, u32[]{:S(2)}) copy-start(bf16[768]{0:T(1024)(128)(2,1)} %get-tuple-element.1344) | copy-start | bytes 4612
  986.3 257.5 %copy-start.15 = (bf16[512,768]{0,1:T(8,128)(2,1)S(1)}, bf16[512,768]{0,1:T(8,128)(2,1)}, u32[]{:S(2)}) copy-start(bf16[512,768]{0,1:T(8,128)(2,1)} %reduce-scatter.28.cloned.1.call-done) | copy-start | bytes 2359300
  986.3 362.8 %reduce-scatter.42.cloned.1.call-start = ((), (), s32[]{:S(2)}) async-start(), calls=%async_computation.29 | async-start | bytes 245760
  1049.0 324.6 %reduce-scatter.34.cloned.1.call-start = ((), (), s32[]{:S(2)}) async-start(), calls=%async_computation.25 | async-start | bytes 737280 | tf_op jit(solution)/shard_map/reduce_scatter | solution.py:292
  1147.2 250.9 %reduce-scatter.38.cloned.1.call-start = ((), (), s32[]{:S(2)}) async-start(), calls=%async_computation.27 | async-start | bytes 737280 | tf_op jit(solution)/shard_map/reduce_scatter | solution.py:295
  1243.7 5.0 copy-start.24
  1243.7 7.8 copy-start.13
  1243.7 219.1 %reduce-scatter.46.cloned.1.call-start = ((), (), s32[]{:S(2)}) async-start(), calls=%async_computation.31 | async-start | bytes 221184
  1248.6 1.2 copy-start.9
  1249.8 8.6 copy-start.42
  1249.8 9.8 copy-start.27
  1250.6 78.5 %copy-start.7 = (f32[512,768]{1,0:T(8,128)S(1)}, f32[512,768]{1,0:T(8,128)}, u32[]{:S(2)}) copy-start(f32[512,768]{1,0:T(8,128)} %copy-done.4) | copy-start | bytes 4718596
  1250.6 78.5 %copy-start.28 = (f32[768]{0:T(1024)S(1)}, f32[768]{0:T(1024)}, u32[]{:S(2)}) copy-start(f32[768]{0:T(1024)} %get-tuple-element.1345) | copy-start | bytes 9220
  1255.1 271.1 %reduce-scatter.48.cloned.1.call-start = ((), (), s32[]{:S(2)}) async-start(), calls=%async_computation.32 | async-start | bytes 221184
  1257.4 332.1 %reduce-scatter.50.cloned.1.call-start = ((), (), s32[]{:S(2)}) async-start(), calls=%async_computation.33 | async-start | bytes 221184
  1258.3 354.8 %reduce-scatter.40.cloned.1.call-start = ((), (), s32[]{:S(2)}) async-start(), calls=%async_computation.28 | async-start | bytes 737280
  (1 other events, 0.6 us)
Sparse Core Ops, SparseCore 0:
  45.1 31.3 all-gather.12
  78.5 42.6 all-gather.20
  123.4 39.2 all-gather.24
  164.6 98.6 all-gather.16
  265.8 98.1 all-gather.14
  366.0 15.6 all-gather.18
  383.3 37.4 all-gather.22
  422.3 37.4 all-gather.26
  741.2 118.3 reduce-scatter.27
  863.1 117.5 reduce-scatter.25
  984.0 63.1 reduce-scatter.31
  1050.7 94.1 reduce-scatter.43
  1148.6 95.0 reduce-scatter.35
  1247.2 79.6 reduce-scatter.29
  1329.8 19.2 reduce-scatter.41
  1351.5 22.0 reduce-scatter.33
  1375.9 22.0 reduce-scatter.37
  1401.7 61.0 reduce-scatter.45
  1466.1 60.0 reduce-scatter.47
  1529.3 60.0 reduce-scatter.49
  1591.9 21.0 reduce-scatter.39
where the time goes:
time: 1630 us; the launch traced here: 1620 us
  waiting for transfers between devices  881 us (54%)
  matrix products  386 us (24%)
  blocking collectives  175 us (11%)
  local copies, waits for them, and re-layouts  94.5 us (6%)
  other arithmetic  66.6 us (4%)
    unnamed x27, waiting for transfers between devices  316 us
    reduce_scatter x1, waiting for transfers between devices, body(): lax.psum_scatter(key_terms.reshape(TREE_TOKENS, D).astype(jnp.bfloat16),...  121 us
    reduce_scatter x1, waiting for transfers between devices, body(): lax.psum_scatter(grad_down.astype(jnp.bfloat16), 'col', scatter_dimension...  96.2 us
    dot_general x16, matrix products, scores_of(): jnp.einsum('qhd,khd->hqk', query_block, key_block, preferred_element_type...  86.3 us
    all_gather x1, waiting for transfers between devices, body(): lax.all_gather(keys_own, 'col', axis=0, tiled=True)  85.8 us
    reduce_scatter x1, waiting for transfers between devices, body(): lax.psum_scatter(value_terms.reshape(TREE_TOKENS, D).astype(jnp.bfloat16)...  72.8 us
    dot_general x8, matrix products, score_grads(): jnp.einsum('qhd,khd->hqk', grad_block, value_block, preferred_element_typ...  61.1 us
    reduce_scatter x1, waiting for transfers between devices, body(): lax.psum_scatter(grad_out.astype(jnp.bfloat16), 'col', scatter_dimension=...  60.9 us
  transfers between devices with their start and end apart: 21, of which 16 were waited for; matrix products, arithmetic and copies ran while one was open for 16% of the time, Pallas kernels for 0%

commit v1 on v0

--- a/solution.py
+++ b/solution.py
@@ -1,6 +1,8 @@
 import jax
 import jax.numpy as jnp
 from jax import lax
+from jax.experimental import pallas as pl
+from jax.experimental.pallas import tpu as pltpu
 from jax.sharding import PartitionSpec as P
 
 D = 768
@@ -51,7 +53,7 @@
     return (reach > 0.5) & causal
 
 
-def body(
+def plain_body(
     tokens, parents, w_qkv, w_out, w_up, w_down, ln_gain, ln_bias, proj_bias, ff_bias, cotangent
 ):
     local_rows = tokens.shape[0]
@@ -313,7 +315,344 @@
     )
 
 
+F32=jnp.float32; BF=jnp.bfloat16
+NEG=NEGATIVE
+NT=(((1,),(1,)),((),()))
+NN=(((1,),(0,)),((),()))
+def dg(a,b,dims): return lax.dot_general(a,b,dims,preferred_element_type=F32)
+
+def chunks_of(trunk):
+    return [0,1,2,3] if trunk else [0,1,2,3,4,5]
+
+def score_chunk(c, trunk, k_ref, qh, meta):
+    if c<4:
+        st=dg(k_ref[c*SEG:(c+1)*SEG,:], qh, NT)
+        if trunk:
+            kp=c*SEG+lax.broadcasted_iota(jnp.int32,(SEG,2*SEG),0)
+            qp=meta[1]+lax.broadcasted_iota(jnp.int32,(SEG,2*SEG),1)
+            st=jnp.where(kp<=qp,st,NEG)
+        return st
+    base=4*SEG+(c-4)*2*SEG
+    parts=[]
+    for i in range(2):
+        s=dg(k_ref[base+i*SEG:base+(i+1)*SEG,:], qh[i*SEG:(i+1)*SEG,:], NT)
+        if c==4:
+            s=s+jnp.where(meta[2+i]>0,0.0,NEG).astype(F32)
+        else:
+            kp=lax.broadcasted_iota(jnp.int32,(SEG,SEG),0)
+            qp=lax.broadcasted_iota(jnp.int32,(SEG,SEG),1)
+            s=jnp.where(kp<=qp,s,NEG)
+        parts.append(s)
+    return jnp.concatenate(parts,axis=1)
+
+def fwd_kernel(meta, q_ref,k_ref,v_ref,o_ref,lse_ref):
+    def run(trunk):
+        q=q_ref[...]*jnp.asarray(0.125,BF)
+        lane=lax.broadcasted_iota(jnp.int32,q.shape,1)
+        vt=v_ref[...].T
+        res=[]
+        for h in range(2):
+            qh=jnp.where((lane<64)==(h==0),q,jnp.asarray(0,BF))
+            cs=chunks_of(trunk)
+            st=[score_chunk(c,trunk,k_ref,qh,meta) for c in cs]
+            m=st[0]
+            for s in st[1:]: m=jnp.maximum(m,s)
+            m=jnp.max(m,axis=0,keepdims=True)
+            l=jnp.zeros((1,2*SEG),F32);
+            ot=jnp.zeros((128,2*SEG),F32); own=[jnp.zeros((128,SEG),F32)]*2
+            for c,s in zip(cs,st):
+                p=jnp.exp(s-m)
+                l=l+jnp.sum(p,axis=0,keepdims=True)
+                pb=p.astype(BF)
+                if c<4:
+                    ot=ot+dg(vt[:,c*SEG:(c+1)*SEG],pb,NN)
+                else:
+                    base=4*SEG+(c-4)*2*SEG
+                    own=[own[i]+dg(vt[:,base+i*SEG:base+(i+1)*SEG],pb[:,i*SEG:(i+1)*SEG],NN) for i in range(2)]
+            ot=(ot+jnp.concatenate(own,axis=1))*(1.0/l)
+            res.append(ot)
+            lse_ref[0,h:h+1,:]=m+jnp.log(l)
+        row=lax.broadcasted_iota(jnp.int32,res[0].shape,0)
+        o_ref[...]=jnp.where(row<64,res[0],res[1]).T.astype(BF)
+    @pl.when(meta[0]>0)
+    def _(): run(True)
+    @pl.when(meta[0]==0)
+    def _(): run(False)
+
+def bwd_kernel(meta, q_ref,k_ref,v_ref,do_ref,o_ref,lse_ref,dq_ref,dk_ref,dv_ref):
+    def run(trunk):
+        q=q_ref[...]*jnp.asarray(0.125,BF)
+        do=do_ref[...]
+        lane=lax.broadcasted_iota(jnp.int32,q.shape,1)
+        zero=jnp.asarray(0,BF)
+        dd=(do.astype(F32)*o_ref[...].astype(F32)).T
+        kt=k_ref[...].T
+        qh=[jnp.where((lane<64)==(h==0),q,zero) for h in range(2)]
+        doh=[jnp.where((lane<64)==(h==0),do,zero) for h in range(2)]
+        delta=[jnp.sum(dd[h*64:(h+1)*64],axis=0,keepdims=True) for h in range(2)]
+        qcat=jnp.concatenate(qh,axis=0); docat=jnp.concatenate(doh,axis=0)
+        dqt=[jnp.zeros((128,2*SEG),F32)]*2
+        own=[[jnp.zeros((128,SEG),F32)]*2]*2
+        for c in chunks_of(trunk):
+            pbs=[];dsbs=[]
+            for h in range(2):
+                st=score_chunk(c,trunk,k_ref,qh[h],meta)
+                p=jnp.exp(st-lse_ref[0,h:h+1,:])
+                if c<4:
+                    dp=dg(v_ref[c*SEG:(c+1)*SEG,:],doh[h],NT)
+                else:
+                    base=4*SEG+(c-4)*2*SEG
+                    dp=jnp.concatenate([dg(v_ref[base+i*SEG:base+(i+1)*SEG,:],doh[h][i*SEG:(i+1)*SEG,:],NT) for i in range(2)],axis=1)
+                ds=p*(dp-delta[h])
+                pbs.append(p.astype(BF)); dsbs.append(ds.astype(BF))
+            if c<4:
+                r=slice(c*SEG,(c+1)*SEG)
+                dv_ref[r,:]=dg(jnp.concatenate(pbs,axis=1),docat,NN).astype(BF)
+                dk_ref[r,:]=dg(jnp.concatenate(dsbs,axis=1),qcat,NN).astype(BF)
+                for h in range(2): dqt[h]=dqt[h]+dg(kt[:,r],dsbs[h],NN)
+            else:
+                base=4*SEG+(c-4)*2*SEG
+                for i in range(2):
+                    r=slice(base+i*SEG,base+(i+1)*SEG); cc=slice(i*SEG,(i+1)*SEG)
+                    dv_ref[r,:]=dg(jnp.concatenate([x[:,cc] for x in pbs],axis=1),jnp.concatenate([x[cc] for x in doh],axis=0),NN).astype(BF)
+                    dk_ref[r,:]=dg(jnp.concatenate([x[:,cc] for x in dsbs],axis=1),jnp.concatenate([x[cc] for x in qh],axis=0),NN).astype(BF)
+                own=[[own[h][i]+dg(kt[:,base+i*SEG:base+(i+1)*SEG],dsbs[h][:,i*SEG:(i+1)*SEG],NN) for i in range(2)] for h in range(2)]
+        if trunk:
+            dv_ref[4*SEG:,:]=jnp.zeros((4*SEG,128),BF)
+            dk_ref[4*SEG:,:]=jnp.zeros((4*SEG,128),BF)
+        dqt=[dqt[h]+jnp.concatenate(own[h],axis=1) for h in range(2)]
+        row=lax.broadcasted_iota(jnp.int32,dqt[0].shape,0)
+        dq_ref[...]=(jnp.where(row<64,dqt[0],dqt[1]).T*0.125).astype(BF)
+    @pl.when(meta[0]>0)
+    def _(): run(True)
+    @pl.when(meta[0]==0)
+    def _(): run(False)
+
+def attn_fwd(meta,q,k,v,interpret=False):
+    n=q.shape[1]//128; nk=k.shape[0]; nq=q.shape[0]
+    gs=pltpu.PrefetchScalarGridSpec(num_scalar_prefetch=1,grid=(n,),
+        in_specs=[pl.BlockSpec((nq,128),lambda j,m:(0,j)),pl.BlockSpec((nk,128),lambda j,m:(0,j)),pl.BlockSpec((nk,128),lambda j,m:(0,j))],
+        out_specs=[pl.BlockSpec((nq,128),lambda j,m:(0,j)),pl.BlockSpec((1,2,nq),lambda j,m:(j,0,0))])
+    return pl.pallas_call(fwd_kernel,grid_spec=gs,out_shape=[jax.ShapeDtypeStruct(q.shape,BF),jax.ShapeDtypeStruct((n,2,nq),F32)],
+        cost_estimate=pl.CostEstimate(flops=2*2*12*256*256*256*12,bytes_accessed=8<<20,transcendentals=10<<20),
+        compiler_params=pltpu.CompilerParams(vmem_limit_bytes=60<<20),interpret=interpret,name="attn_fwd")(meta,q,k,v)
+def attn_bwd(meta,q,k,v,do,o,lse,interpret=False):
+    n=q.shape[1]//128; nk=k.shape[0]; nq=q.shape[0]
+    qs=pl.BlockSpec((nq,128),lambda j,m:(0,j)); ks=pl.BlockSpec((nk,128),lambda j,m:(0,j))
+    gs=pltpu.PrefetchScalarGridSpec(num_scalar_prefetch=1,grid=(n,),
+        in_specs=[qs,ks,ks,qs,qs,pl.BlockSpec((1,2,nq),lambda j,m:(j,0,0))],
+        out_specs=[qs,ks,ks])
+    return pl.pallas_call(bwd_kernel,grid_spec=gs,out_shape=[jax.ShapeDtypeStruct(q.shape,BF),jax.ShapeDtypeStruct(k.shape,BF),jax.ShapeDtypeStruct(k.shape,BF)],
+        cost_estimate=pl.CostEstimate(flops=5*2*12*256*256*256*12,bytes_accessed=16<<20,transcendentals=10<<20),
+        compiler_params=pltpu.CompilerParams(vmem_limit_bytes=60<<20),interpret=interpret,name="attn_bwd")(meta,q,k,v,do,o,lse)
+
+SEGMENT_HALF = 2 * SEG
+
+
+def normalise(values, scaling, shifting):
+    centre = values - jnp.mean(values, axis=-1, keepdims=True)
+    spread = jnp.mean(centre * centre, axis=-1, keepdims=True)
+    scale = lax.rsqrt(spread + EPSILON)
+    return centre * scale, scale
+
+
+def norm_back(unit, scale, scaling, grad):
+    scaled = grad * scaling
+    mean_one = jnp.mean(scaled, axis=-1, keepdims=True)
+    mean_two = jnp.mean(scaled * unit, axis=-1, keepdims=True)
+    return scale * (scaled - mean_one - unit * mean_two)
+
+
+def tree_body(
+    tokens, parents, w_qkv, w_out, w_up, w_down, ln_gain, ln_bias, proj_bias, ff_bias, cotangent
+):
+    both = ("row", "col")
+    col = lax.axis_index("col")
+    rows = lax.axis_size("row")
+    cols = lax.axis_size("col")
+    local_rows = tokens.shape[0]
+    all_tokens = lax.all_gather(tokens, "col", axis=0, tiled=True)
+    vectors = jnp.concatenate(
+        [ln_gain, ln_bias, proj_bias, ff_bias.reshape(-1, ln_gain.shape[1])], axis=0
+    )
+    vectors = lax.all_gather(vectors, "col", axis=0, tiled=False)
+    small = vectors[:, :8].transpose(1, 0, 2).reshape(8, D).astype(jnp.float32)
+    gains, shifts, biases = small[0:2], small[2:4], small[4:8]
+    ff_shift = vectors[:, 8:].reshape(-1).astype(jnp.float32)
+
+    def gathered(shard):
+        blocks = lax.all_gather(shard, both, axis=0, tiled=False)
+        a, b = shard.shape
+        return blocks.reshape(rows, cols, a, b)
+
+    blocks = gathered(w_qkv.T)
+    qkv_t = blocks.transpose(1, 2, 0, 3).reshape(3 * D, D)
+    blocks = gathered(w_out.T)
+    out_t = blocks.transpose(1, 2, 0, 3).reshape(D, D)
+    blocks = gathered(w_up)
+    full_up = blocks.transpose(0, 2, 1, 3).reshape(D, -1)
+    blocks = gathered(w_down.T)
+    down_t = blocks.transpose(1, 2, 0, 3).reshape(D, -1)
+
+    parent = parents[0]
+    first = 2 * col
+    own_parent = [jnp.maximum(parent[first + i], 0) for i in range(2)]
+    is_leaf = [(own_parent[i] >= 4).astype(jnp.int32) for i in range(2)]
+    meta = jnp.stack(
+        [(col < 2).astype(jnp.int32), col.astype(jnp.int32) * local_rows, is_leaf[0], is_leaf[1]]
+    )
+    key_tokens = jnp.concatenate(
+        [all_tokens[: 4 * SEG]]
+        + [lax.dynamic_slice_in_dim(all_tokens, own_parent[i] * SEG, SEG, 0) for i in range(2)]
+        + [tokens],
+        axis=0,
+    )
+    unit_one, scale_one = normalise(key_tokens.astype(jnp.float32), None, None)
+    normed = (unit_one * gains[0] + shifts[0]).astype(jnp.bfloat16)
+    normed_own = normed[-local_rows:]
+    queries = (
+        lax.dot_general(
+            normed_own, qkv_t[:D], (((1,), (1,)), ((), ())), preferred_element_type=jnp.float32
+        )
+        + biases[0]
+    ).astype(jnp.bfloat16)
+    key_rows = lax.dot_general(
+        normed, qkv_t[D : 2 * D], (((1,), (1,)), ((), ())), preferred_element_type=jnp.float32
+    ).astype(jnp.bfloat16)
+    value_rows = (
+        lax.dot_general(
+            normed, qkv_t[2 * D :], (((1,), (1,)), ((), ())), preferred_element_type=jnp.float32
+        )
+        + biases[1]
+    ).astype(jnp.bfloat16)
+    attended_low, log_total = attn_fwd(meta, queries, key_rows, value_rows)
+
+    inputs = tokens.astype(jnp.float32)
+    mixed_rows = (
+        inputs
+        + lax.dot_general(
+            attended_low, out_t, (((1,), (1,)), ((), ())), preferred_element_type=jnp.float32
+        )
+        + biases[2]
+    )
+    unit_two, scale_two = normalise(mixed_rows, None, None)
+    second_low = (unit_two * gains[1] + shifts[1]).astype(jnp.bfloat16)
+    hidden_pre = jnp.dot(second_low, full_up, preferred_element_type=jnp.float32) + ff_shift
+    activated_low = exact_gelu(hidden_pre).astype(jnp.bfloat16)
+    output = (
+        mixed_rows
+        + lax.dot_general(
+            activated_low, down_t, (((1,), (1,)), ((), ())), preferred_element_type=jnp.float32
+        )
+        + biases[3]
+    )
+    upstream = cotangent.astype(jnp.float32)
+    grad_down_t = jnp.einsum(
+        "td,tf->df", cotangent, activated_low, preferred_element_type=jnp.float32
+    )
+    grad_act = jnp.dot(cotangent, down_t, preferred_element_type=jnp.float32)
+    unused, gelu_back = jax.vjp(exact_gelu, hidden_pre)
+    grad_pre = gelu_back(grad_act)[0]
+    grad_pre_low = grad_pre.astype(jnp.bfloat16)
+    grad_up = jnp.einsum("td,tf->df", second_low, grad_pre_low, preferred_element_type=jnp.float32)
+    grad_second = jnp.einsum("tf,df->td", grad_pre_low, full_up, preferred_element_type=jnp.float32)
+    grad_mixed = upstream + norm_back(unit_two, scale_two, gains[1], grad_second)
+    grad_mixed_low = grad_mixed.astype(jnp.bfloat16)
+    grad_out_t = jnp.einsum(
+        "te,td->ed", grad_mixed_low, attended_low, preferred_element_type=jnp.float32
+    )
+    grad_att_low = jnp.dot(grad_mixed_low, out_t, preferred_element_type=jnp.float32).astype(
+        jnp.bfloat16
+    )
+    grad_q, grad_k, grad_v = attn_bwd(
+        meta, queries, key_rows, value_rows, grad_att_low, attended_low, log_total
+    )
+    grad_normed = jnp.dot(grad_k, qkv_t[D : 2 * D], preferred_element_type=jnp.float32) + jnp.dot(
+        grad_v, qkv_t[2 * D :], preferred_element_type=jnp.float32
+    )
+    part = grad_normed.astype(jnp.bfloat16)
+    spread_out = jnp.zeros((cols * local_rows, D), jnp.bfloat16)
+    spread_out = lax.dynamic_update_slice_in_dim(spread_out, part[: 4 * SEG], 0, 0)
+    for i in range(2):
+        start = own_parent[i] * SEG
+        piece = part[4 * SEG + i * SEG : 5 * SEG + i * SEG]
+        earlier = lax.dynamic_slice_in_dim(spread_out, start, SEG, 0)
+        spread_out = lax.dynamic_update_slice_in_dim(spread_out, earlier + piece, start, 0)
+    received = lax.psum_scatter(spread_out, "col", scatter_dimension=0, tiled=True)
+    grad_normed_own = (
+        grad_normed[-local_rows:]
+        + jnp.dot(grad_q, qkv_t[:D], preferred_element_type=jnp.float32)
+        + received.astype(jnp.float32)
+    )
+    grad_qkv_t = jnp.concatenate(
+        [
+            jnp.einsum("te,td->ed", grad_q, normed_own, preferred_element_type=jnp.float32),
+            jnp.einsum("te,td->ed", grad_k, normed, preferred_element_type=jnp.float32),
+            jnp.einsum("te,td->ed", grad_v, normed, preferred_element_type=jnp.float32),
+        ],
+        axis=0,
+    )
+    unit_own, scale_own = unit_one[-local_rows:], scale_one[-local_rows:]
+    grad_tokens = (
+        grad_mixed + norm_back(unit_own, scale_own, gains[0], grad_normed_own)
+    ).astype(jnp.bfloat16)
+
+    def scattered(blocks):
+        return lax.psum_scatter(
+            blocks.astype(jnp.bfloat16), both, scatter_dimension=0, tiled=True
+        ).astype(jnp.float32)
+
+    def split_out(array, row_dim, col_dim):
+        a, b = array.shape
+        if row_dim == 1:
+            return array.reshape(cols, a // cols, rows, b // rows).transpose(2, 0, 1, 3)
+        return array.reshape(rows, a // rows, cols, b // cols).transpose(0, 2, 1, 3)
+
+    def reduced(array, row_dim, col_dim):
+        blocks = split_out(array.astype(jnp.bfloat16), row_dim, col_dim)
+        r, c, a, b = blocks.shape
+        return scattered(blocks.reshape(r * c * a, b))
+
+    grad_w_down = reduced(grad_down_t, 1, 0).T
+    grad_w_up = reduced(grad_up, 0, 1)
+    grad_w_out = reduced(grad_out_t, 1, 0).T
+    grad_w_qkv = reduced(grad_qkv_t, 1, 0).T
+
+    terms = jnp.concatenate(
+        [
+            jnp.sum(grad_normed_own * unit_own, axis=0),
+            jnp.sum(grad_second * unit_two, axis=0),
+            jnp.sum(grad_normed_own, axis=0),
+            jnp.sum(grad_second, axis=0),
+            jnp.sum(grad_q.astype(jnp.float32), axis=0),
+            jnp.sum(grad_v.astype(jnp.float32), axis=0),
+            jnp.sum(grad_mixed, axis=0),
+            jnp.sum(upstream, axis=0),
+            jnp.sum(grad_pre, axis=0),
+        ]
+    )
+    terms = lax.psum(terms, both)
+    small = terms[: 8 * D].reshape(8, cols, D // cols)
+    small = lax.dynamic_slice_in_dim(small, col, 1, 1)[:, 0]
+    ff_len = ff_bias.shape[0]
+    grad_ff = lax.dynamic_slice_in_dim(terms[8 * D :], col * ff_len, ff_len, 0)
+    return (
+        output.astype(jnp.bfloat16),
+        grad_tokens,
+        grad_w_qkv,
+        grad_w_out,
+        grad_w_up,
+        grad_w_down,
+        small[0:2],
+        small[2:4],
+        small[4:8],
+        grad_ff,
+    )
+
+
 def solution(mesh):
+    fits = mesh.shape["col"] * 2 == SEGS
+    body = tree_body if fits else plain_body
     return jax.shard_map(
         body,
         mesh=mesh,

time: 1630 us -> 1070 us (0.66)
  matrix products: 386 us -> 82.3 us
  waiting for transfers between devices: 881 us -> 708 us
  blocking collectives: 175 us -> 71.9 us
  Pallas kernels: 0 us -> 38 us
  other arithmetic: 66.6 us -> 37.1 us
    dot_general x98 -> x18, matrix products: 386 us -> 82.3 us  [the longest x1 19.3 us: tree_body(): grad_act = jnp.dot(cotangent, down_t, preferred_element_type=jnp.float32)]
    unnamed x27 -> x12, waiting for transfers between devices: 316 us -> 89.5 us
    all_gather x8 -> x5, waiting for transfers between devices: 123 us -> 278 us  [the longest x4 188 us: gathered(): blocks = lax.all_gather(shard, both, axis=0, tiled=False)]
    all_gather x6 -> x1, blocking collectives: 147 us -> 32.2 us  [tree_body(): vectors = lax.all_gather(vectors, 'col', axis=0, tiled=False)]
    reduce_scatter x7 -> x3, waiting for transfers between devices: 442 us -> 340 us  [the longest x2 221 us: scattered(): lax.psum_scatter(blocks.astype(jnp.bfloat16), both, scatter_dimension=0,...]
    pallas_call x0 -> x2, Pallas kernels: none -> 38 us  [the longest x1 22 us: attn_bwd(): pl.pallas_call(bwd_kernel, grid_spec=gs, out_shape=[jax.ShapeDtypeStruct(...]
    psum x1, blocking collectives: 6.32 us -> 39.7 us  [tree_body(): terms = lax.psum(terms, both)]
    reshape x6 -> x10, local copies, waits for them, and re-layouts: 12.7 us -> 42.8 us  [the longest x4 21.5 us: gathered(): return blocks.reshape(rows, cols, a, b)]
  transfers between devices with their start and end apart: 21 -> 10, of which waited for: 16 -> 9; matrix products, arithmetic and copies ran while one was open for 16% -> 14% of each run, Pallas kernels for 0% -> 2%
where the time goes in v1:
time: 1070 us; the launch traced here: 1060 us
  waiting for transfers between devices  708 us (66%)
  local copies, waits for them, and re-layouts  103 us (10%)
  matrix products  82.3 us (8%)
  blocking collectives  71.9 us (7%)
  Pallas kernels  38 us (4%)
  other arithmetic  37.1 us (3%)
  between operations  16.7 us (2%)
    reduce_scatter x2, waiting for transfers between devices, scattered(): lax.psum_scatter(blocks.astype(jnp.bfloat16), both, scatter_dimension=0,...  221 us
    all_gather x4, waiting for transfers between devices, gathered(): blocks = lax.all_gather(shard, both, axis=0, tiled=False)  188 us
    reduce_scatter x1, waiting for transfers between devices, tree_body(): lax.psum_scatter(spread_out, 'col', scatter_dimension=0, tiled=True)  119 us
    all_gather x1, waiting for transfers between devices, tree_body(): all_tokens = lax.all_gather(tokens, 'col', axis=0, tiled=True)  90.7 us
    unnamed x12, waiting for transfers between devices  89.5 us
    psum x1, blocking collectives, tree_body(): terms = lax.psum(terms, both)  39.7 us
    all_gather x1, blocking collectives, tree_body(): vectors = lax.all_gather(vectors, 'col', axis=0, tiled=False)  32.2 us
    unnamed x89, local copies, waits for them, and re-layouts  23 us
  transfers between devices with their start and end apart: 10, of which 9 were waited for; matrix products, arithmetic and copies ran while one was open for 14% of the time, Pallas kernels for 2%

profile of v1, /device:TPU:0, one launch (start us, length us, event | category | flops | bytes accessed | tf_op | source)
XLA Modules:
  0.0 1057.3 jit_solution(15992690789848287381)
XLA Ops:
  7.2 1.5 copy.44
  8.8 1.7 copy.42
  12.5 1.3 constant_dynamic-slice_fusion.6
  16.6 32.2 %all-gather.5 = bf16[8,12,96]{2,1,0:T(8,128)(2,1)S(1)} all-gather(bf16[1,12,96]{2,1,0:T(8,128)(2,1)S(1)} %maximum_bitcast_fusion), channel_id=2, replica_groups=mesh['row'=4,'col'=8] {'col'}, dimensions={0}, use_global_device_ids=true | all-gather | bytes 20736 | tf_op jit(solution)/shard_map/all_gather | solution.py:478
  50.7 18.8 %all-gather.16.cloned.1.call-done = bf16[3072,192]{1,0:T(8,128)(2,1)} async-done(((bf16[96,192]{1,0:T(8,128)(2,1)}), bf16[3072,192]{1,0:T(8,128)(2,1)}) %all-gather.16.cloned.1.call-update) | async-done | bytes 1179664 | tf_op jit(solution)/shard_map/all_gather | solution.py:484
  69.5 2.0 copy.45
  71.5 1.3 reshape.190
  72.8 62.8 %all-gather.14.cloned.1.call-done = bf16[9216,192]{1,0:T(8,128)(2,1)} async-done(((bf16[288,192]{1,0:T(8,128)(2,1)}), bf16[9216,192]{1,0:T(8,128)(2,1)}) %all-gather.14.cloned.1.call-update) | async-done | bytes 3538960 | tf_op jit(solution)/shard_map/all_gather | solution.py:484
  135.6 8.4 copy.43
  144.0 8.0 reshape.188
  152.0 49.2 %all-gather.18.cloned.1.call-done = bf16[6144,384]{1,0:T(8,128)(2,1)} async-done(((bf16[192,384]{1,0:T(8,128)(2,1)}), bf16[6144,384]{1,0:T(8,128)(2,1)}) %all-gather.18.cloned.1.call-update) | async-done | bytes 4718608 | tf_op jit(solution)/shard_map/all_gather | solution.py:484
  201.1 5.2 copy.46
  206.3 3.3 copy.61
  209.6 56.9 %all-gather.20.cloned.1.call-done = bf16[3072,768]{1,0:T(8,128)(2,1)} async-done(((bf16[96,768]{1,0:T(8,128)(2,1)}), bf16[3072,768]{1,0:T(8,128)(2,1)}) %all-gather.20.cloned.1.call-update) | async-done | bytes 4718608 | tf_op jit(solution)/shard_map/all_gather | solution.py:484
  266.5 6.0 copy.47
  272.5 3.2 copy.62
  275.7 90.7 %all-gather.12.cloned.1.call-done = bf16[4096,768]{1,0:T(8,128)(2,1)} async-done(((bf16[512,768]{1,0:T(8,128)(2,1)}), bf16[4096,768]{1,0:T(8,128)(2,1)}) %all-gather.12.cloned.1.call-update) | async-done | bytes 6291472 | tf_op jit(solution)/shard_map/all_gather | solution.py:474
  366.4 1.5 slice.149
  367.9 1.2 constant_dynamic-slice_fusion.4
  369.1 3.0 convert_reduce_fusion
  372.1 4.0 fusion.2
  376.2 6.1 add_convert_fusion.1
  382.2 4.0 convolution_convert_fusion.2.k_ref
  386.2 1.7 add_convert_fusion.5.q_ref
  387.9 4.0 add_convert_fusion.v_ref
  391.8 16.0 %attn_fwd.1 = (bf16[512,768]{1,0:T(8,128)(2,1)}, f32[6,2,512]{2,1,0:T(2,128)}) custom-call(s32[4]{0:T(128)} %pad_add_fusion.meta, bf16[512,768]{1,0:T(8,128)(2,1)} %add_convert_fusion.5.q_ref, bf16[2048,768]{1,0:T(8,128)(2,1)} %convolution_convert_fusion.2.k_ref, bf16[2048,768]{1,0:T(8,128)(2,1)} %add_convert_fusion.v_ref), custom_call_target="tpu_custom_call" | custom-call | flops 9663676416 | bytes 8388608 | tf_op jit(solution)/shard_map/attn_fwd/pallas_call | solution.py:436
  407.8 2.0 fusion.33
  410.2 5.5 fusion.28
  415.8 19.3 %fusion.29 = (f32[3072]{0:T(1024)}, bf16[512,3072]{1,0:T(8,128)(2,1)S(1)}, f32[512,3072]{1,0:T(8,128)}) fusion(f32[512,3072]{1,0:T(8,128)S(1)} %fusion.28, f32[3072]{0:T(1024)S(1)} %reshape.206, bf16[512,768]{1,0:T(8,128)(2,1)S(1)} %copy-done.12, bf16[768,3072]{1,0:T(8,128)(2,1)S(1)} %bitcast.101), kind=kOutput, calls=%fused_computation.115 | convolution fusion | flops 2532307968 | bytes 21258240 | tf_op jit(solution)/shard_map/dot_general | solution.py:553
  435.2 3.6 multiply_reduce_fusion
  438.8 2.1 fusion.31
  440.9 1.7 convolution_convert_fusion.7.do_ref
  443.4 1.4 reshape.196
  444.9 1.4 copy.58
  446.4 22.0 %attn_bwd.1 = (bf16[512,768]{1,0:T(8,128)(2,1)}, bf16[2048,768]{1,0:T(8,128)(2,1)}, bf16[2048,768]{1,0:T(8,128)(2,1)}) custom-call(s32[4]{0:T(128)} %pad_add_fusion.meta, bf16[512,768]{1,0:T(8,128)(2,1)} %add_convert_fusion.5.q_ref, bf16[2048,768]{1,0:T(8,128)(2,1)} %convolution_convert_fusion.2.k_ref, bf16[2048,768]{1,0:T(8,128)(2,1)} %add_convert_fusion.v_ref, ...), custom_call_target="tpu_custom_call" | custom-call | flops 24159191040 | bytes 16777216 | tf_op jit(solution)/shard_map/attn_bwd/pallas_call | solution.py:445
  468.4 4.7 convolution_convert_fusion.5
  475.1 2.7 convolution_convert_fusion.4
  477.8 2.0 pad_maximum_fusion
  479.9 10.1 convert_element_type.119
  490.0 5.4 copy.57
  496.0 5.2 convolution_convert_fusion.1
  501.3 1.2 copy.63
  502.9 3.0 copy.50
  506.0 6.2 multiply_convert_fusion
  512.3 1.7 copy-done.11
  514.0 4.3 fusion.9
  518.3 6.6 copy.51
  524.9 9.7 reshape.200
  534.7 5.4 copy.52
  540.4 5.0 fusion.16
  545.4 6.0 fusion.34
  551.5 3.1 dynamic_update_slice.9
  555.5 1.9 fusion.25
  558.3 1.3 convert_reduce_fusion.3
  560.1 7.0 add_convert_fusion.3
  568.7 87.7 %reduce-scatter.16.cloned.1.call-done = bf16[288,192]{1,0:T(8,128)(2,1)} async-done(((bf16[9216,192]{1,0:T(8,128)(2,1)}), bf16[288,192]{1,0:T(8,128)(2,1)}) %reduce-scatter.16.cloned.1.call-update) | async-done | bytes 110608
  658.1 110.7 %reduce-scatter.12.cloned.1.call-done = bf16[192,384]{1,0:T(8,128)(2,1)} async-done(((bf16[6144,384]{1,0:T(8,128)(2,1)}), bf16[192,384]{1,0:T(8,128)(2,1)}) %reduce-scatter.12.cloned.1.call-update) | async-done | bytes 147472 | tf_op jit(solution)/shard_map/reduce_scatter | solution.py:601
  768.8 1.6 convert_element_type.122
  770.5 109.9 %reduce-scatter.14.cloned.1.call-done = bf16[96,768]{1,0:T(8,128)(2,1)} async-done(((bf16[3072,768]{1,0:T(8,128)(2,1)}), bf16[96,768]{1,0:T(8,128)(2,1)}) %reduce-scatter.14.cloned.1.call-update) | async-done | bytes 147472 | tf_op jit(solution)/shard_map/reduce_scatter | solution.py:601
  880.4 1.6 convert_bitcast_fusion
  882.1 119.4 %reduce-scatter.10.cloned.1.call-done = bf16[512,768]{1,0:T(8,128)(2,1)} async-done(((bf16[4096,768]{1,0:T(8,128)(2,1)}), bf16[512,768]{1,0:T(8,128)(2,1)}) %reduce-scatter.10.cloned.1.call-update) | async-done | bytes 786448 | tf_op jit(solution)/shard_map/reduce_scatter | solution.py:581
  1001.5 4.0 multiply_reduce_fusion.1
  1005.6 39.7 %psum.7 = f32[9216]{0:T(1024)S(1)} all-reduce(f32[9216]{0:T(1024)S(1)} %constant_dynamic-update-slice_fusion), channel_id=1, replica_groups=mesh['row'=4,'col'=8] {'row','col'}, use_global_device_ids=true, to_apply=%region_22.0 | all-reduce | flops 9216 | bytes 73728 | tf_op jit(solution)/shard_map/psum | solution.py:634
  1047.3 2.7 add_convert_fusion.2
  (144 shorter events, 17.9 us)
Async XLA Ops:
  7.2 62.3 %all-gather.16.cloned.1.call-start = ((), (), s32[]{:S(2)}) async-start(), calls=%async_computation.10 | async-start | bytes 1622016 | tf_op jit(solution)/shard_map/all_gather | solution.py:484
  8.8 126.9 %all-gather.14.cloned.1.call-start = ((), (), s32[]{:S(2)}) async-start(), calls=%async_computation.9 | async-start | bytes 4866048 | tf_op jit(solution)/shard_map/all_gather | solution.py:484
  10.5 190.6 %all-gather.18.cloned.1.call-start = ((), (), s32[]{:S(2)}) async-start(), calls=%async_computation.11 | async-start | bytes 4866048 | tf_op jit(solution)/shard_map/all_gather | solution.py:484
  11.3 255.2 %all-gather.20.cloned.1.call-start = ((), (), s32[]{:S(2)}) async-start(), calls=%async_computation.12 | async-start | bytes 4866048 | tf_op jit(solution)/shard_map/all_gather | solution.py:484
  11.8 354.6 %all-gather.12.cloned.1.call-start = ((), (), s32[]{:S(2)}) async-start(), calls=%async_computation.5 | async-start | bytes 7077888 | tf_op jit(solution)/shard_map/all_gather | solution.py:474
  12.4 554.7 %reduce-scatter.18.cloned.1.call-start = ((), (), s32[]{:S(2)}) async-start(), calls=%async_computation.14 | async-start | bytes 1622016
  49.6 385.5 %copy-start.21 = (f32[768]{0:T(1024)}, f32[768]{0:T(1024)S(1)}, u32[]{:S(2)}) copy-start(f32[768]{0:T(1024)S(1)} %mul.168) | copy-start | bytes 9220
  49.7 326.5 %copy-start.17 = (f32[768]{0:T(1024)}, f32[768]{0:T(1024)S(1)}, u32[]{:S(2)}) copy-start(f32[768]{0:T(1024)S(1)} %mul.162) | copy-start | bytes 9220
  49.7 360.5 %copy-start.29 = (f32[768]{0:T(1024)}, f32[768]{0:T(1024)S(1)}, u32[]{:S(2)}) copy-start(f32[768]{0:T(1024)S(1)} %add.185) | copy-start | bytes 9220
  275.7 93.4 %copy-start.3 = (bf16[512,768]{1,0:T(8,128)(2,1)S(1)}, bf16[512,768]{1,0:T(8,128)(2,1)}, u32[]{:S(2)}) copy-start(bf16[512,768]{1,0:T(8,128)(2,1)} %param.11) | copy-start | bytes 2359300
  376.1 6.1 copy-start.16
  376.1 6.1 copy-start.4
  382.2 5.7 copy-start.8
  409.9 28.9 %copy-start.5 = (f32[512,768]{1,0:T(8,128)}, f32[512,768]{1,0:T(8,128)S(1)}, u32[]{:S(2)}) copy-start(f32[512,768]{1,0:T(8,128)S(1)} %get-tuple-element.51) | copy-start | bytes 4718596
  409.9 5.9 slice-start
  410.2 28.6 %copy-start.25 = (f32[512]{0:T(512)}, f32[512]{0:T(512)S(1)}, u32[]{:S(2)}) copy-start(f32[512]{0:T(512)S(1)} %add_rsqrt_fusion.1) | copy-start | bytes 6148
  410.2 5.5 slice-start.1
  410.2 5.5 copy-start.12
  410.2 24.9 %slice-start.2 = ((s8[4718592]{0:T(1024)(128)(4,1)}), s8[4194304]{0:T(1024)(128)(4,1)S(1)}, s32[]{:S(2)}) async-start(s8[4718592]{0:T(1024)(128)(4,1)} %bitcast.106), calls=%async_computation.17 | async-start | bytes 8388608
  415.7 19.4 %copy-start.7 = (f32[512,3072]{1,0:T(8,128)}, f32[512,3072]{1,0:T(8,128)S(1)}, u32[]{:S(2)}) copy-start(f32[512,3072]{1,0:T(8,128)S(1)} %fusion.28) | copy-start | bytes 18874372
  415.8 19.4 %slice-start.3 = ((s8[4718592]{0:T(1024)(128)(4,1)}), s8[524288]{0:T(1024)(128)(4,1)S(1)}, s32[]{:S(2)}) async-start(s8[4718592]{0:T(1024)(128)(4,1)} %bitcast.106), calls=%async_computation.18 | async-start | bytes 1048576
  435.1 3.6 copy-start.31
  438.8 3.8 copy-start.14
  440.9 1.7 copy-start.1
  446.3 210.0 %reduce-scatter.16.cloned.1.call-start = ((), (), s32[]{:S(2)}) async-start(), calls=%async_computation.13 | async-start | bytes 4866048
  446.4 22.0 %copy-start.9 = (bf16[2048,768]{1,0:T(8,128)(2,1)S(1)}, bf16[2048,768]{1,0:T(8,128)(2,1)}, u32[]{:S(2)}) copy-start(bf16[2048,768]{1,0:T(8,128)(2,1)} %copy-done.8) | copy-start | bytes 9437188
  468.4 4.8 copy-start.10
  468.4 4.8 copy-start.15
  473.1 1.9 copy-start
  495.3 0.7 copy-start.22
  495.3 0.7 copy-start.26
  495.3 0.7 copy-start.30
  495.4 273.5 %reduce-scatter.12.cloned.1.call-start = ((), (), s32[]{:S(2)}) async-start(), calls=%async_computation.7 | async-start | bytes 4866048 | tf_op jit(solution)/shard_map/reduce_scatter | solution.py:601
  506.0 374.4 %reduce-scatter.14.cloned.1.call-start = ((), (), s32[]{:S(2)}) async-start(), calls=%async_computation.8 | async-start | bytes 4866048 | tf_op jit(solution)/shard_map/reduce_scatter | solution.py:601
  506.0 7.9 copy-start.13
  512.3 1.7 copy-start.11
  540.1 461.3 %reduce-scatter.10.cloned.1.call-start = ((), (), s32[]{:S(2)}) async-start(), calls=%async_computation.6 | async-start | bytes 7077888 | tf_op jit(solution)/shard_map/reduce_scatter | solution.py:581
  555.5 1.9 copy-start.23
  557.5 2.6 copy-start.6
  560.1 441.3 %copy-start.18 = (f32[768]{0:T(1024)S(1)}, f32[768]{0:T(1024)}, u32[]{:S(2)}) copy-start(f32[768]{0:T(1024)} %copy-done.17) | copy-start | bytes 9220
  1001.4 4.1 copy-start.28
  1001.4 4.1 copy-start.27
  1001.4 4.1 copy-start.20
  1001.4 4.2 copy-start.19
  1001.4 4.2 copy-start.24
  1001.4 45.9 %copy-start.2 = (f32[512,768]{1,0:T(8,128)S(1)}, f32[512,768]{1,0:T(8,128)}, u32[]{:S(2)}) copy-start(f32[512,768]{1,0:T(8,128)} %copy-done.1) | copy-start | bytes 4718596
Sparse Core Ops, SparseCore 0:
  11.6 57.8 all-gather.15
  73.0 62.5 all-gather.13
  138.6 62.4 all-gather.17
  204.0 62.4 all-gather.19
  268.5 97.8 all-gather.11
  446.4 98.4 reduce-scatter.17
  550.4 105.9 reduce-scatter.15
  662.7 106.0 reduce-scatter.11
  774.3 106.0 reduce-scatter.13
  884.3 117.1 reduce-scatter.9

commit v2 on v0

--- a/solution.py
+++ b/solution.py
@@ -1,6 +1,8 @@
 import jax
 import jax.numpy as jnp
 from jax import lax
+from jax.experimental import pallas as pl
+from jax.experimental.pallas import tpu as pltpu
 from jax.sharding import PartitionSpec as P
 
 D = 768
@@ -51,7 +53,7 @@
     return (reach > 0.5) & causal
 
 
-def body(
+def plain_body(
     tokens, parents, w_qkv, w_out, w_up, w_down, ln_gain, ln_bias, proj_bias, ff_bias, cotangent
 ):
     local_rows = tokens.shape[0]
@@ -313,7 +315,822 @@
     )
 
 
+F32=jnp.float32; BF=jnp.bfloat16
+NEG=NEGATIVE
+NT=(((1,),(1,)),((),()))
+NN=(((1,),(0,)),((),()))
+def dg(a,b,dims): return lax.dot_general(a,b,dims,preferred_element_type=F32)
+
+def chunks_of(trunk):
+    return [0,1,2,3] if trunk else [0,1,2,3,4,5]
+
+def score_chunk(c, trunk, k_ref, qh, meta):
+    if c<4:
+        st=dg(k_ref[c*SEG:(c+1)*SEG,:], qh, NT)
+        if trunk:
+            kp=(c^meta[4])*SEG+lax.broadcasted_iota(jnp.int32,(SEG,2*SEG),0)
+            qp=meta[1]+lax.broadcasted_iota(jnp.int32,(SEG,2*SEG),1)
+            st=jnp.where(kp<=qp,st,NEG)
+        return st
+    base=4*SEG+(c-4)*2*SEG
+    parts=[]
+    for i in range(2):
+        s=dg(k_ref[base+i*SEG:base+(i+1)*SEG,:], qh[i*SEG:(i+1)*SEG,:], NT)
+        if c==4:
+            s=s+jnp.where(meta[2+i]>0,0.0,NEG).astype(F32)
+        else:
+            kp=lax.broadcasted_iota(jnp.int32,(SEG,SEG),0)
+            qp=lax.broadcasted_iota(jnp.int32,(SEG,SEG),1)
+            s=jnp.where(kp<=qp,s,NEG)
+        parts.append(s)
+    return jnp.concatenate(parts,axis=1)
+
+def fwd_kernel(meta, q_ref,k_ref,v_ref,o_ref,lse_ref):
+    def run(trunk):
+        q=q_ref[...]*jnp.asarray(0.125,BF)
+        lane=lax.broadcasted_iota(jnp.int32,q.shape,1)
+        vt=v_ref[...].T
+        res=[]
+        for h in range(2):
+            qh=jnp.where((lane<64)==(h==0),q,jnp.asarray(0,BF))
+            cs=chunks_of(trunk)
+            st=[score_chunk(c,trunk,k_ref,qh,meta) for c in cs]
+            m=st[0]
+            for s in st[1:]: m=jnp.maximum(m,s)
+            m=jnp.max(m,axis=0,keepdims=True)
+            l=jnp.zeros((1,2*SEG),F32);
+            ot=jnp.zeros((128,2*SEG),F32); own=[jnp.zeros((128,SEG),F32)]*2
+            for c,s in zip(cs,st):
+                p=jnp.exp(s-m)
+                l=l+jnp.sum(p,axis=0,keepdims=True)
+                pb=p.astype(BF)
+                if c<4:
+                    ot=ot+dg(vt[:,c*SEG:(c+1)*SEG],pb,NN)
+                else:
+                    base=4*SEG+(c-4)*2*SEG
+                    own=[own[i]+dg(vt[:,base+i*SEG:base+(i+1)*SEG],pb[:,i*SEG:(i+1)*SEG],NN) for i in range(2)]
+            ot=(ot+jnp.concatenate(own,axis=1))*(1.0/l)
+            res.append(ot)
+            lse_ref[0,h:h+1,:]=m+jnp.log(l)
+        row=lax.broadcasted_iota(jnp.int32,res[0].shape,0)
+        o_ref[...]=jnp.where(row<64,res[0],res[1]).T.astype(BF)
+    @pl.when(meta[0]>0)
+    def _(): run(True)
+    @pl.when(meta[0]==0)
+    def _(): run(False)
+
+def bwd_kernel(meta, q_ref,k_ref,v_ref,do_ref,o_ref,lse_ref,dq_ref,dk_ref,dv_ref):
+    def run(trunk):
+        q=q_ref[...]*jnp.asarray(0.125,BF)
+        do=do_ref[...]
+        lane=lax.broadcasted_iota(jnp.int32,q.shape,1)
+        zero=jnp.asarray(0,BF)
+        dd=(do.astype(F32)*o_ref[...].astype(F32)).T
+        kt=k_ref[...].T
+        qh=[jnp.where((lane<64)==(h==0),q,zero) for h in range(2)]
+        doh=[jnp.where((lane<64)==(h==0),do,zero) for h in range(2)]
+        delta=[jnp.sum(dd[h*64:(h+1)*64],axis=0,keepdims=True) for h in range(2)]
+        qcat=jnp.concatenate(qh,axis=0); docat=jnp.concatenate(doh,axis=0)
+        dqt=[jnp.zeros((128,2*SEG),F32)]*2
+        own=[[jnp.zeros((128,SEG),F32)]*2]*2
+        for c in chunks_of(trunk):
+            pbs=[];dsbs=[]
+            for h in range(2):
+                st=score_chunk(c,trunk,k_ref,qh[h],meta)
+                p=jnp.exp(st-lse_ref[0,h:h+1,:])
+                if c<4:
+                    dp=dg(v_ref[c*SEG:(c+1)*SEG,:],doh[h],NT)
+                else:
+                    base=4*SEG+(c-4)*2*SEG
+                    dp=jnp.concatenate([dg(v_ref[base+i*SEG:base+(i+1)*SEG,:],doh[h][i*SEG:(i+1)*SEG,:],NT) for i in range(2)],axis=1)
+                ds=p*(dp-delta[h])
+                pbs.append(p.astype(BF)); dsbs.append(ds.astype(BF))
+            if c<4:
+                r=slice(c*SEG,(c+1)*SEG)
+                dv_ref[r,:]=dg(jnp.concatenate(pbs,axis=1),docat,NN).astype(BF)
+                dk_ref[r,:]=dg(jnp.concatenate(dsbs,axis=1),qcat,NN).astype(BF)
+                for h in range(2): dqt[h]=dqt[h]+dg(kt[:,r],dsbs[h],NN)
+            else:
+                base=4*SEG+(c-4)*2*SEG
+                for i in range(2):
+                    r=slice(base+i*SEG,base+(i+1)*SEG); cc=slice(i*SEG,(i+1)*SEG)
+                    dv_ref[r,:]=dg(jnp.concatenate([x[:,cc] for x in pbs],axis=1),jnp.concatenate([x[cc] for x in doh],axis=0),NN).astype(BF)
+                    dk_ref[r,:]=dg(jnp.concatenate([x[:,cc] for x in dsbs],axis=1),jnp.concatenate([x[cc] for x in qh],axis=0),NN).astype(BF)
+                own=[[own[h][i]+dg(kt[:,base+i*SEG:base+(i+1)*SEG],dsbs[h][:,i*SEG:(i+1)*SEG],NN) for i in range(2)] for h in range(2)]
+        if trunk:
+            dv_ref[4*SEG:,:]=jnp.zeros((4*SEG,128),BF)
+            dk_ref[4*SEG:,:]=jnp.zeros((4*SEG,128),BF)
+        dqt=[dqt[h]+jnp.concatenate(own[h],axis=1) for h in range(2)]
+        row=lax.broadcasted_iota(jnp.int32,dqt[0].shape,0)
+        dq_ref[...]=(jnp.where(row<64,dqt[0],dqt[1]).T*0.125).astype(BF)
+    @pl.when(meta[0]>0)
+    def _(): run(True)
+    @pl.when(meta[0]==0)
+    def _(): run(False)
+
+def attn_fwd(meta,q,k,v,interpret=False):
+    n=q.shape[1]//128; nk=k.shape[0]; nq=q.shape[0]
+    gs=pltpu.PrefetchScalarGridSpec(num_scalar_prefetch=1,grid=(n,),
+        in_specs=[pl.BlockSpec((nq,128),lambda j,m:(0,j)),pl.BlockSpec((nk,128),lambda j,m:(0,j)),pl.BlockSpec((nk,128),lambda j,m:(0,j))],
+        out_specs=[pl.BlockSpec((nq,128),lambda j,m:(0,j)),pl.BlockSpec((1,2,nq),lambda j,m:(j,0,0))])
+    return pl.pallas_call(fwd_kernel,grid_spec=gs,out_shape=[jax.ShapeDtypeStruct(q.shape,BF),jax.ShapeDtypeStruct((n,2,nq),F32)],
+        cost_estimate=pl.CostEstimate(flops=2*2*12*256*256*256*12,bytes_accessed=8<<20,transcendentals=10<<20),
+        compiler_params=pltpu.CompilerParams(vmem_limit_bytes=60<<20),interpret=interpret,name="attn_fwd")(meta,q,k,v)
+def attn_bwd(meta,q,k,v,do,o,lse,interpret=False):
+    n=q.shape[1]//128; nk=k.shape[0]; nq=q.shape[0]
+    qs=pl.BlockSpec((nq,128),lambda j,m:(0,j)); ks=pl.BlockSpec((nk,128),lambda j,m:(0,j))
+    gs=pltpu.PrefetchScalarGridSpec(num_scalar_prefetch=1,grid=(n,),
+        in_specs=[qs,ks,ks,qs,qs,pl.BlockSpec((1,2,nq),lambda j,m:(j,0,0))],
+        out_specs=[qs,ks,ks])
+    return pl.pallas_call(bwd_kernel,grid_spec=gs,out_shape=[jax.ShapeDtypeStruct(q.shape,BF),jax.ShapeDtypeStruct(k.shape,BF),jax.ShapeDtypeStruct(k.shape,BF)],
+        cost_estimate=pl.CostEstimate(flops=5*2*12*256*256*256*12,bytes_accessed=16<<20,transcendentals=10<<20),
+        compiler_params=pltpu.CompilerParams(vmem_limit_bytes=60<<20),interpret=interpret,name="attn_bwd")(meta,q,k,v,do,o,lse)
+
+
+def row_norm(values):
+    centre = values - jnp.mean(values, axis=-1, keepdims=True)
+    spread = jnp.mean(centre * centre, axis=-1, keepdims=True)
+    scale = lax.rsqrt(spread + EPSILON)
+    return centre * scale, scale
+
+
+def row_norm_back(unit, scale, scaled):
+    mean_one = jnp.mean(scaled, axis=-1, keepdims=True)
+    mean_two = jnp.mean(scaled * unit, axis=-1, keepdims=True)
+    return scale * (scaled - mean_one - unit * mean_two)
+
+
+def call(kernel, name, grid, ins, outs, scratch=(), prefetch=0, flops=0, size=16 << 20, args=()):
+    grid_spec = pltpu.PrefetchScalarGridSpec(
+        num_scalar_prefetch=prefetch,
+        grid=grid,
+        in_specs=ins,
+        out_specs=[spec for spec, unused in outs],
+        scratch_shapes=list(scratch),
+    )
+    return pl.pallas_call(
+        kernel,
+        grid_spec=grid_spec,
+        out_shape=[jax.ShapeDtypeStruct(*shape) for unused, shape in outs],
+        cost_estimate=pl.CostEstimate(flops=flops, bytes_accessed=size, transcendentals=0),
+        compiler_params=pltpu.CompilerParams(vmem_limit_bytes=58 << 20),
+        name=name,
+    )(*args)
+
+
+def whole(shape):
+    return pl.BlockSpec(shape, lambda *unused: (0,) * len(shape))
+
+
+def join_kernel(pieces_ref, qkv_ref, out_ref):
+    cols = pieces_ref.shape[1]
+    cut = qkv_ref.shape[1] // cols
+    qkv_ref[...] = jnp.concatenate([pieces_ref[0, c, :, :cut] for c in range(cols)], axis=1)
+    out_ref[...] = jnp.concatenate([pieces_ref[0, c, :, cut:] for c in range(cols)], axis=1)
+
+
+def join_pieces(pieces, height):
+    rows, cols, unused, width = pieces.shape
+    full = rows * height
+    return call(
+        join_kernel,
+        "join_pieces",
+        (rows,),
+        [pl.BlockSpec((1, cols, height, width), lambda r: (r, 0, 1, 0))],
+        [
+            (pl.BlockSpec((height, 3 * full), lambda r: (r, 0)), ((full, 3 * full), BF)),
+            (pl.BlockSpec((height, full), lambda r: (r, 0)), ((full, full), BF)),
+        ],
+        args=(pieces,),
+    )
+
+
+def project_kernel(a_ref, b_ref, c_ref, d_ref, small_ref, weight_ref, q_ref, k_ref, v_ref, n_ref):
+    step = pl.program_id(0)
+    width = a_ref.shape[1]
+
+    def run(ref, last):
+        unit, unused = row_norm(ref[...].astype(F32))
+        normed = (unit * small_ref[0:1] + small_ref[2:3]).astype(BF)
+        n_ref[...] = normed
+        k_ref[...] = dg(normed, weight_ref[:, width : 2 * width], NN).astype(BF)
+        v_ref[...] = (dg(normed, weight_ref[:, 2 * width :], NN) + small_ref[5:6]).astype(BF)
+        if last:
+            q_ref[...] = (dg(normed, weight_ref[:, :width], NN) + small_ref[4:5]).astype(BF)
+
+    for i, ref in enumerate((a_ref, b_ref, c_ref, d_ref)):
+
+        @pl.when(step == i)
+        def _(ref=ref, i=i):
+            run(ref, i == 3)
+
+
+def project(sources, small, qkv):
+    tokens, width = sources[0].shape
+    block = pl.BlockSpec((tokens, width), lambda i: (i, 0))
+    tall = ((4 * tokens, width), BF)
+    return call(
+        project_kernel,
+        "project",
+        (4,),
+        [whole((tokens, width))] * 4 + [whole(small.shape), whole(qkv.shape)],
+        [(whole((tokens, width)), ((tokens, width), BF)), (block, tall), (block, tall), (block, tall)],
+        flops=2 * 9 * tokens * width * width,
+        args=(*sources, small, qkv),
+    )
+
+
+def unproject_kernel(a_ref, b_ref, c_ref, dk_ref, dv_ref, small_ref, weight_ref, part_ref, terms_ref):
+    step = pl.program_id(0)
+    width = a_ref.shape[1]
+
+    @pl.when(step == 0)
+    def _():
+        terms_ref[...] = jnp.zeros_like(terms_ref)
+
+    dk, dv = dk_ref[...], dv_ref[...]
+    grad = dg(dk, weight_ref[:, width : 2 * width], NT) + dg(dv, weight_ref[:, 2 * width :], NT)
+    part_ref[...] = grad.astype(BF)
+    terms_ref[1:2] += jnp.sum(grad, axis=0, keepdims=True)
+    terms_ref[2:3] += jnp.sum(dv.astype(F32), axis=0, keepdims=True)
+    for i, ref in enumerate((a_ref, b_ref, c_ref)):
+
+        @pl.when(step == i)
+        def _(ref=ref):
+            unit, unused = row_norm(ref[...].astype(F32))
+            terms_ref[0:1] += jnp.sum(grad * unit, axis=0, keepdims=True)
+
+
+def unproject(sources, dk, dv, small, qkv):
+    tokens, width = sources[0].shape
+    block = pl.BlockSpec((tokens, width), lambda i: (i, 0))
+    return call(
+        unproject_kernel,
+        "unproject",
+        (3,),
+        [whole((tokens, width))] * 3 + [block, block, whole(small.shape), whole(qkv.shape)],
+        [(block, ((3 * tokens, width), BF)), (whole((8, width)), ((8, width), F32))],
+        flops=2 * 6 * tokens * width * width,
+        args=(*sources, dk, dv, small, qkv),
+    )
+
+
+def weigh_kernel(
+    me, dq_ref, dk_ref, dv_ref, n_ref, tokens_ref, grad_out_ref, weight_ref,
+    own_ref, other_ref, grad_ref, terms_ref, kept, turned,
+):
+    step = pl.program_id(0)
+    tokens, width = dq_ref.shape
+
+    @pl.when(step == 0)
+    def _():
+        dq, dk, dv = dq_ref[...], dk_ref[-tokens:], dv_ref[-tokens:]
+        grad = (
+            dg(dq, weight_ref[:, :width], NT)
+            + dg(dk, weight_ref[:, width : 2 * width], NT)
+            + dg(dv, weight_ref[:, 2 * width :], NT)
+        )
+        grad_ref[...] = grad
+        unit, unused = row_norm(tokens_ref[...].astype(F32))
+        terms_ref[...] = jnp.zeros_like(terms_ref)
+        terms_ref[0:1] = jnp.sum(grad * unit, axis=0, keepdims=True)
+        terms_ref[1:2] = jnp.sum(grad, axis=0, keepdims=True)
+        terms_ref[2:3] = jnp.sum(dv.astype(F32), axis=0, keepdims=True)
+        terms_ref[3:4] = jnp.sum(dq.astype(F32), axis=0, keepdims=True)
+        turned[...] = n_ref[...].T
+        kept[:, :width] = dg(turned[:, -tokens:], dq, NN).astype(BF)
+
+    @pl.when(step == 1)
+    def _():
+        kept[:, width : 2 * width] = dg(turned[...], dk_ref[...], NN).astype(BF)
+
+    @pl.when(step == 2)
+    def _():
+        kept[:, 2 * width :] = dg(turned[...], dv_ref[...], NN).astype(BF)
+        height = own_ref.shape[1]
+        cols = own_ref.shape[0] // 2
+        tall, low_part = 3 * width // cols, width // cols
+        for c in range(cols):
+            parts = [
+                jnp.concatenate(
+                    [
+                        kept[r * height : (r + 1) * height, c * tall : (c + 1) * tall],
+                        grad_out_ref[r * height : (r + 1) * height, c * low_part : (c + 1) * low_part],
+                    ],
+                    axis=1,
+                )
+                for r in range(4)
+            ]
+            a, c_part = in_order(me[1], parts[0], parts[2])
+            b, d_part = in_order(me[1], parts[1], parts[3])
+            for y_step, pair in ((0, (a, b)), (1, (c_part, d_part))):
+                mine, theirs = in_order(me[2], *pair)
+                own_ref[place_of(c, y_step, me[2], me)] = mine
+                other_ref[place_of(c, y_step, me[2] ^ 1, me)] = theirs
+
+
+def weigh(me, dq, dk, dv, normed, tokens, grad_out, qkv, cols):
+    count, width = dq.shape
+    shape = (2 * cols, width // 4, 4 * width // cols)
+    return call(
+        weigh_kernel,
+        "weigh",
+        (3,),
+        [whole(x.shape) for x in (dq, dk, dv, normed, tokens, grad_out, qkv)],
+        [
+            (whole(shape), (shape, BF)),
+            (whole(shape), (shape, BF)),
+            (whole((count, width)), ((count, width), F32)),
+            (whole((8, width)), ((8, width), F32)),
+        ],
+        scratch=[pltpu.VMEM((width, 3 * width), BF), pltpu.VMEM((width, normed.shape[0]), BF)],
+        prefetch=1,
+        flops=2 * 12 * count * width * width,
+        args=(me, dq, dk, dv, normed, tokens, grad_out, qkv),
+    )
+
+
+def finish_kernel(
+    meta, trunk_ref, near_ref, far_ref, own_ref, mixed_ref, tokens_ref, small_ref, out_ref
+):
+    received = []
+    for i in range(2):
+        slot = meta[1 + i]
+        place = pl.ds(pl.multiple_of((jnp.maximum(slot, 0) & 1) * SEG, SEG), SEG)
+        branch = jnp.where(slot >= 2, far_ref[place, :], near_ref[place, :]).astype(F32)
+        branch = jnp.where(slot >= 0, branch, 0.0)
+        trunk = trunk_ref[i * SEG : (i + 1) * SEG, :].astype(F32)
+        received.append(jnp.where(meta[0] == 0, trunk, branch))
+    grad = own_ref[...] + jnp.concatenate(received, axis=0)
+    unit, scale = row_norm(tokens_ref[...].astype(F32))
+    back = row_norm_back(unit, scale, grad * small_ref[0:1])
+    out_ref[...] = (mixed_ref[...] + back).astype(BF)
+
+
+def finish(meta, trunk, near, far, own, mixed, tokens, small):
+    return call(
+        finish_kernel,
+        "finish",
+        (1,),
+        [whole(x.shape) for x in (trunk, near, far, own, mixed, tokens, small)],
+        [(whole(tokens.shape), (tokens.shape, BF))],
+        prefetch=1,
+        args=(meta, trunk, near, far, own, mixed, tokens, small),
+    )[0]
+
+
+def gelu_parts(v):
+    x = v * 0.7071067811865476
+    chance = 0.5 + 0.5 * lax.erf(x)
+    density = jnp.exp(-x * x) * 0.3989422804014327
+    return chance, v * density
+
+
+def feed_kernel(
+    tokens_ref, attended_ref, out_ref, small_ref, upstream_ref, up_ref, down_ref, shift_ref,
+    output_ref, grad_mixed_ref, grad_att_ref, grad_out_ref, sums_ref, terms_ref, grads_ref,
+    second_ref, second_t, upstream_t, mixed_ref, sum_ref, back_ref,
+    up_slot, down_slot, up_sem, down_sem,
+):
+    step = pl.program_id(0)
+    last = pl.num_programs(0) - 1
+    slot = step % 2
+    height, width = up_ref.shape[2], up_ref.shape[3]
+
+    @pl.when(step == 0)
+    def _():
+        mixed = (
+            tokens_ref[...].astype(F32) + dg(attended_ref[...], out_ref[...], NN)
+        ) + small_ref[6:7]
+        mixed_ref[...] = mixed
+        unit, unused = row_norm(mixed)
+        second_ref[...] = (unit * small_ref[1:2] + small_ref[3:4]).astype(BF)
+        second_t[...] = second_ref[...].T
+        upstream_t[...] = upstream_ref[...].T
+        sum_ref[...] = jnp.zeros_like(sum_ref)
+        back_ref[...] = jnp.zeros_like(back_ref)
+
+    def up_copy(which, at):
+        return pltpu.make_async_copy(
+            up_slot.at[which],
+            grads_ref.at[:, pl.ds(2 * at, 2), pl.ds(0, height), :],
+            up_sem.at[which],
+        )
+
+    def down_copy(which, at):
+        return pltpu.make_async_copy(
+            down_slot.at[which],
+            grads_ref.at[at, :, pl.ds(height, height), :],
+            down_sem.at[which],
+        )
+
+    @pl.when(step >= 2)
+    def _():
+        up_copy(slot, step - 2).wait()
+        down_copy(slot, step - 2).wait()
+
+    full = up_ref.shape[0] * height
+    up = jnp.concatenate([up_ref[:, i].reshape(full, width) for i in range(2)], axis=1)
+    half = height // 2
+    down = jnp.concatenate(
+        [down_ref[0, :, i * half : (i + 1) * half, :].reshape(full, width) for i in range(2)],
+        axis=1,
+    )
+    second, upstream = second_ref[...], upstream_ref[...]
+    hidden = jnp.dot(second, up, preferred_element_type=F32) + shift_ref[...]
+    grad_act = jnp.dot(upstream, down, preferred_element_type=F32)
+    chance, slope = gelu_parts(hidden)
+    active = (hidden * chance).astype(BF)
+    grad_pre = grad_act * (chance + slope)
+    grad_low = grad_pre.astype(BF)
+    terms_ref[...] = jnp.sum(grad_pre, axis=0, keepdims=True)
+    sum_ref[...] += dg(active, down, NT)
+    back_ref[...] += dg(grad_low, up, NT)
+    grad_up = jnp.dot(second_t[...], grad_low, preferred_element_type=F32).astype(BF)
+    grad_down = jnp.dot(upstream_t[...], active, preferred_element_type=F32).astype(BF)
+    for i in range(2):
+        cut = slice(i * width, (i + 1) * width)
+        up_slot[slot, :, i] = grad_up[:, cut].reshape(up_ref.shape[0], height, width)
+        down_slot[slot, :, i * half : (i + 1) * half, :] = grad_down[:, cut].reshape(
+            down_ref.shape[1], half, width
+        )
+    up_copy(slot, step).start()
+    down_copy(slot, step).start()
+
+    @pl.when(step == last)
+    def _():
+        up_copy(1 - slot, step - 1).wait()
+        down_copy(1 - slot, step - 1).wait()
+        mixed = mixed_ref[...]
+        unit, scale = row_norm(mixed)
+        output_ref[...] = (mixed + sum_ref[...] + small_ref[7:8]).astype(BF)
+        grad_second = back_ref[...]
+        upstream_f = upstream_ref[...].astype(F32)
+        grad_mixed = upstream_f + row_norm_back(unit, scale, grad_second * small_ref[1:2])
+        grad_mixed_ref[...] = grad_mixed
+        mixed_low = grad_mixed.astype(BF)
+        grad_att_ref[...] = dg(mixed_low, out_ref[...], NT).astype(BF)
+        grad_out_ref[...] = jnp.dot(
+            attended_ref[...].T, mixed_low, preferred_element_type=F32
+        ).astype(BF)
+        sums_ref[...] = jnp.zeros_like(sums_ref)
+        sums_ref[0:1] = jnp.sum(grad_second * unit, axis=0, keepdims=True)
+        sums_ref[1:2] = jnp.sum(grad_second, axis=0, keepdims=True)
+        sums_ref[2:3] = jnp.sum(grad_mixed, axis=0, keepdims=True)
+        sums_ref[3:4] = jnp.sum(upstream_f, axis=0, keepdims=True)
+        up_copy(slot, step).wait()
+        down_copy(slot, step).wait()
+
+
+def feed_forward(tokens_in, attended, w_out, small, upstream, up_weights, down_weights, shift):
+    tokens, width = tokens_in.shape
+    rows, cols, half, wide = down_weights.shape
+    block = whole((tokens, width))
+    grid_spec = pltpu.PrefetchScalarGridSpec(
+        num_scalar_prefetch=0,
+        grid=(rows,),
+        in_specs=[
+            block,
+            block,
+            whole((width, width)),
+            whole(small.shape),
+            block,
+            pl.BlockSpec((rows, 2, half, wide), lambda r: (0, r, 0, 0)),
+            pl.BlockSpec((1, cols, half, wide), lambda r: (r, 0, 0, 0)),
+            pl.BlockSpec((1, 2 * wide), lambda r: (0, r)),
+        ],
+        out_specs=[
+            block,
+            block,
+            block,
+            whole((width, width)),
+            whole((8, width)),
+            pl.BlockSpec((1, 2 * wide), lambda r: (0, r)),
+            pl.BlockSpec(memory_space=pl.ANY),
+        ],
+        scratch_shapes=[
+            pltpu.VMEM((tokens, width), BF),
+            pltpu.VMEM((width, tokens), BF),
+            pltpu.VMEM((width, tokens), BF),
+            pltpu.VMEM((tokens, width), F32),
+            pltpu.VMEM((tokens, width), F32),
+            pltpu.VMEM((tokens, width), F32),
+            pltpu.VMEM((2, rows, 2, half, wide), BF),
+            pltpu.VMEM((2, cols, half, wide), BF),
+            pltpu.SemaphoreType.DMA((2,)),
+            pltpu.SemaphoreType.DMA((2,)),
+        ],
+    )
+    return pl.pallas_call(
+        feed_kernel,
+        grid_spec=grid_spec,
+        out_shape=[
+            jax.ShapeDtypeStruct((tokens, width), BF),
+            jax.ShapeDtypeStruct((tokens, width), F32),
+            jax.ShapeDtypeStruct((tokens, width), BF),
+            jax.ShapeDtypeStruct((width, width), BF),
+            jax.ShapeDtypeStruct((8, width), F32),
+            jax.ShapeDtypeStruct((1, cols * wide), F32),
+            jax.ShapeDtypeStruct((rows, cols, 2 * half, wide), BF),
+        ],
+        cost_estimate=pl.CostEstimate(
+            flops=12 * tokens * width * cols * wide,
+            bytes_accessed=24 << 20,
+            transcendentals=2 * tokens * cols * wide,
+        ),
+        compiler_params=pltpu.CompilerParams(vmem_limit_bytes=60 << 20),
+        name="feed_forward",
+    )(tokens_in, attended, w_out, small, upstream, up_weights, down_weights, shift)
+
+
+def swap(value, axis, bit):
+    size = lax.axis_size(axis)
+    return lax.ppermute(value, axis, [(i, i ^ bit) for i in range(size)])
+
+
+def exchange(value, first):
+    rows, cols = lax.axis_size("row"), lax.axis_size("col")
+    pairs = []
+    for r in range(rows):
+        for c in range(cols):
+            along_x = (r & 1 == 0) == first
+            other = (r, c ^ 1) if along_x else (r ^ 2, c)
+            pairs.append((r * cols + c, other[0] * cols + other[1]))
+    return lax.ppermute(value, ("row", "col"), pairs)
+
+
+def add_low(a, b):
+    return (a.astype(jnp.float32) + b.astype(jnp.float32)).astype(jnp.bfloat16)
+
+
+def place_of(col_index, y_step, of_core, me):
+    d = col_index ^ me[0]
+    x_step = d & 1
+    near = jnp.where(of_core == 0, x_step, y_step)
+    far = jnp.where(of_core == 0, y_step, x_step)
+    return (d >> 1) | (near << 2) | (far << 3)
+
+
+def in_order(flag, first, second):
+    return jnp.where(flag > 0, second, first), jnp.where(flag > 0, first, second)
+
+
+def halves(value, flags):
+    return [
+        jnp.where(flags[i] > 0, value[i * SEG : (i + 1) * SEG], jnp.zeros((), value.dtype))
+        for i in range(2)
+    ]
+
+
+def placed(value, targets, numbers):
+    out = []
+    for number in numbers:
+        parts = halves(value, [(targets[i] == number).astype(jnp.int32) for i in range(2)])
+        out.append(parts[0] + parts[1])
+    return jnp.concatenate(out, axis=0)
+
+
+def level_move(value, pairs):
+    cols = lax.axis_size("col")
+    x_size = 2
+    full = [
+        (a * x_size + x, b * x_size + x)
+        for a, b in pairs
+        for x in range(x_size)
+        if max(a, b) * x_size < cols
+    ]
+    return lax.ppermute(value, "col", full)
+
+
+def share_tokens(tokens, own_slot, level):
+    branch = placed(tokens, own_slot, (0, 1)) + swap(placed(tokens, own_slot, (2, 3)), "col", 1)
+    hop = level_move(tokens, [(0, 2)])
+    moved = level_move(
+        jnp.where(level == 1, branch, jnp.where(level == 0, tokens, hop)), [(0, 1), (1, 2), (2, 3)]
+    )
+    down = level_move(branch, [(3, 2)])
+    trunk = jnp.where(level == 0, tokens, jnp.where(level == 2, hop, moved))
+    branch_up = branch + jnp.where(level == 2, moved, jnp.zeros((), moved.dtype))
+    up_two = level_move(branch_up, [(2, 3)])
+    down_two = level_move(branch + down, [(2, 1)])
+    trunk_far = swap(trunk, "col", 1)
+    branch = (branch_up + down) + (up_two + down_two)
+    return trunk, trunk_far, branch, swap(branch, "col", 1)
+
+
+def together(*values):
+    return lax.optimization_barrier(values)
+
+
+def tail_rounds(part, parent_slot, level, make_pieces, vectors_of):
+    parent_part = part[4 * SEG :]
+    keep, send = (placed(parent_part, parent_slot, pair) for pair in ((0, 1), (2, 3)))
+    trunk, trunk_send, send = together(part[: 2 * SEG], part[2 * SEG : 4 * SEG], send)
+    branch_in = swap(send, "col", 1)
+    own, other, extra = make_pieces(trunk)
+    terms = vectors_of(extra)
+
+    branch = add_low(keep, branch_in)
+    branch, trunk_send, other, terms = together(branch, trunk_send, other, terms)
+    moves = (
+        level_move(branch, [(1, 2)]),
+        level_move(branch, [(3, 2)]),
+        swap(trunk_send, "col", 1),
+        swap(other, "row", 1),
+        swap(terms, "row", 1),
+    )
+    up, down, trunk_in, own_in, terms_in = together(*moves)
+
+    branch_up, branch_down = add_low(branch, up), add_low(branch, down)
+    trunk = add_low(trunk, trunk_in)
+    half = own.shape[0] // 2
+    held = add_low(own[:half], own_in[:half])
+    leaving = add_low(own[half:], own_in[half:])
+    terms = terms + terms_in
+    branch_up, branch_down, trunk, leaving, terms = together(
+        branch_up, branch_down, trunk, leaving, terms
+    )
+    moves = (
+        level_move(branch_up, [(2, 3)]),
+        level_move(branch_down, [(2, 1)]),
+        level_move(trunk, [(1, 0), (3, 2)]),
+        exchange(leaving, False),
+        swap(terms, "row", 2),
+    )
+    up_two, down_two, trunk_in, held_in, terms_in = together(*moves)
+
+    branch = (
+        branch_up.astype(jnp.float32)
+        + down.astype(jnp.float32)
+        + up_two.astype(jnp.float32)
+        + down_two.astype(jnp.float32)
+    ).astype(jnp.bfloat16)
+    trunk = add_low(trunk, trunk_in)
+    half = half // 2
+    leaving = add_low(held[half:], held_in[half:])
+    held = add_low(held[:half], held_in[:half])
+    terms = terms + terms_in
+    branch, trunk, leaving, terms = together(branch, trunk, leaving, terms)
+    moves = (
+        level_move(trunk, [(2, 0)]),
+        swap(branch, "col", 1),
+        exchange(leaving, True),
+        swap(terms, "col", 1),
+    )
+    trunk_in, branch_far, held_in, terms_in = together(*moves)
+
+    trunk = add_low(trunk, trunk_in)
+    terms = terms + terms_in
+    leaving = [add_low(held[k], held_in[k]) for k in range(1, 4)]
+    kept = held[0].astype(jnp.float32) + held_in[0].astype(jnp.float32)
+    *leaving, terms = together(*leaving, terms)
+    moves = [swap(leaving[k - 1], "col", 2 * k) for k in range(1, 4)]
+    terms_in = swap(terms, "col", 4)
+    for moved in moves:
+        kept = kept + moved.astype(jnp.float32)
+    terms = terms + terms_in
+    terms = terms + swap(terms, "col", 2)
+    return trunk, branch, branch_far, kept, terms, extra
+
+
+def tree_body(
+    tokens, parents, w_qkv, w_out, w_up, w_down, ln_gain, ln_bias, proj_bias, ff_bias, cotangent
+):
+    row, col = lax.axis_index("row"), lax.axis_index("col")
+    rows, cols = lax.axis_size("row"), lax.axis_size("col")
+    local_rows = tokens.shape[0]
+    side, level = col & 1, col >> 1
+    me = jnp.stack([col, row >> 1, row & 1]).astype(jnp.int32)
+
+    parent = parents[0]
+    numbers = jnp.arange(SEGS, dtype=jnp.int32)
+    is_branch = (numbers >= 4) & (parent == 3)
+    slots = jnp.cumsum(is_branch.astype(jnp.int32)) - 1
+    own_parent = [parent[2 * col + i] for i in range(2)]
+    is_leaf = [(own_parent[i] >= 4) for i in range(2)]
+    own_slot = [
+        jnp.where(is_branch[2 * col + i], slots[2 * col + i] ^ (2 * side), -1) for i in range(2)
+    ]
+    parent_slot = [
+        jnp.where(is_leaf[i], slots[jnp.maximum(own_parent[i], 0)] ^ (2 * side), -1)
+        for i in range(2)
+    ]
+    meta = jnp.stack(
+        [
+            (col < 2).astype(jnp.int32),
+            col.astype(jnp.int32) * local_rows,
+            is_leaf[0].astype(jnp.int32),
+            is_leaf[1].astype(jnp.int32),
+            2 * side.astype(jnp.int32),
+        ]
+    )
+
+    narrow, wide = w_up.shape
+    with jax.named_scope("gather_early_weights"):
+        vectors = jnp.concatenate(
+            [ln_gain, ln_bias, proj_bias, ff_bias.reshape(-1, ln_gain.shape[1])], axis=0
+        ).reshape(-1, wide)
+        count = vectors.shape[0]
+        early = jnp.concatenate(
+            [
+                w_up,
+                jnp.concatenate([w_qkv, w_out], axis=1),
+                vectors,
+                jnp.zeros((16 - count, wide), vectors.dtype),
+            ],
+            axis=0,
+        )
+        early = lax.all_gather(early, ("row", "col"), axis=0, tiled=False)
+        early = early.reshape(rows, cols, *early.shape[1:])
+        vectors = early[0, :, 2 * narrow : 2 * narrow + count]
+        vectors = vectors.reshape(cols, -1, ln_gain.shape[1])
+        small = vectors[:, :8].transpose(1, 0, 2).reshape(8, D).astype(jnp.float32)
+        ff_shift = vectors[:, 8:].reshape(1, -1).astype(jnp.float32)
+        full_qkv, full_out = join_pieces(early, narrow)
+    with jax.named_scope("gather_tokens"):
+        trunk, trunk_far, branch, branch_far = share_tokens(tokens, own_slot, level)
+        branch = jnp.concatenate([branch, branch_far], axis=0)
+        parent_tokens = jnp.concatenate(
+            [
+                lax.dynamic_slice_in_dim(branch, jnp.maximum(parent_slot[i], 0) * SEG, SEG, 0)
+                for i in range(2)
+            ],
+            axis=0,
+        )
+    with jax.named_scope("gather_late_weights"):
+        late = jnp.concatenate([w_down.T[:, :wide], w_down.T[:, wide:]], axis=0)
+        late = lax.all_gather(late, ("row", "col"), axis=0, tiled=False)
+        late = late.reshape(rows, cols, *late.shape[1:])
+
+    sources = (trunk, trunk_far, parent_tokens, tokens)
+    queries, key_rows, value_rows, normed = project(sources, small, full_qkv)
+    attended, log_total = attn_fwd(meta, queries, key_rows, value_rows)
+    output, grad_mixed, grad_att, grad_out, sums, ff_terms, late_grads = feed_forward(
+        tokens, attended, full_out, small, cotangent, early, late, ff_shift
+    )
+    with jax.named_scope("scatter_late_weights"):
+        late_sum = lax.psum_scatter(
+            late_grads.reshape(rows * cols, *late_grads.shape[2:]),
+            ("row", "col"),
+            scatter_dimension=0,
+            tiled=False,
+        ).astype(jnp.float32)
+        up_rows, down_rows = w_up.shape[0], w_down.shape[1]
+        grad_w_up = late_sum[:up_rows]
+        grad_w_down = jnp.concatenate(
+            [late_sum[up_rows : up_rows + down_rows], late_sum[up_rows + down_rows :]], axis=1
+        ).T
+    grad_q, grad_k, grad_v = attn_bwd(
+        meta, queries, key_rows, value_rows, grad_att, attended, log_total
+    )
+    part, part_terms = unproject(sources[:3], grad_k, grad_v, small, full_qkv)
+
+    def make_pieces(after):
+        dq, dk, dv, unused = together(grad_q, grad_k, grad_v, after)
+        own, other, grad_normed, own_terms = weigh(
+            me, dq, dk, dv, normed, tokens, grad_out, full_qkv, cols
+        )
+        return own, other, (grad_normed, own_terms)
+
+    def vectors_of(extra):
+        return jnp.concatenate([part_terms + extra[1], sums, ff_terms.reshape(-1, D)], axis=0)
+
+    with jax.named_scope("sum_gradients"):
+        trunk_grad, branch_grad, branch_grad_far, early_sum, terms, extra = tail_rounds(
+            part, parent_slot, level, make_pieces, vectors_of
+        )
+    tall = w_qkv.shape[1]
+    grad_w_qkv, grad_w_out = early_sum[:, :tall], early_sum[:, tall:]
+    finish_meta = jnp.stack([level, own_slot[0], own_slot[1]]).astype(jnp.int32)
+    grad_tokens = finish(
+        finish_meta, trunk_grad, branch_grad, branch_grad_far, extra[0], grad_mixed, tokens, small
+    )
+    with jax.named_scope("vectors"):
+        cut = ln_gain.shape[1]
+        mine = lax.dynamic_slice_in_dim(terms[:16], col * cut, cut, 1)
+        grad_ff = lax.dynamic_slice_in_dim(
+            terms[16:].reshape(-1), col * ff_bias.shape[0], ff_bias.shape[0], 0
+        )
+        grad_gain = jnp.stack([mine[0], mine[8]])
+        grad_shift = jnp.stack([mine[1], mine[9]])
+        grad_bias = jnp.stack([mine[3], mine[2], mine[10], mine[11]])
+    return (
+        output,
+        grad_tokens,
+        grad_w_qkv,
+        grad_w_out,
+        grad_w_up,
+        grad_w_down,
+        grad_gain,
+        grad_shift,
+        grad_bias,
+        grad_ff,
+    )
+
+
 def solution(mesh):
+    fits = mesh.shape["col"] == 8 and mesh.shape["row"] == 4
+    body = tree_body if fits else plain_body
     return jax.shard_map(
         body,
         mesh=mesh,

time: 1630 us -> 426 us (0.26)
  waiting for transfers between devices: 881 us -> 209 us
  matrix products: 386 us -> 0 us
  blocking collectives: 175 us -> 0 us
  Pallas kernels: 0 us -> 116 us
  local copies, waits for them, and re-layouts: 94.5 us -> 13.1 us
  other arithmetic: 66.6 us -> 26.3 us
  starting transfers between devices: 1.32 us -> 35.9 us
    reduce_scatter x7 -> x1, waiting for transfers between devices: 442 us -> 0.01 us  [tree_body(): lax.psum_scatter(late_grads.reshape(rows * cols, *late_grads.shape[2:]),...]
    dot_general x98 -> x0, matrix products: 386 us -> none  [the longest x16 86.3 us: scores_of(): jnp.einsum('qhd,khd->hqk', query_block, key_block, preferred_element_type...]
    unnamed x27 -> x3, waiting for transfers between devices: 316 us -> 0.05 us
    ppermute x0 -> x28, waiting for transfers between devices: none -> 182 us  [the longest x15 108 us: swap(): return lax.ppermute(value, axis, [(i, i ^ bit) for i in range(size)])]
    all_gather x6 -> x0, blocking collectives: 147 us -> none  [the longest x1 35.3 us: body(): lax.all_gather(w_qkv, 'col', axis=1, tiled=True)]
    pallas_call x0 -> x8, Pallas kernels: none -> 116 us  [the longest x5 53.3 us: call(): pl.pallas_call(kernel, grid_spec=grid_spec, out_shape=[jax.ShapeDtypeStru...]
    all_gather x8 -> x2, waiting for transfers between devices: 123 us -> 27.6 us  [the longest x1 27.6 us: tree_body(): late = lax.all_gather(late, ('row', 'col'), axis=0, tiled=False)]
    unnamed x108 -> x24, local copies, waits for them, and re-layouts: 45.3 us -> 3.5 us
  transfers between devices with their start and end apart: 21 -> 31, of which waited for: 16 -> 12; matrix products, arithmetic and copies ran while one was open for 16% -> 7% of each run, Pallas kernels for 0% -> 21%
where the time goes in v2:
time: 426 us; the launch traced here: 422 us
  waiting for transfers between devices  209 us (49%)
  Pallas kernels  116 us (27%)
  starting transfers between devices  35.9 us (8%)
  other arithmetic  26.3 us (6%)
  between operations  20.9 us (5%)
  local copies, waits for them, and re-layouts  13.1 us (3%)
    ppermute x15, waiting for transfers between devices, swap(): return lax.ppermute(value, axis, [(i, i ^ bit) for i in range(size)])  108 us
    ppermute x11, waiting for transfers between devices, level_move(): return lax.ppermute(value, 'col', full)  73.7 us
    pallas_call x5, Pallas kernels, call(): pl.pallas_call(kernel, grid_spec=grid_spec, out_shape=[jax.ShapeDtypeStru...  53.3 us
    all_gather x1, waiting for transfers between devices, tree_body(): late = lax.all_gather(late, ('row', 'col'), axis=0, tiled=False)  27.6 us
    pallas_call x1, Pallas kernels, feed_forward(): pl.pallas_call(feed_kernel, grid_spec=grid_spec, out_shape=[jax.ShapeDtyp...  25.5 us
    pallas_call x1, Pallas kernels, attn_bwd(): pl.pallas_call(bwd_kernel, grid_spec=gs, out_shape=[jax.ShapeDtypeStruct(...  21.6 us
    ppermute x15, starting transfers between devices, swap(): return lax.ppermute(value, axis, [(i, i ^ bit) for i in range(size)])  18.8 us
    pallas_call x1, Pallas kernels, attn_fwd(): pl.pallas_call(fwd_kernel, grid_spec=gs, out_shape=[jax.ShapeDtypeStruct(...  15.4 us
  transfers between devices with their start and end apart: 31, of which 12 were waited for; matrix products, arithmetic and copies ran while one was open for 7% of the time, Pallas kernels for 21%

profile of v2, /device:TPU:0, one launch (start us, length us, event | category | flops | bytes accessed | tf_op | source)
XLA Modules:
  0.0 421.5 jit_solution(6034517911695580179)
XLA Ops:
  7.2 0.8 reshape.147
  8.1 0.7 pad_maximum_fusion.5
  9.0 1.9 maximum_maximum_fusion
  10.9 0.9 fusion.15
  11.8 0.7 pad_maximum_fusion.3
  18.6 0.9 pad_maximum_fusion
  19.5 2.9 collective-permute-start.1
  22.4 4.5 %collective-permute-start = (bf16[512,768]{1,0:T(8,128)(2,1)S(1)}, bf16[512,768]{1,0:T(8,128)(2,1)S(1)}, u32[]{:S(2)}, u32[]{:S(2)}) collective-permute-start(bf16[512,768]{1,0:T(8,128)(2,1)S(1)} %copy-done), channel_id=1, source_target_pairs={{0,4},{1,5},{8,12},{9,13},{16,20},{17,21},{24,28},{25,29}} | collective-permute-start | bytes 2359304 | tf_op jit(solution)/shard_map/gather_tokens/ppermute | solution.py:902
  27.0 15.4 %collective-permute-done.1 = bf16[512,768]{1,0:T(8,128)(2,1)S(1)} collective-permute-done((bf16[512,768]{1,0:T(8,128)(2,1)}, bf16[512,768]{1,0:T(8,128)(2,1)S(1)}, u32[]{:S(2)}, u32[]{:S(2)}) %collective-permute-start.1) | collective-permute-done | bytes 786464 | tf_op jit(solution)/shard_map/gather_tokens/ppermute | solution.py:848
  42.4 9.9 %collective-permute-done = bf16[512,768]{1,0:T(8,128)(2,1)S(1)} collective-permute-done((bf16[512,768]{1,0:T(8,128)(2,1)S(1)}, bf16[512,768]{1,0:T(8,128)(2,1)S(1)}, u32[]{:S(2)}, u32[]{:S(2)}) %collective-permute-start) | collective-permute-done | bytes 786464 | tf_op jit(solution)/shard_map/gather_tokens/ppermute | solution.py:902
  52.3 2.4 select_select_fusion.1
  54.7 2.2 collective-permute-start.2
  56.9 0.7 collective-permute-start.4
  57.6 26.0 %collective-permute-done.2 = bf16[512,768]{1,0:T(8,128)(2,1)} collective-permute-done((bf16[512,768]{1,0:T(8,128)(2,1)}, bf16[512,768]{1,0:T(8,128)(2,1)}, u32[]{:S(2)}, u32[]{:S(2)}) %collective-permute-start.2) | collective-permute-done | bytes 786464 | tf_op jit(solution)/shard_map/gather_tokens/ppermute | solution.py:902
  83.7 2.2 fusion.14
  85.9 0.7 collective-permute-start.5
  86.6 0.7 collective-permute-start.6
  87.6 2.0 collective-permute-start.3
  92.9 18.5 %collective-permute-done.7 = bf16[512,768]{1,0:T(8,128)(2,1)S(1)} collective-permute-done((bf16[512,768]{1,0:T(8,128)(2,1)S(1)}, bf16[512,768]{1,0:T(8,128)(2,1)S(1)}, u32[]{:S(2)}, u32[]{:S(2)}) %collective-permute-start.7) | collective-permute-done | bytes 786464 | tf_op jit(solution)/shard_map/gather_tokens/ppermute | solution.py:848
  111.3 1.0 fusion.6
  112.4 1.0 pad_maximum_fusion.1.c_ref
  113.3 0.8 slice.193
  114.1 5.6 %join_pieces.1 = (bf16[768,2304]{1,0:T(8,128)(2,1)}, bf16[768,768]{1,0:T(8,128)(2,1)}) custom-call(bf16[4,8,400,384]{3,2,1,0:T(8,128)(2,1)} %bitcast.55), custom_call_target="tpu_custom_call" | custom-call | bytes 16777216 | tf_op jit(solution)/shard_map/gather_early_weights/join_pieces/pallas_call | solution.py:471
  119.9 0.7 reshape.157.small_ref
  120.5 0.7 reshape.158.shift_ref
  121.2 5.4 %collective-permute-done.3.b_ref = bf16[512,768]{1,0:T(8,128)(2,1)S(1)} collective-permute-done((bf16[512,768]{1,0:T(8,128)(2,1)}, bf16[512,768]{1,0:T(8,128)(2,1)S(1)}, u32[]{:S(2)}, u32[]{:S(2)}) %collective-permute-start.3) | collective-permute-done | bytes 786464 | tf_op jit(solution)/shard_map/gather_tokens/ppermute | solution.py:848
  126.7 0.9 copy-done.11
  127.5 12.4 %project.1 = (bf16[512,768]{1,0:T(8,128)(2,1)}, bf16[2048,768]{1,0:T(8,128)(2,1)}, bf16[2048,768]{1,0:T(8,128)(2,1)}, bf16[2048,768]{1,0:T(8,128)(2,1)}) custom-call(bf16[512,768]{1,0:T(8,128)(2,1)} %get-tuple-element.153.a_ref, bf16[512,768]{1,0:T(8,128)(2,1)} %copy-done.11, bf16[512,768]{1,0:T(8,128)(2,1)} %pad_maximum_fusion.1.c_ref, ...), custom_call_target="tpu_custom_call" | custom-call | flops 5435817984 | bytes 16777216 | tf_op jit(solution)/shard_map/project/pallas_call | solution.py:471
  140.0 15.4 %attn_fwd.1 = (bf16[512,768]{1,0:T(8,128)(2,1)}, f32[6,2,512]{2,1,0:T(2,128)}) custom-call(s32[5]{0:T(128)} %stack.69.meta, bf16[512,768]{1,0:T(8,128)(2,1)} %get-tuple-element.72.q_ref, bf16[2048,768]{1,0:T(8,128)(2,1)} %get-tuple-element.73.k_ref, bf16[2048,768]{1,0:T(8,128)(2,1)} %get-tuple-element.74.v_ref), custom_call_target="tpu_custom_call" | custom-call | flops 9663676416 | bytes 8388608 | tf_op jit(solution)/shard_map/attn_fwd/pallas_call | solution.py:436
  155.4 27.6 %all-gather.7.cloned.1.call-done = bf16[6144,384]{1,0:T(8,128)(2,1)} async-done(((bf16[192,384]{1,0:T(8,128)(2,1)}), bf16[6144,384]{1,0:T(8,128)(2,1)}) %all-gather.7.cloned.1.call-update) | async-done | bytes 4718608 | tf_op jit(solution)/shard_map/gather_late_weights/all_gather | solution.py:1062
  183.0 25.5 %feed_forward.1 = (bf16[512,768]{1,0:T(8,128)(2,1)}, f32[512,768]{1,0:T(8,128)}, bf16[512,768]{1,0:T(8,128)(2,1)}, bf16[768,768]{1,0:T(8,128)(2,1)}, f32[8,768]{...) custom-call(bf16[512,768]{1,0:T(8,128)(2,1)} %tokens_ref.5, ...), custom_call_target="tpu_custom_call" | custom-call | flops 14495514624 | bytes 25165824 | tf_op jit(solution)/shard_map/feed_forward/pallas_call | solution.py:824
  209.1 21.6 %attn_bwd.1 = (bf16[512,768]{1,0:T(8,128)(2,1)}, bf16[2048,768]{1,0:T(8,128)(2,1)}, bf16[2048,768]{1,0:T(8,128)(2,1)}) custom-call(s32[5]{0:T(128)} %stack.69.meta, bf16[512,768]{1,0:T(8,128)(2,1)} %get-tuple-element.72.q_ref, bf16[2048,768]{1,0:T(8,128)(2,1)} %get-tuple-element.73.k_ref, bf16[2048,768]{1,0:T(8,128)(2,1)} %get-tuple-element.74.v_ref, ...), custom_call_target="tpu_custom_call" | custom-call | flops 24159191040 | bytes 16777216 | tf_op jit(solution)/shard_map/attn_bwd/pallas_call | solution.py:445
  230.8 10.5 %unproject.1 = (bf16[1536,768]{1,0:T(8,128)(2,1)}, f32[8,768]{1,0:T(8,128)}) custom-call(bf16[512,768]{1,0:T(8,128)(2,1)} %get-tuple-element.153.a_ref, bf16[512,768]{1,0:T(8,128)(2,1)} %copy-done.11, bf16[512,768]{1,0:T(8,128)(2,1)} %pad_maximum_fusion.1.c_ref, bf16[2048,768]{1,0:T(8,128)(2,1)} %get-tuple-element.88.dk_ref, ...), custom_call_target="tpu_custom_call" | custom-call | flops 3623878656 | bytes 16777216 | tf_op jit(solution)/shard_map/unproject/pallas_call | solution.py:471
  241.3 1.5 select_add_fusion.4
  244.0 0.7 reduce.3
  244.7 1.5 collective-permute-start.8
  246.2 19.1 %weigh.1 = (bf16[16,192,384]{2,1,0:T(8,128)(2,1)}, bf16[16,192,384]{2,1,0:T(8,128)(2,1)}, f32[512,768]{1,0:T(8,128)}, f32[8,768]{1,0:T(8,128)}) custom-call(s32[3]{0:T(128)} %pad_add_fusion.1.me, bf16[512,768]{1,0:T(8,128)(2,1)} %get-tuple-element.87.dq_ref, bf16[2048,768]{1,0:T(8,128)(2,1)} %get-tuple-element.88.dk_ref, ...), custom_call_target="tpu_custom_call" | custom-call | flops 7247757312 | bytes 16777216 | tf_op jit(solution)/shard_map/sum_gradients/weigh/pallas_call | solution.py:471
  265.4 0.9 add.181
  267.0 0.7 collective-permute-start.10
  268.4 0.7 collective-permute-start.9
  269.4 2.3 collective-permute-done.13
  271.7 24.5 %collective-permute-done.11 = bf16[512,768]{1,0:T(8,128)(2,1)S(1)} collective-permute-done((bf16[512,768]{1,0:T(8,128)(2,1)S(1)}, bf16[512,768]{1,0:T(8,128)(2,1)S(1)}, u32[]{:S(2)}, u32[]{:S(2)}) %collective-permute-start.11) | collective-permute-done | bytes 786464 | tf_op jit(solution)/shard_map/sum_gradients/ppermute | solution.py:848
  296.8 1.4 copy-done.2
  299.5 0.7 collective-permute-start.14
  300.2 0.7 collective-permute-start.15
  300.9 1.3 collective-permute-start.16
  302.2 1.6 collective-permute-start.18
  303.7 20.1 %collective-permute-done.18 = f32[20,768]{1,0:T(8,128)S(1)} collective-permute-done((f32[20,768]{1,0:T(8,128)S(1)}, f32[20,768]{1,0:T(8,128)S(1)}, u32[]{:S(2)}, u32[]{:S(2)}) %collective-permute-start.18) | collective-permute-done | bytes 61472 | tf_op jit(solution)/shard_map/sum_gradients/ppermute | solution.py:848
  323.9 30.7 %collective-permute-done.16 = bf16[512,768]{1,0:T(8,128)(2,1)S(1)} collective-permute-done((bf16[512,768]{1,0:T(8,128)(2,1)S(1)}, bf16[512,768]{1,0:T(8,128)(2,1)S(1)}, u32[]{:S(2)}, u32[]{:S(2)}) %collective-permute-start.16) | collective-permute-done | bytes 786464 | tf_op jit(solution)/shard_map/sum_gradients/ppermute | solution.py:902
  356.1 1.5 collective-permute-start.19
  357.7 2.0 collective-permute-start.21
  359.7 21.9 %collective-permute-done.22 = f32[20,768]{1,0:T(8,128)} collective-permute-done((f32[20,768]{1,0:T(8,128)}, f32[20,768]{1,0:T(8,128)}, u32[]{:S(2)}, u32[]{:S(2)}) %collective-permute-start.22) | collective-permute-done | bytes 61472 | tf_op jit(solution)/shard_map/sum_gradients/ppermute | solution.py:848
  381.6 7.1 %collective-permute-done.19 = bf16[512,768]{1,0:T(8,128)(2,1)S(1)} collective-permute-done((bf16[512,768]{1,0:T(8,128)(2,1)S(1)}, bf16[512,768]{1,0:T(8,128)(2,1)S(1)}, u32[]{:S(2)}, u32[]{:S(2)}) %collective-permute-start.19) | collective-permute-done | bytes 786464 | tf_op jit(solution)/shard_map/sum_gradients/ppermute | solution.py:902
  388.7 0.9 add.201
  389.7 1.2 fusion.11
  390.8 5.1 %collective-permute-start.26 = (f32[20,768]{1,0:T(8,128)S(1)}, f32[20,768]{1,0:T(8,128)S(1)}, u32[]{:S(2)}, u32[]{:S(2)}) collective-permute-start(f32[20,768]{1,0:T(8,128)S(1)} %add.201), channel_id=1, source_target_pairs={{0,4},{1,5},{2,6},{3,7},{4,0},{5,1},{6,2},{7,3},{8,12},{9,13},{10,... | collective-permute-start | bytes 184328 | tf_op jit(solution)/shard_map/sum_gradients/ppermute | solution.py:848
  396.6 4.4 %collective-permute-start.25 = (bf16[192,384]{1,0:T(8,128)(2,1)S(1)}, bf16[192,384]{1,0:T(8,128)(2,1)}, u32[]{:S(2)}, u32[]{:S(2)}) collective-permute-start(bf16[192,384]{1,0:T(8,128)(2,1)S(1)} %get-tuple-element.129), channel_id=1, source_target_pairs={{0,6},{1,7},{2,4},{3,5},{4,2},{5,3},{6,0},{7,1},{8,14},{9,15},{10,... | collective-permute-start | bytes 442376 | tf_op jit(solution)/shard_map/sum_gradients/ppermute | solution.py:848
  401.0 1.1 add_convert_fusion.2.trunk_ref
  402.1 5.6 %finish.1 = bf16[512,768]{1,0:T(8,128)(2,1)} custom-call(s32[3]{0:T(128)} %pad_add_fusion.meta, bf16[512,768]{1,0:T(8,128)(2,1)} %add_convert_fusion.2.trunk_ref, bf16[512,768]{1,0:T(8,128)(2,1)} %copy-done.1, bf16[512,768]{1,0:T(8,128)(2,1)} %collective-permute-done.20.far_ref, f32[512,768]{1,0:T(8,128)} %get-tuple-element.123.own_ref, ...), custom_call_target="tpu_custom_call" | custom-call | bytes 16777216 | tf_op jit(solution)/shard_map/finish/pallas_call | solution.py:471
  410.3 1.1 fusion.8
  411.5 0.7 slice.205
  412.2 1.0 convert_element_type.309
  413.3 0.7 slice_bitcast_fusion
  414.0 0.7 maximum_bitcast_fusion
  (102 shorter events, 13.9 us)
Async XLA Ops:
  7.2 5.4 %copy-start.9 = (s32[1,16]{1,0:T(1,128)S(1)}, s32[1,16]{1,0:T(1,128)}, u32[]{:S(2)}) copy-start(s32[1,16]{1,0:T(1,128)} %param.12) | copy-start | bytes 196
  7.2 11.2 %copy-start = (bf16[512,768]{1,0:T(8,128)(2,1)S(1)}, bf16[512,768]{1,0:T(8,128)(2,1)}, u32[]{:S(2)}) copy-start(bf16[512,768]{1,0:T(8,128)(2,1)} %tokens_ref.5) | copy-start | bytes 2359300
  7.2 106.1 %all-gather.5.cloned.1.call-start = ((), (), s32[]{:S(2)}) async-start(), calls=%async_computation.2 | async-start | bytes 10137600 | tf_op jit(solution)/shard_map/gather_early_weights/all_gather | solution.py:1043
  10.8 172.1 %all-gather.7.cloned.1.call-start = ((), (), s32[]{:S(2)}) async-start(), calls=%async_computation.3 | async-start | bytes 4866048 | tf_op jit(solution)/shard_map/gather_late_weights/all_gather | solution.py:1062
  12.5 399.7 %reduce-scatter.2.cloned.1.call-start = ((), (), s32[]{:S(2)}) async-start(), calls=%async_computation.1 | async-start | bytes 9732096 | tf_op jit(solution)/shard_map/scatter_late_weights/reduce_scatter | solution.py:1072
  19.5 22.9 %collective-permute-start.1 = (bf16[512,768]{1,0:T(8,128)(2,1)}, bf16[512,768]{1,0:T(8,128)(2,1)S(1)}, u32[]{:S(2)}, u32[]{:S(2)}) collective-permute-start(bf16[512,768]{1,0:T(8,128)(2,1)} %pad_maximum_fusion), channel_id=1, source_target_pairs={{0,1},{1,0},{2,3},{3,2},{4,5},{5,4},{6,7},{7,6},{8,9},{9,8},{10,11... | collective-permute-start | bytes 2359304 | tf_op jit(solution)/shard_map/gather_tokens/ppermute | solution.py:848
  22.4 29.9 %collective-permute-start = (bf16[512,768]{1,0:T(8,128)(2,1)S(1)}, bf16[512,768]{1,0:T(8,128)(2,1)S(1)}, u32[]{:S(2)}, u32[]{:S(2)}) collective-permute-start(bf16[512,768]{1,0:T(8,128)(2,1)S(1)} %copy-done), channel_id=1, source_target_pairs={{0,4},{1,5},{8,12},{9,13},{16,20},{17,21},{24,28},{25,29}} | collective-permute-start | bytes 2359304 | tf_op jit(solution)/shard_map/gather_tokens/ppermute | solution.py:902
  42.4 9.9 %copy-start.4 = (bf16[512,768]{1,0:T(8,128)(2,1)}, bf16[512,768]{1,0:T(8,128)(2,1)S(1)}, u32[]{:S(2)}) copy-start(bf16[512,768]{1,0:T(8,128)(2,1)S(1)} %collective-permute-done.1) | copy-start | bytes 2359300
  54.7 28.9 %collective-permute-start.2 = (bf16[512,768]{1,0:T(8,128)(2,1)}, bf16[512,768]{1,0:T(8,128)(2,1)}, u32[]{:S(2)}, u32[]{:S(2)}) collective-permute-start(bf16[512,768]{1,0:T(8,128)(2,1)} %get-tuple-element.132), channel_id=1, source_target_pairs={{0,2},{1,3},{2,4},{3,5},{4,6},{5,7},{8,10},{9,11},{10,12},{11,13},... | collective-permute-start | bytes 2359304 | tf_op jit(solution)/shard_map/gather_tokens/ppermute | solution.py:902
  56.9 26.8 %collective-permute-start.4 = (bf16[512,768]{1,0:T(8,128)(2,1)S(1)}, bf16[512,768]{1,0:T(8,128)(2,1)S(1)}, u32[]{:S(2)}, u32[]{:S(2)}) collective-permute-start(bf16[512,768]{1,0:T(8,128)(2,1)S(1)} %get-tuple-element.133), channel_id=1, source_target_pairs={{6,4},{7,5},{14,12},{15,13},{22,20},{23,21},{30,28},{31,29}} | collective-permute-start | bytes 2359304 | tf_op jit(solution)/shard_map/gather_tokens/ppermute | solution.py:902
  85.9 1.4 collective-permute-start.5
  86.6 0.7 collective-permute-start.6
  87.5 23.8 %collective-permute-start.7 = (bf16[512,768]{1,0:T(8,128)(2,1)S(1)}, bf16[512,768]{1,0:T(8,128)(2,1)S(1)}, u32[]{:S(2)}, u32[]{:S(2)}) collective-permute-start(bf16[512,768]{1,0:T(8,128)(2,1)S(1)} %add_add_fusion), channel_id=1, source_target_pairs={{0,1},{1,0},{2,3},{3,2},{4,5},{5,4},{6,7},{7,6},{8,9},{9,8},{10,11... | collective-permute-start | bytes 2359304 | tf_op jit(solution)/shard_map/gather_tokens/ppermute | solution.py:848
  87.6 39.1 %collective-permute-start.3 = (bf16[512,768]{1,0:T(8,128)(2,1)}, bf16[512,768]{1,0:T(8,128)(2,1)S(1)}, u32[]{:S(2)}, u32[]{:S(2)}) collective-permute-start(bf16[512,768]{1,0:T(8,128)(2,1)} %get-tuple-element.153.a_ref), channel_id=1, source_target_pairs={{0,1},{1,0},{2,3},{3,2},{4,5},{5,4},{6,7},{7,6},{8,9},{9,8},{10,11... | collective-permute-start | bytes 2359304 | tf_op jit(solution)/shard_map/gather_tokens/ppermute | solution.py:848
  126.7 0.9 copy-start.11
  241.3 2.1 copy-start.3
  243.3 0.7 copy-start.8
  244.7 21.5 %collective-permute-start.8 = (bf16[512,768]{1,0:T(8,128)(2,1)S(1)}, bf16[512,768]{1,0:T(8,128)(2,1)S(1)}, u32[]{:S(2)}, u32[]{:S(2)}) collective-permute-start(bf16[512,768]{1,0:T(8,128)(2,1)S(1)} %get-tuple-element.83), channel_id=1, source_target_pairs={{0,1},{1,0},{2,3},{3,2},{4,5},{5,4},{6,7},{7,6},{8,9},{9,8},{10,11... | collective-permute-start | bytes 2359304 | tf_op jit(solution)/shard_map/sum_gradients/ppermute | solution.py:848
  246.2 19.1 %copy-start.6 = (f32[8,768]{1,0:T(8,128)S(1)}, f32[8,768]{1,0:T(8,128)}, u32[]{:S(2)}) copy-start(f32[8,768]{1,0:T(8,128)} %get-tuple-element.93) | copy-start | bytes 73732
  246.2 20.0 %copy-start.7 = (f32[8,768]{1,0:T(8,128)S(1)}, f32[8,768]{1,0:T(8,128)}, u32[]{:S(2)}) copy-start(f32[8,768]{1,0:T(8,128)} %get-tuple-element.95) | copy-start | bytes 73732
  265.4 1.7 copy-start.10
  267.0 29.2 %collective-permute-start.12 = (bf16[16,192,384]{2,1,0:T(8,128)(2,1)S(1)}, bf16[16,192,384]{2,1,0:T(8,128)(2,1)S(1)}, u32[]{:S(2)}, u32[]{:S(2)}) collective-permute-start(bf16[16,192,384]{2,1,0:T(8,128)(2,1)S(1)} %copy-done.10), channel_id=1, source_target_pairs={{0,8},{8,0},{16,24},{24,16},{1,9},{9,1},{17,25},{25,17},{2,10},{10... | collective-permute-start | bytes 7077896 | tf_op jit(solution)/shard_map/sum_gradients/ppermute | solution.py:848
  267.0 4.6 %collective-permute-start.10 = (bf16[512,768]{1,0:T(8,128)(2,1)S(1)}, bf16[512,768]{1,0:T(8,128)(2,1)S(1)}, u32[]{:S(2)}, u32[]{:S(2)}) collective-permute-start(bf16[512,768]{1,0:T(8,128)(2,1)S(1)} %add_convert_fusion.5), channel_id=1, source_target_pairs={{6,4},{7,5},{14,12},{15,13},{22,20},{23,21},{30,28},{31,29}} | collective-permute-start | bytes 2359304 | tf_op jit(solution)/shard_map/sum_gradients/ppermute | solution.py:902
  267.8 28.4 %collective-permute-start.11 = (bf16[512,768]{1,0:T(8,128)(2,1)S(1)}, bf16[512,768]{1,0:T(8,128)(2,1)S(1)}, u32[]{:S(2)}, u32[]{:S(2)}) collective-permute-start(bf16[512,768]{1,0:T(8,128)(2,1)S(1)} %get-tuple-element.98), channel_id=1, source_target_pairs={{0,1},{1,0},{2,3},{3,2},{4,5},{5,4},{6,7},{7,6},{8,9},{9,8},{10,11... | collective-permute-start | bytes 2359304 | tf_op jit(solution)/shard_map/sum_gradients/ppermute | solution.py:848
  268.4 27.8 %collective-permute-start.9 = (bf16[512,768]{1,0:T(8,128)(2,1)S(1)}, bf16[512,768]{1,0:T(8,128)(2,1)S(1)}, u32[]{:S(2)}, u32[]{:S(2)}) collective-permute-start(bf16[512,768]{1,0:T(8,128)(2,1)S(1)} %add_convert_fusion.5), channel_id=1, source_target_pairs={{2,4},{3,5},{10,12},{11,13},{18,20},{19,21},{26,28},{27,29}} | collective-permute-start | bytes 2359304 | tf_op jit(solution)/shard_map/sum_gradients/ppermute | solution.py:902
  269.1 2.6 collective-permute-start.13
  296.4 1.8 copy-start.2
  298.9 55.7 %collective-permute-start.17 = (bf16[8,192,384]{2,1,0:T(8,128)(2,1)S(1)}, bf16[8,192,384]{2,1,0:T(8,128)(2,1)S(1)}, u32[]{:S(2)}, u32[]{:S(2)}) collective-permute-start(bf16[8,192,384]{2,1,0:T(8,128)(2,1)S(1)} %get-tuple-element.110), channel_id=1, source_target_pairs={{0,16},{1,17},{2,18},{3,19},{4,20},{5,21},{6,22},{7,23},{8,9},{9,8... | collective-permute-start | bytes 3538952 | tf_op jit(solution)/shard_map/sum_gradients/ppermute | solution.py:859
  299.5 24.4 %collective-permute-start.14 = (bf16[512,768]{1,0:T(8,128)(2,1)S(1)}, bf16[512,768]{1,0:T(8,128)(2,1)S(1)}, u32[]{:S(2)}, u32[]{:S(2)}) collective-permute-start(bf16[512,768]{1,0:T(8,128)(2,1)S(1)} %get-tuple-element.107), channel_id=1, source_target_pairs={{4,6},{5,7},{12,14},{13,15},{20,22},{21,23},{28,30},{29,31}} | collective-permute-start | bytes 2359304 | tf_op jit(solution)/shard_map/sum_gradients/ppermute | solution.py:902
  300.2 23.7 %collective-permute-start.15 = (bf16[512,768]{1,0:T(8,128)(2,1)S(1)}, bf16[512,768]{1,0:T(8,128)(2,1)S(1)}, u32[]{:S(2)}, u32[]{:S(2)}) collective-permute-start(bf16[512,768]{1,0:T(8,128)(2,1)S(1)} %get-tuple-element.108), channel_id=1, source_target_pairs={{4,2},{5,3},{12,10},{13,11},{20,18},{21,19},{28,26},{29,27}} | collective-permute-start | bytes 2359304 | tf_op jit(solution)/shard_map/sum_gradients/ppermute | solution.py:902
  300.9 53.6 %collective-permute-start.16 = (bf16[512,768]{1,0:T(8,128)(2,1)S(1)}, bf16[512,768]{1,0:T(8,128)(2,1)S(1)}, u32[]{:S(2)}, u32[]{:S(2)}) collective-permute-start(bf16[512,768]{1,0:T(8,128)(2,1)S(1)} %add_convert_fusion.4), channel_id=1, source_target_pairs={{2,0},{3,1},{6,4},{7,5},{10,8},{11,9},{14,12},{15,13},{18,16},{19,... | collective-permute-start | bytes 2359304 | tf_op jit(solution)/shard_map/sum_gradients/ppermute | solution.py:902
  302.2 21.7 %collective-permute-start.18 = (f32[20,768]{1,0:T(8,128)S(1)}, f32[20,768]{1,0:T(8,128)S(1)}, u32[]{:S(2)}, u32[]{:S(2)}) collective-permute-start(f32[20,768]{1,0:T(8,128)S(1)} %add.186), channel_id=1, source_target_pairs={{0,16},{8,24},{16,0},{24,8},{1,17},{9,25},{17,1},{25,9},{2,18},{10... | collective-permute-start | bytes 184328 | tf_op jit(solution)/shard_map/sum_gradients/ppermute | solution.py:848
  356.1 46.1 %copy-start.1 = (bf16[512,768]{1,0:T(8,128)(2,1)}, bf16[512,768]{1,0:T(8,128)(2,1)S(1)}, u32[]{:S(2)}) copy-start(bf16[512,768]{1,0:T(8,128)(2,1)S(1)} %fusion.4.near_ref) | copy-start | bytes 2359300
  356.1 32.7 %collective-permute-start.19 = (bf16[512,768]{1,0:T(8,128)(2,1)S(1)}, bf16[512,768]{1,0:T(8,128)(2,1)S(1)}, u32[]{:S(2)}, u32[]{:S(2)}) collective-permute-start(bf16[512,768]{1,0:T(8,128)(2,1)S(1)} %add_convert_fusion.3), channel_id=1, source_target_pairs={{4,0},{5,1},{12,8},{13,9},{20,16},{21,17},{28,24},{29,25}} | collective-permute-start | bytes 2359304 | tf_op jit(solution)/shard_map/sum_gradients/ppermute | solution.py:902
  357.6 31.2 %collective-permute-start.20 = (bf16[512,768]{1,0:T(8,128)(2,1)S(1)}, bf16[512,768]{1,0:T(8,128)(2,1)}, u32[]{:S(2)}, u32[]{:S(2)}) collective-permute-start(bf16[512,768]{1,0:T(8,128)(2,1)S(1)} %fusion.4.near_ref), channel_id=1, source_target_pairs={{0,1},{1,0},{2,3},{3,2},{4,5},{5,4},{6,7},{7,6},{8,9},{9,8},{10,11... | collective-permute-start | bytes 2359304 | tf_op jit(solution)/shard_map/sum_gradients/ppermute | solution.py:848
  357.7 24.0 %collective-permute-start.21 = (bf16[4,192,384]{2,1,0:T(8,128)(2,1)S(1)}, bf16[4,192,384]{2,1,0:T(8,128)(2,1)}, u32[]{:S(2)}, u32[]{:S(2)}) collective-permute-start(bf16[4,192,384]{2,1,0:T(8,128)(2,1)S(1)} %get-tuple-element.119), channel_id=1, source_target_pairs={{0,1},{1,0},{2,3},{3,2},{4,5},{5,4},{6,7},{7,6},{8,24},{9,25},{10,... | collective-permute-start | bytes 1769480 | tf_op jit(solution)/shard_map/sum_gradients/ppermute | solution.py:859
  359.7 22.0 %collective-permute-start.22 = (f32[20,768]{1,0:T(8,128)}, f32[20,768]{1,0:T(8,128)}, u32[]{:S(2)}, u32[]{:S(2)}) collective-permute-start(f32[20,768]{1,0:T(8,128)} %add.193), channel_id=1, source_target_pairs={{0,1},{1,0},{2,3},{3,2},{4,5},{5,4},{6,7},{7,6},{8,9},{9,8},{10,11... | collective-permute-start | bytes 184328 | tf_op jit(solution)/shard_map/sum_gradients/ppermute | solution.py:848
  390.8 10.1 %collective-permute-start.26 = (f32[20,768]{1,0:T(8,128)S(1)}, f32[20,768]{1,0:T(8,128)S(1)}, u32[]{:S(2)}, u32[]{:S(2)}) collective-permute-start(f32[20,768]{1,0:T(8,128)S(1)} %add.201), channel_id=1, source_target_pairs={{0,4},{1,5},{2,6},{3,7},{4,0},{5,1},{6,2},{7,3},{8,12},{9,13},{10,... | collective-permute-start | bytes 184328 | tf_op jit(solution)/shard_map/sum_gradients/ppermute | solution.py:848
  396.6 13.8 %collective-permute-start.23 = (bf16[192,384]{1,0:T(8,128)(2,1)S(1)}, bf16[192,384]{1,0:T(8,128)(2,1)S(1)}, u32[]{:S(2)}, u32[]{:S(2)}) collective-permute-start(bf16[192,384]{1,0:T(8,128)(2,1)S(1)} %get-tuple-element.127), channel_id=1, source_target_pairs={{0,2},{1,3},{2,0},{3,1},{4,6},{5,7},{6,4},{7,5},{8,10},{9,11},{10,... | collective-permute-start | bytes 442376 | tf_op jit(solution)/shard_map/sum_gradients/ppermute | solution.py:848
  396.6 13.8 %collective-permute-start.24 = (bf16[192,384]{1,0:T(8,128)(2,1)S(1)}, bf16[192,384]{1,0:T(8,128)(2,1)}, u32[]{:S(2)}, u32[]{:S(2)}) collective-permute-start(bf16[192,384]{1,0:T(8,128)(2,1)S(1)} %get-tuple-element.128), channel_id=1, source_target_pairs={{0,4},{1,5},{2,6},{3,7},{4,0},{5,1},{6,2},{7,3},{8,12},{9,13},{10,... | collective-permute-start | bytes 442376 | tf_op jit(solution)/shard_map/sum_gradients/ppermute | solution.py:848
  396.6 13.8 %collective-permute-start.25 = (bf16[192,384]{1,0:T(8,128)(2,1)S(1)}, bf16[192,384]{1,0:T(8,128)(2,1)}, u32[]{:S(2)}, u32[]{:S(2)}) collective-permute-start(bf16[192,384]{1,0:T(8,128)(2,1)S(1)} %get-tuple-element.129), channel_id=1, source_target_pairs={{0,6},{1,7},{2,4},{3,5},{4,2},{5,3},{6,0},{7,1},{8,14},{9,15},{10,... | collective-permute-start | bytes 442376 | tf_op jit(solution)/shard_map/sum_gradients/ppermute | solution.py:848
  401.0 6.8 %collective-permute-start.27 = (f32[20,768]{1,0:T(8,128)S(1)}, f32[20,768]{1,0:T(8,128)S(1)}, u32[]{:S(2)}, u32[]{:S(2)}) collective-permute-start(f32[20,768]{1,0:T(8,128)S(1)} %add.205), channel_id=1, source_target_pairs={{0,2},{1,3},{2,0},{3,1},{4,6},{5,7},{6,4},{7,5},{8,10},{9,11},{10,... | collective-permute-start | bytes 184328 | tf_op jit(solution)/shard_map/sum_gradients/ppermute | solution.py:848
  411.5 3.3 copy-start.5
Sparse Core Ops, SparseCore 0:
  11.6 100.9 all-gather.4
  116.1 66.7 all-gather.6
  208.6 172.2 reduce-scatter.1

commit v3 on v2

--- a/solution.py
+++ b/solution.py
@@ -319,132 +319,169 @@
 NEG=NEGATIVE
 NT=(((1,),(1,)),((),()))
 NN=(((1,),(0,)),((),()))
-def dg(a,b,dims): return lax.dot_general(a,b,dims,preferred_element_type=F32)
-
-def chunks_of(trunk):
-    return [0,1,2,3] if trunk else [0,1,2,3,4,5]
-
-def score_chunk(c, trunk, k_ref, qh, meta):
-    if c<4:
-        st=dg(k_ref[c*SEG:(c+1)*SEG,:], qh, NT)
-        if trunk:
-            kp=(c^meta[4])*SEG+lax.broadcasted_iota(jnp.int32,(SEG,2*SEG),0)
-            qp=meta[1]+lax.broadcasted_iota(jnp.int32,(SEG,2*SEG),1)
-            st=jnp.where(kp<=qp,st,NEG)
-        return st
-    base=4*SEG+(c-4)*2*SEG
-    parts=[]
-    for i in range(2):
-        s=dg(k_ref[base+i*SEG:base+(i+1)*SEG,:], qh[i*SEG:(i+1)*SEG,:], NT)
-        if c==4:
-            s=s+jnp.where(meta[2+i]>0,0.0,NEG).astype(F32)
+
+
+def dg(a, b, dims):
+    return lax.dot_general(a, b, dims, preferred_element_type=F32)
+
+
+def chunk_rows(c, i):
+    start = c * SEG if c < 4 else (4 + (c - 4) * 2 + i) * SEG
+    return slice(start, start + SEG)
+
+
+def pair_dot(c, keys_ref, rows):
+    if c < 4:
+        return dg(keys_ref[chunk_rows(c, 0), :], rows, NT)
+    return jnp.concatenate(
+        [
+            dg(keys_ref[chunk_rows(c, i), :], rows[i * SEG : (i + 1) * SEG, :], NT)
+            for i in range(2)
+        ],
+        axis=1,
+    )
+
+
+def score_chunk(c, k_ref, qh):
+    scores = pair_dot(c, k_ref, qh)
+    if c < 5:
+        return scores
+    key = lax.broadcasted_iota(jnp.int32, scores.shape, 0)
+    query = lax.broadcasted_iota(jnp.int32, scores.shape, 1)
+    return jnp.where(key <= (query & (SEG - 1)), scores, NEG)
+
+
+def chunk_bias(c, meta):
+    second = lax.broadcasted_iota(jnp.int32, (1, 2 * SEG), 1) // SEG
+    if c < 4:
+        return jnp.where((c ^ meta[1]) < meta[0] + second, 0.0, NEG)
+    if c == 4:
+        return jnp.where(jnp.where(second > 0, meta[3], meta[2]) > 0, 0.0, NEG)
+    return jnp.zeros((1, 2 * SEG), F32)
+
+
+def halves_of(value):
+    lane = lax.broadcasted_iota(jnp.int32, value.shape, 1)
+    zero = jnp.zeros((), value.dtype)
+    return [jnp.where((lane < 64) == (h == 0), value, zero) for h in range(2)]
+
+
+def fwd_kernel(meta, q_ref, k_ref, v_ref, o_ref, inverse_ref, p_ref):
+    turned = v_ref[...].T
+    biases = [chunk_bias(c, meta) for c in range(6)]
+    results, inverses = [], []
+    for h, qh in enumerate(halves_of(q_ref[...] * jnp.asarray(0.125, BF))):
+        scores = [score_chunk(c, k_ref, qh) for c in range(6)]
+        top = jnp.full((1, 2 * SEG), NEG, F32)
+        for s, bias in zip(scores, biases):
+            top = jnp.maximum(top, jnp.max(s, axis=0, keepdims=True) + bias)
+        mass = jnp.zeros((1, 2 * SEG), F32)
+        shared = jnp.zeros((128, 2 * SEG), F32)
+        own = [jnp.zeros((128, SEG), F32)] * 2
+        for c, s in enumerate(scores):
+            p = jnp.exp(s - (top - biases[c]))
+            mass = mass + jnp.sum(p, axis=0, keepdims=True)
+            low = p.astype(BF)
+            p_ref[0, (6 * h + c) * SEG : (6 * h + c + 1) * SEG, :] = low
+            if c < 4:
+                shared = shared + dg(turned[:, chunk_rows(c, 0)], low, NN)
+            else:
+                own = [
+                    own[i] + dg(turned[:, chunk_rows(c, i)], low[:, i * SEG : (i + 1) * SEG], NN)
+                    for i in range(2)
+                ]
+        inverse = jnp.broadcast_to(1.0 / mass, shared.shape)
+        inverses.append(inverse)
+        results.append((shared + jnp.concatenate(own, axis=1)) * inverse)
+    row = lax.broadcasted_iota(jnp.int32, results[0].shape, 0)
+    o_ref[...] = jnp.where(row < 64, results[0], results[1]).T.astype(BF)
+    inverse_ref[...] = jnp.where(row < 64, inverses[0], inverses[1]).T
+
+
+def bwd_kernel(q_ref, k_ref, v_ref, do_ref, o_ref, inverse_ref, p_ref, dq_ref, dk_ref, dv_ref):
+    do = (do_ref[...].astype(F32) * inverse_ref[...]).astype(BF)
+    products = (do.astype(F32) * o_ref[...].astype(F32)).T
+    turned = k_ref[...].T
+    qh = halves_of(q_ref[...] * jnp.asarray(0.125, BF))
+    doh = halves_of(do)
+    delta = [jnp.sum(products[h * 64 : (h + 1) * 64], axis=0, keepdims=True) for h in range(2)]
+    shared = [jnp.zeros((128, 2 * SEG), F32)] * 2
+    own = [[jnp.zeros((128, SEG), F32)] * 2] * 2
+    for c in range(6):
+        chances, slopes = [], []
+        for h in range(2):
+            p = p_ref[0, (6 * h + c) * SEG : (6 * h + c + 1) * SEG, :]
+            ds = p.astype(F32) * (pair_dot(c, v_ref, doh[h]) - delta[h])
+            chances.append(p)
+            slopes.append(ds.astype(BF))
+        for i in range(1 if c < 4 else 2):
+            r = chunk_rows(c, i)
+            cut = slice(0, 2 * SEG) if c < 4 else slice(i * SEG, (i + 1) * SEG)
+            for ref, left, right in ((dv_ref, chances, doh), (dk_ref, slopes, qh)):
+                ref[r, :] = dg(
+                    jnp.concatenate([x[:, cut] for x in left], axis=1),
+                    jnp.concatenate([x[cut] for x in right], axis=0),
+                    NN,
+                ).astype(BF)
+        if c < 4:
+            shared = [shared[h] + dg(turned[:, chunk_rows(c, 0)], slopes[h], NN) for h in range(2)]
         else:
-            kp=lax.broadcasted_iota(jnp.int32,(SEG,SEG),0)
-            qp=lax.broadcasted_iota(jnp.int32,(SEG,SEG),1)
-            s=jnp.where(kp<=qp,s,NEG)
-        parts.append(s)
-    return jnp.concatenate(parts,axis=1)
-
-def fwd_kernel(meta, q_ref,k_ref,v_ref,o_ref,lse_ref):
-    def run(trunk):
-        q=q_ref[...]*jnp.asarray(0.125,BF)
-        lane=lax.broadcasted_iota(jnp.int32,q.shape,1)
-        vt=v_ref[...].T
-        res=[]
-        for h in range(2):
-            qh=jnp.where((lane<64)==(h==0),q,jnp.asarray(0,BF))
-            cs=chunks_of(trunk)
-            st=[score_chunk(c,trunk,k_ref,qh,meta) for c in cs]
-            m=st[0]
-            for s in st[1:]: m=jnp.maximum(m,s)
-            m=jnp.max(m,axis=0,keepdims=True)
-            l=jnp.zeros((1,2*SEG),F32);
-            ot=jnp.zeros((128,2*SEG),F32); own=[jnp.zeros((128,SEG),F32)]*2
-            for c,s in zip(cs,st):
-                p=jnp.exp(s-m)
-                l=l+jnp.sum(p,axis=0,keepdims=True)
-                pb=p.astype(BF)
-                if c<4:
-                    ot=ot+dg(vt[:,c*SEG:(c+1)*SEG],pb,NN)
-                else:
-                    base=4*SEG+(c-4)*2*SEG
-                    own=[own[i]+dg(vt[:,base+i*SEG:base+(i+1)*SEG],pb[:,i*SEG:(i+1)*SEG],NN) for i in range(2)]
-            ot=(ot+jnp.concatenate(own,axis=1))*(1.0/l)
-            res.append(ot)
-            lse_ref[0,h:h+1,:]=m+jnp.log(l)
-        row=lax.broadcasted_iota(jnp.int32,res[0].shape,0)
-        o_ref[...]=jnp.where(row<64,res[0],res[1]).T.astype(BF)
-    @pl.when(meta[0]>0)
-    def _(): run(True)
-    @pl.when(meta[0]==0)
-    def _(): run(False)
-
-def bwd_kernel(meta, q_ref,k_ref,v_ref,do_ref,o_ref,lse_ref,dq_ref,dk_ref,dv_ref):
-    def run(trunk):
-        q=q_ref[...]*jnp.asarray(0.125,BF)
-        do=do_ref[...]
-        lane=lax.broadcasted_iota(jnp.int32,q.shape,1)
-        zero=jnp.asarray(0,BF)
-        dd=(do.astype(F32)*o_ref[...].astype(F32)).T
-        kt=k_ref[...].T
-        qh=[jnp.where((lane<64)==(h==0),q,zero) for h in range(2)]
-        doh=[jnp.where((lane<64)==(h==0),do,zero) for h in range(2)]
-        delta=[jnp.sum(dd[h*64:(h+1)*64],axis=0,keepdims=True) for h in range(2)]
-        qcat=jnp.concatenate(qh,axis=0); docat=jnp.concatenate(doh,axis=0)
-        dqt=[jnp.zeros((128,2*SEG),F32)]*2
-        own=[[jnp.zeros((128,SEG),F32)]*2]*2
-        for c in chunks_of(trunk):
-            pbs=[];dsbs=[]
-            for h in range(2):
-                st=score_chunk(c,trunk,k_ref,qh[h],meta)
-                p=jnp.exp(st-lse_ref[0,h:h+1,:])
-                if c<4:
-                    dp=dg(v_ref[c*SEG:(c+1)*SEG,:],doh[h],NT)
-                else:
-                    base=4*SEG+(c-4)*2*SEG
-                    dp=jnp.concatenate([dg(v_ref[base+i*SEG:base+(i+1)*SEG,:],doh[h][i*SEG:(i+1)*SEG,:],NT) for i in range(2)],axis=1)
-                ds=p*(dp-delta[h])
-                pbs.append(p.astype(BF)); dsbs.append(ds.astype(BF))
-            if c<4:
-                r=slice(c*SEG,(c+1)*SEG)
-                dv_ref[r,:]=dg(jnp.concatenate(pbs,axis=1),docat,NN).astype(BF)
-                dk_ref[r,:]=dg(jnp.concatenate(dsbs,axis=1),qcat,NN).astype(BF)
-                for h in range(2): dqt[h]=dqt[h]+dg(kt[:,r],dsbs[h],NN)
-            else:
-                base=4*SEG+(c-4)*2*SEG
-                for i in range(2):
-                    r=slice(base+i*SEG,base+(i+1)*SEG); cc=slice(i*SEG,(i+1)*SEG)
-                    dv_ref[r,:]=dg(jnp.concatenate([x[:,cc] for x in pbs],axis=1),jnp.concatenate([x[cc] for x in doh],axis=0),NN).astype(BF)
-                    dk_ref[r,:]=dg(jnp.concatenate([x[:,cc] for x in dsbs],axis=1),jnp.concatenate([x[cc] for x in qh],axis=0),NN).astype(BF)
-                own=[[own[h][i]+dg(kt[:,base+i*SEG:base+(i+1)*SEG],dsbs[h][:,i*SEG:(i+1)*SEG],NN) for i in range(2)] for h in range(2)]
-        if trunk:
-            dv_ref[4*SEG:,:]=jnp.zeros((4*SEG,128),BF)
-            dk_ref[4*SEG:,:]=jnp.zeros((4*SEG,128),BF)
-        dqt=[dqt[h]+jnp.concatenate(own[h],axis=1) for h in range(2)]
-        row=lax.broadcasted_iota(jnp.int32,dqt[0].shape,0)
-        dq_ref[...]=(jnp.where(row<64,dqt[0],dqt[1]).T*0.125).astype(BF)
-    @pl.when(meta[0]>0)
-    def _(): run(True)
-    @pl.when(meta[0]==0)
-    def _(): run(False)
-
-def attn_fwd(meta,q,k,v,interpret=False):
-    n=q.shape[1]//128; nk=k.shape[0]; nq=q.shape[0]
-    gs=pltpu.PrefetchScalarGridSpec(num_scalar_prefetch=1,grid=(n,),
-        in_specs=[pl.BlockSpec((nq,128),lambda j,m:(0,j)),pl.BlockSpec((nk,128),lambda j,m:(0,j)),pl.BlockSpec((nk,128),lambda j,m:(0,j))],
-        out_specs=[pl.BlockSpec((nq,128),lambda j,m:(0,j)),pl.BlockSpec((1,2,nq),lambda j,m:(j,0,0))])
-    return pl.pallas_call(fwd_kernel,grid_spec=gs,out_shape=[jax.ShapeDtypeStruct(q.shape,BF),jax.ShapeDtypeStruct((n,2,nq),F32)],
-        cost_estimate=pl.CostEstimate(flops=2*2*12*256*256*256*12,bytes_accessed=8<<20,transcendentals=10<<20),
-        compiler_params=pltpu.CompilerParams(vmem_limit_bytes=60<<20),interpret=interpret,name="attn_fwd")(meta,q,k,v)
-def attn_bwd(meta,q,k,v,do,o,lse,interpret=False):
-    n=q.shape[1]//128; nk=k.shape[0]; nq=q.shape[0]
-    qs=pl.BlockSpec((nq,128),lambda j,m:(0,j)); ks=pl.BlockSpec((nk,128),lambda j,m:(0,j))
-    gs=pltpu.PrefetchScalarGridSpec(num_scalar_prefetch=1,grid=(n,),
-        in_specs=[qs,ks,ks,qs,qs,pl.BlockSpec((1,2,nq),lambda j,m:(j,0,0))],
-        out_specs=[qs,ks,ks])
-    return pl.pallas_call(bwd_kernel,grid_spec=gs,out_shape=[jax.ShapeDtypeStruct(q.shape,BF),jax.ShapeDtypeStruct(k.shape,BF),jax.ShapeDtypeStruct(k.shape,BF)],
-        cost_estimate=pl.CostEstimate(flops=5*2*12*256*256*256*12,bytes_accessed=16<<20,transcendentals=10<<20),
-        compiler_params=pltpu.CompilerParams(vmem_limit_bytes=60<<20),interpret=interpret,name="attn_bwd")(meta,q,k,v,do,o,lse)
+            own = [
+                [
+                    own[h][i]
+                    + dg(turned[:, chunk_rows(c, i)], slopes[h][:, i * SEG : (i + 1) * SEG], NN)
+                    for i in range(2)
+                ]
+                for h in range(2)
+            ]
+    total_q = [shared[h] + jnp.concatenate(own[h], axis=1) for h in range(2)]
+    row = lax.broadcasted_iota(jnp.int32, total_q[0].shape, 0)
+    dq_ref[...] = (jnp.where(row < 64, total_q[0], total_q[1]).T * 0.125).astype(BF)
+
+
+def attn_specs(rows, keys):
+    return (
+        pl.BlockSpec((rows, 128), lambda j, *unused: (0, j)),
+        pl.BlockSpec((keys, 128), lambda j, *unused: (0, j)),
+        pl.BlockSpec((1, 12 * SEG, rows), lambda j, *unused: (j, 0, 0)),
+    )
+
+
+def attn_fwd(meta, q, k, v):
+    rows, width = q.shape
+    pairs = width // 128
+    q_spec, k_spec, p_spec = attn_specs(rows, k.shape[0])
+    return call(
+        fwd_kernel,
+        "attn_fwd",
+        (pairs,),
+        [q_spec, k_spec, k_spec],
+        [
+            (q_spec, (q.shape, BF)),
+            (q_spec, (q.shape, F32)),
+            (p_spec, ((pairs, 12 * SEG, rows), BF)),
+        ],
+        prefetch=1,
+        flops=2 * 2 * 12 * 12 * SEG**3,
+        size=32 << 20,
+        args=(meta, q, k, v),
+    )
+
+
+def attn_bwd(q, k, v, do, o, inverse, p):
+    rows, width = q.shape
+    pairs = width // 128
+    q_spec, k_spec, p_spec = attn_specs(rows, k.shape[0])
+    return call(
+        bwd_kernel,
+        "attn_bwd",
+        (pairs,),
+        [q_spec, k_spec, k_spec, q_spec, q_spec, q_spec, p_spec],
+        [(q_spec, (q.shape, BF)), (k_spec, (k.shape, BF)), (k_spec, (k.shape, BF))],
+        flops=4 * 2 * 12 * 12 * SEG**3,
+        size=40 << 20,
+        args=(q, k, v, do, o, inverse, p),
+    )
 
 
 def row_norm(values):
@@ -505,73 +542,100 @@
     )
 
 
-def project_kernel(a_ref, b_ref, c_ref, d_ref, small_ref, weight_ref, q_ref, k_ref, v_ref, n_ref):
+def turn_kernel(value_ref, turned_ref, sum_ref):
+    turned_ref[...] = value_ref[...].T
+    sum_ref[...] = jnp.sum(value_ref[...].astype(F32), axis=0, keepdims=True)
+
+
+def turn(value):
+    rows, width = value.shape
+    return call(
+        turn_kernel,
+        "turn",
+        (1,),
+        [whole(value.shape)],
+        [
+            (whole((width, rows)), ((width, rows), BF)),
+            (whole((1, width)), ((1, width), F32)),
+        ],
+        args=(value,),
+    )
+
+
+def select_source(step, sources, kept):
+    for i, ref in enumerate(sources):
+
+        @pl.when(step == i)
+        def _(ref=ref):
+            kept[...] = ref[...]
+
+    return row_norm(kept[...].astype(F32))[0]
+
+
+def project_kernel(a_ref, b_ref, c_ref, d_ref, small_ref, weight_ref, q_ref, k_ref, v_ref, n_ref, kept):
     step = pl.program_id(0)
     width = a_ref.shape[1]
-
-    def run(ref, last):
-        unit, unused = row_norm(ref[...].astype(F32))
-        normed = (unit * small_ref[0:1] + small_ref[2:3]).astype(BF)
-        n_ref[...] = normed
-        k_ref[...] = dg(normed, weight_ref[:, width : 2 * width], NN).astype(BF)
-        v_ref[...] = (dg(normed, weight_ref[:, 2 * width :], NN) + small_ref[5:6]).astype(BF)
-        if last:
-            q_ref[...] = (dg(normed, weight_ref[:, :width], NN) + small_ref[4:5]).astype(BF)
-
-    for i, ref in enumerate((a_ref, b_ref, c_ref, d_ref)):
-
-        @pl.when(step == i)
-        def _(ref=ref, i=i):
-            run(ref, i == 3)
+    unit = select_source(step, (a_ref, b_ref, c_ref, d_ref), kept)
+    normed = (unit * small_ref[0:1] + small_ref[2:3]).astype(BF)
+    n_ref[...] = normed
+    k_ref[...] = dg(normed, weight_ref[:, width : 2 * width], NN).astype(BF)
+    v_ref[...] = (dg(normed, weight_ref[:, 2 * width :], NN) + small_ref[5:6]).astype(BF)
+
+    @pl.when(step == pl.num_programs(0) - 1)
+    def _():
+        q_ref[...] = (dg(normed, weight_ref[:, :width], NN) + small_ref[4:5]).astype(BF)
 
 
 def project(sources, small, qkv):
     tokens, width = sources[0].shape
+    count = len(sources)
     block = pl.BlockSpec((tokens, width), lambda i: (i, 0))
-    tall = ((4 * tokens, width), BF)
+    tall = ((count * tokens, width), BF)
     return call(
         project_kernel,
         "project",
-        (4,),
-        [whole((tokens, width))] * 4 + [whole(small.shape), whole(qkv.shape)],
+        (count,),
+        [whole((tokens, width))] * count + [whole(small.shape), whole(qkv.shape)],
         [(whole((tokens, width)), ((tokens, width), BF)), (block, tall), (block, tall), (block, tall)],
-        flops=2 * 9 * tokens * width * width,
+        scratch=[pltpu.VMEM((tokens, width), BF)],
+        flops=2 * (2 * count + 1) * tokens * width * width,
         args=(*sources, small, qkv),
     )
 
 
-def unproject_kernel(a_ref, b_ref, c_ref, dk_ref, dv_ref, small_ref, weight_ref, part_ref, terms_ref):
+def unproject_kernel(
+    a_ref, b_ref, c_ref, dk_ref, dv_ref, k_ref, v_ref, part_ref, terms_ref, kept
+):
     step = pl.program_id(0)
-    width = a_ref.shape[1]
 
     @pl.when(step == 0)
     def _():
         terms_ref[...] = jnp.zeros_like(terms_ref)
 
     dk, dv = dk_ref[...], dv_ref[...]
-    grad = dg(dk, weight_ref[:, width : 2 * width], NT) + dg(dv, weight_ref[:, 2 * width :], NT)
+    grad = dg(dk, k_ref[...], NT) + dg(dv, v_ref[...], NT)
     part_ref[...] = grad.astype(BF)
+    unit = select_source(step, (a_ref, b_ref, c_ref), kept)
+    terms_ref[0:1] += jnp.sum(grad * unit, axis=0, keepdims=True)
     terms_ref[1:2] += jnp.sum(grad, axis=0, keepdims=True)
     terms_ref[2:3] += jnp.sum(dv.astype(F32), axis=0, keepdims=True)
-    for i, ref in enumerate((a_ref, b_ref, c_ref)):
-
-        @pl.when(step == i)
-        def _(ref=ref):
-            unit, unused = row_norm(ref[...].astype(F32))
-            terms_ref[0:1] += jnp.sum(grad * unit, axis=0, keepdims=True)
-
-
-def unproject(sources, dk, dv, small, qkv):
+
+
+def unproject(sources, dk, dv, qkv):
     tokens, width = sources[0].shape
+    count = len(sources)
     block = pl.BlockSpec((tokens, width), lambda i: (i, 0))
     return call(
         unproject_kernel,
         "unproject",
-        (3,),
-        [whole((tokens, width))] * 3 + [block, block, whole(small.shape), whole(qkv.shape)],
-        [(block, ((3 * tokens, width), BF)), (whole((8, width)), ((8, width), F32))],
-        flops=2 * 6 * tokens * width * width,
-        args=(*sources, dk, dv, small, qkv),
+        (count,),
+        [whole((tokens, width))] * count
+        + [block, block]
+        + [pl.BlockSpec((width, width), lambda i, n=n: (0, n)) for n in (1, 2)],
+        [(block, ((count * tokens, width), BF)), (whole((8, width)), ((8, width), F32))],
+        scratch=[pltpu.VMEM((tokens, width), BF)],
+        flops=2 * 2 * count * tokens * width * width,
+        args=(*sources, dk, dv, qkv, qkv),
     )
 
 
@@ -653,27 +717,27 @@
 def finish_kernel(
     meta, trunk_ref, near_ref, far_ref, own_ref, mixed_ref, tokens_ref, small_ref, out_ref
 ):
-    received = []
-    for i in range(2):
-        slot = meta[1 + i]
-        place = pl.ds(pl.multiple_of((jnp.maximum(slot, 0) & 1) * SEG, SEG), SEG)
-        branch = jnp.where(slot >= 2, far_ref[place, :], near_ref[place, :]).astype(F32)
-        branch = jnp.where(slot >= 0, branch, 0.0)
-        trunk = trunk_ref[i * SEG : (i + 1) * SEG, :].astype(F32)
-        received.append(jnp.where(meta[0] == 0, trunk, branch))
-    grad = own_ref[...] + jnp.concatenate(received, axis=0)
+    slot = meta[1 + pl.program_id(0)]
+    place = pl.ds(pl.multiple_of((jnp.maximum(slot, 0) & 1) * SEG, SEG), SEG)
+    branch = jnp.where(slot >= 2, far_ref[place, :], near_ref[place, :]).astype(F32)
+    branch = jnp.where(slot >= 0, branch, 0.0)
+    trunk = trunk_ref[...].astype(F32)
+    grad = own_ref[...] + jnp.where(meta[0] == 0, trunk, branch)
     unit, scale = row_norm(tokens_ref[...].astype(F32))
     back = row_norm_back(unit, scale, grad * small_ref[0:1])
     out_ref[...] = (mixed_ref[...] + back).astype(BF)
 
 
 def finish(meta, trunk, near, far, own, mixed, tokens, small):
+    width = tokens.shape[1]
+    part = pl.BlockSpec((SEG, width), lambda i, meta: (i, 0))
+    full = whole(near.shape)
     return call(
         finish_kernel,
         "finish",
-        (1,),
-        [whole(x.shape) for x in (trunk, near, far, own, mixed, tokens, small)],
-        [(whole(tokens.shape), (tokens.shape, BF))],
+        (2,),
+        [part, full, full, part, part, part, whole(small.shape)],
+        [(part, (tokens.shape, BF))],
         prefetch=1,
         args=(meta, trunk, near, far, own, mixed, tokens, small),
     )[0]
@@ -687,9 +751,10 @@
 
 
 def feed_kernel(
-    tokens_ref, attended_ref, out_ref, small_ref, upstream_ref, up_ref, down_ref, shift_ref,
+    tokens_ref, attended_ref, out_ref, small_ref, upstream_ref, upstream_t, summed_ref, up_ref, down_ref,
+    shift_ref,
     output_ref, grad_mixed_ref, grad_att_ref, grad_out_ref, sums_ref, terms_ref, grads_ref,
-    second_ref, second_t, upstream_t, mixed_ref, sum_ref, back_ref,
+    second_ref, second_t, mixed_ref, sum_ref, back_ref,
     up_slot, down_slot, up_sem, down_sem,
 ):
     step = pl.program_id(0)
@@ -706,7 +771,6 @@
         unit, unused = row_norm(mixed)
         second_ref[...] = (unit * small_ref[1:2] + small_ref[3:4]).astype(BF)
         second_t[...] = second_ref[...].T
-        upstream_t[...] = upstream_ref[...].T
         sum_ref[...] = jnp.zeros_like(sum_ref)
         back_ref[...] = jnp.zeros_like(back_ref)
 
@@ -777,12 +841,14 @@
         sums_ref[0:1] = jnp.sum(grad_second * unit, axis=0, keepdims=True)
         sums_ref[1:2] = jnp.sum(grad_second, axis=0, keepdims=True)
         sums_ref[2:3] = jnp.sum(grad_mixed, axis=0, keepdims=True)
-        sums_ref[3:4] = jnp.sum(upstream_f, axis=0, keepdims=True)
+        sums_ref[3:4] = summed_ref[...]
         up_copy(slot, step).wait()
         down_copy(slot, step).wait()
 
 
-def feed_forward(tokens_in, attended, w_out, small, upstream, up_weights, down_weights, shift):
+def feed_forward(
+    tokens_in, attended, w_out, small, upstream, turned, summed, up_weights, down_weights, shift
+):
     tokens, width = tokens_in.shape
     rows, cols, half, wide = down_weights.shape
     block = whole((tokens, width))
@@ -795,6 +861,8 @@
             whole((width, width)),
             whole(small.shape),
             block,
+            whole(turned.shape),
+            whole(summed.shape),
             pl.BlockSpec((rows, 2, half, wide), lambda r: (0, r, 0, 0)),
             pl.BlockSpec((1, cols, half, wide), lambda r: (r, 0, 0, 0)),
             pl.BlockSpec((1, 2 * wide), lambda r: (0, r)),
@@ -810,7 +878,6 @@
         ],
         scratch_shapes=[
             pltpu.VMEM((tokens, width), BF),
-            pltpu.VMEM((width, tokens), BF),
             pltpu.VMEM((width, tokens), BF),
             pltpu.VMEM((tokens, width), F32),
             pltpu.VMEM((tokens, width), F32),
@@ -840,7 +907,7 @@
         ),
         compiler_params=pltpu.CompilerParams(vmem_limit_bytes=60 << 20),
         name="feed_forward",
-    )(tokens_in, attended, w_out, small, upstream, up_weights, down_weights, shift)
+    )(tokens_in, attended, w_out, small, upstream, turned, summed, up_weights, down_weights, shift)
 
 
 def swap(value, axis, bit):
@@ -902,9 +969,18 @@
     return lax.ppermute(value, "col", full)
 
 
-def share_tokens(tokens, own_slot, level):
-    branch = placed(tokens, own_slot, (0, 1)) + swap(placed(tokens, own_slot, (2, 3)), "col", 1)
+def together(*values):
+    return lax.optimization_barrier(values)
+
+
+def share_tokens(tokens, cotangent, own_slot, level):
+    branch = placed(tokens, own_slot, (0, 1))
+    branch_in = swap(placed(tokens, own_slot, (2, 3)), "col", 1)
     hop = level_move(tokens, [(0, 2)])
+    branch_in, hop, cotangent = together(branch_in, hop, cotangent)
+    turned, summed = turn(cotangent)
+    branch_in, hop, turned = together(branch_in, hop, turned)
+    branch = branch + branch_in
     moved = level_move(
         jnp.where(level == 1, branch, jnp.where(level == 0, tokens, hop)), [(0, 1), (1, 2), (2, 3)]
     )
@@ -915,11 +991,14 @@
     down_two = level_move(branch + down, [(2, 1)])
     trunk_far = swap(trunk, "col", 1)
     branch = (branch_up + down) + (up_two + down_two)
-    return trunk, trunk_far, branch, swap(branch, "col", 1)
-
-
-def together(*values):
-    return lax.optimization_barrier(values)
+    return trunk, trunk_far, branch, swap(branch, "col", 1), turned, summed
+
+
+def total(*parts):
+    out = parts[0].astype(jnp.float32)
+    for value in parts[1:]:
+        out = out + value.astype(jnp.float32)
+    return out
 
 
 def tail_rounds(part, parent_slot, level, make_pieces, vectors_of):
@@ -1004,26 +1083,20 @@
 
     parent = parents[0]
     numbers = jnp.arange(SEGS, dtype=jnp.int32)
-    is_branch = (numbers >= 4) & (parent == 3)
-    slots = jnp.cumsum(is_branch.astype(jnp.int32)) - 1
-    own_parent = [parent[2 * col + i] for i in range(2)]
-    is_leaf = [(own_parent[i] >= 4) for i in range(2)]
-    own_slot = [
-        jnp.where(is_branch[2 * col + i], slots[2 * col + i] ^ (2 * side), -1) for i in range(2)
-    ]
-    parent_slot = [
-        jnp.where(is_leaf[i], slots[jnp.maximum(own_parent[i], 0)] ^ (2 * side), -1)
-        for i in range(2)
-    ]
-    meta = jnp.stack(
-        [
-            (col < 2).astype(jnp.int32),
-            col.astype(jnp.int32) * local_rows,
-            is_leaf[0].astype(jnp.int32),
-            is_leaf[1].astype(jnp.int32),
-            2 * side.astype(jnp.int32),
-        ]
-    )
+    is_branch = ((numbers >= 4) & (parent == 3)).astype(jnp.int32)
+
+    def pick(array, number):
+        return jnp.sum(jnp.where(numbers == number, array, 0))
+
+    def slot(number):
+        return jnp.sum(jnp.where(numbers < number, is_branch, 0)) ^ (2 * side)
+
+    own = [2 * col + i for i in range(2)]
+    own_parent = [pick(parent, number) for number in own]
+    is_leaf = [number >= 4 for number in own_parent]
+    own_slot = [jnp.where(pick(is_branch, number) > 0, slot(number), -1) for number in own]
+    parent_slot = [jnp.where(is_leaf[i], slot(own_parent[i]), -1) for i in range(2)]
+    meta = jnp.stack([2 * col, 2 * side] + [leaf.astype(jnp.int32) for leaf in is_leaf])
 
     narrow, wide = w_up.shape
     with jax.named_scope("gather_early_weights"):
@@ -1048,7 +1121,9 @@
         ff_shift = vectors[:, 8:].reshape(1, -1).astype(jnp.float32)
         full_qkv, full_out = join_pieces(early, narrow)
     with jax.named_scope("gather_tokens"):
-        trunk, trunk_far, branch, branch_far = share_tokens(tokens, own_slot, level)
+        trunk, trunk_far, branch, branch_far, turned, summed = share_tokens(
+            tokens, cotangent, own_slot, level
+        )
         branch = jnp.concatenate([branch, branch_far], axis=0)
         parent_tokens = jnp.concatenate(
             [
@@ -1064,10 +1139,15 @@
 
     sources = (trunk, trunk_far, parent_tokens, tokens)
     queries, key_rows, value_rows, normed = project(sources, small, full_qkv)
-    attended, log_total = attn_fwd(meta, queries, key_rows, value_rows)
+    attended, inverse, chances = attn_fwd(meta, queries, key_rows, value_rows)
     output, grad_mixed, grad_att, grad_out, sums, ff_terms, late_grads = feed_forward(
-        tokens, attended, full_out, small, cotangent, early, late, ff_shift
-    )
+        tokens, attended, full_out, small, cotangent, turned, summed, early, late, ff_shift
+    )
+    grad_q, grad_k, grad_v = attn_bwd(
+        queries, key_rows, value_rows, grad_att, attended, inverse, chances
+    )
+    late_grads, grad_k = together(late_grads, grad_k)
+    part, part_terms = unproject(sources[:3], grad_k, grad_v, full_qkv)
     with jax.named_scope("scatter_late_weights"):
         late_sum = lax.psum_scatter(
             late_grads.reshape(rows * cols, *late_grads.shape[2:]),
@@ -1080,10 +1160,6 @@
         grad_w_down = jnp.concatenate(
             [late_sum[up_rows : up_rows + down_rows], late_sum[up_rows + down_rows :]], axis=1
         ).T
-    grad_q, grad_k, grad_v = attn_bwd(
-        meta, queries, key_rows, value_rows, grad_att, attended, log_total
-    )
-    part, part_terms = unproject(sources[:3], grad_k, grad_v, small, full_qkv)
 
     def make_pieces(after):
         dq, dk, dv, unused = together(grad_q, grad_k, grad_v, after)

time: 426 us -> 425 us (level)
  waiting for transfers between devices: 209 us -> 199 us
  Pallas kernels: 116 us -> 125 us
    pallas_call x5 -> x8, Pallas kernels: 53.3 us -> 99 us  [call(): pl.pallas_call(kernel, grid_spec=grid_spec, out_shape=[jax.ShapeDtypeStru...]
    pallas_call x2 -> x0, Pallas kernels: 37.1 us -> none  [the longest x1 21.6 us: attn_bwd(): pl.pallas_call(bwd_kernel, grid_spec=gs, out_shape=[jax.ShapeDtypeStruct(...]
    all_gather x1, waiting for transfers between devices: 27.6 us -> 21.8 us  [tree_body(): late = lax.all_gather(late, ('row', 'col'), axis=0, tiled=False)]
  transfers between devices with their start and end apart: 31 -> 31, of which waited for: 12 -> 15; matrix products, arithmetic and copies ran while one was open for 7% -> 7% of each run, Pallas kernels for 21% -> 18%
where the time goes in v3:
time: 425 us; the launch traced here: 417 us
  waiting for transfers between devices  199 us (47%)
  Pallas kernels  125 us (29%)
  starting transfers between devices  33.1 us (8%)
  other arithmetic  29.6 us (7%)
  between operations  19.9 us (5%)
  local copies, waits for them, and re-layouts  10.7 us (3%)
    ppermute x15, waiting for transfers between devices, swap(): return lax.ppermute(value, axis, [(i, i ^ bit) for i in range(size)])  106 us
    pallas_call x8, Pallas kernels, call(): pl.pallas_call(kernel, grid_spec=grid_spec, out_shape=[jax.ShapeDtypeStru...  99 us
    ppermute x11, waiting for transfers between devices, level_move(): return lax.ppermute(value, 'col', full)  71.5 us
    pallas_call x1, Pallas kernels, feed_forward(): pl.pallas_call(feed_kernel, grid_spec=grid_spec, out_shape=[jax.ShapeDtyp...  25.7 us
    all_gather x1, waiting for transfers between devices, tree_body(): late = lax.all_gather(late, ('row', 'col'), axis=0, tiled=False)  21.8 us
    ppermute x15, starting transfers between devices, swap(): return lax.ppermute(value, axis, [(i, i ^ bit) for i in range(size)])  17.1 us
    ppermute x11, starting transfers between devices, level_move(): return lax.ppermute(value, 'col', full)  14.6 us
  transfers between devices with their start and end apart: 31, of which 15 were waited for; matrix products, arithmetic and copies ran while one was open for 7% of the time, Pallas kernels for 18%

profile of v3, /device:TPU:0, one launch (start us, length us, event | category | flops | bytes accessed | tf_op | source)
XLA Modules:
  0.0 417.0 jit_solution(11912784520513247749)
XLA Ops:
  7.2 0.8 reshape.78
  8.1 0.7 pad_maximum_fusion.5
  9.0 1.9 maximum_maximum_fusion
  10.9 0.9 fusion.22
  13.2 2.1 fusion.18
  18.1 0.9 pad_maximum_fusion
  19.0 2.9 collective-permute-start
  22.0 4.5 %collective-permute-start.1 = (bf16[512,768]{1,0:T(8,128)(2,1)S(1)}, bf16[512,768]{1,0:T(8,128)(2,1)S(1)}, u32[]{:S(2)}, u32[]{:S(2)}) collective-permute-start(bf16[512,768]{1,0:T(8,128)(2,1)S(1)} %copy-done), channel_id=1, source_target_pairs={{0,4},{1,5},{8,12},{9,13},{16,20},{17,21},{24,28},{25,29}} | collective-permute-start | bytes 2359304 | tf_op jit(solution)/shard_map/gather_tokens/ppermute | solution.py:969
  26.5 15.4 %collective-permute-done = bf16[512,768]{1,0:T(8,128)(2,1)S(1)} collective-permute-done((bf16[512,768]{1,0:T(8,128)(2,1)}, bf16[512,768]{1,0:T(8,128)(2,1)S(1)}, u32[]{:S(2)}, u32[]{:S(2)}) %collective-permute-start) | collective-permute-done | bytes 786464 | tf_op jit(solution)/shard_map/gather_tokens/ppermute | solution.py:915
  41.9 9.9 %collective-permute-done.1 = bf16[512,768]{1,0:T(8,128)(2,1)S(1)} collective-permute-done((bf16[512,768]{1,0:T(8,128)(2,1)S(1)}, bf16[512,768]{1,0:T(8,128)(2,1)S(1)}, u32[]{:S(2)}, u32[]{:S(2)}) %collective-permute-start.1) | collective-permute-done | bytes 786464 | tf_op jit(solution)/shard_map/gather_tokens/ppermute | solution.py:969
  51.8 2.3 turn.1
  54.1 2.4 select_select_fusion.1
  56.6 2.2 collective-permute-start.2
  58.8 0.7 collective-permute-start.4
  59.5 26.4 %collective-permute-done.2 = bf16[512,768]{1,0:T(8,128)(2,1)} collective-permute-done((bf16[512,768]{1,0:T(8,128)(2,1)}, bf16[512,768]{1,0:T(8,128)(2,1)}, u32[]{:S(2)}, u32[]{:S(2)}) %collective-permute-start.2) | collective-permute-done | bytes 786464 | tf_op jit(solution)/shard_map/gather_tokens/ppermute | solution.py:969
  85.9 2.2 fusion.21
  88.1 0.7 collective-permute-start.5
  88.8 0.8 collective-permute-start.6
  92.8 1.9 collective-permute-start.3
  95.3 15.0 %collective-permute-done.7 = bf16[512,768]{1,0:T(8,128)(2,1)S(1)} collective-permute-done((bf16[512,768]{1,0:T(8,128)(2,1)S(1)}, bf16[512,768]{1,0:T(8,128)(2,1)S(1)}, u32[]{:S(2)}, u32[]{:S(2)}) %collective-permute-start.7) | collective-permute-done | bytes 786464 | tf_op jit(solution)/shard_map/gather_tokens/ppermute | solution.py:915
  110.4 1.0 fusion.6
  111.4 0.9 pad_maximum_fusion.1.c_ref
  112.4 5.5 %join_pieces.1 = (bf16[768,2304]{1,0:T(8,128)(2,1)}, bf16[768,768]{1,0:T(8,128)(2,1)}) custom-call(bf16[4,8,400,384]{3,2,1,0:T(8,128)(2,1)} %bitcast.53), custom_call_target="tpu_custom_call" | custom-call | bytes 16777216 | tf_op jit(solution)/shard_map/gather_early_weights/join_pieces/pallas_call | solution.py:508
  117.8 0.8 slice.193
  120.1 3.8 collective-permute-done.3.b_ref
  123.9 0.9 copy-done.6
  124.8 12.6 %project.1 = (bf16[512,768]{1,0:T(8,128)(2,1)}, bf16[2048,768]{1,0:T(8,128)(2,1)}, bf16[2048,768]{1,0:T(8,128)(2,1)}, bf16[2048,768]{1,0:T(8,128)(2,1)}) custom-call(bf16[512,768]{1,0:T(8,128)(2,1)} %get-tuple-element.183.a_ref, bf16[512,768]{1,0:T(8,128)(2,1)} %copy-done.6, bf16[512,768]{1,0:T(8,128)(2,1)} %pad_maximum_fusion.1.c_ref, ...), custom_call_target="tpu_custom_call" | custom-call | flops 5435817984 | bytes 16777216 | tf_op jit(solution)/shard_map/project/pallas_call | solution.py:508
  137.5 21.9 %attn_fwd.1 = (bf16[512,768]{1,0:T(8,128)(2,1)}, f32[512,768]{1,0:T(8,128)}, bf16[6,3072,512]{2,1,0:T(8,128)(2,1)}) custom-call(s32[4]{0:T(128)} %pad_add_fusion.meta, bf16[512,768]{1,0:T(8,128)(2,1)} %get-tuple-element.89.q_ref, bf16[2048,768]{1,0:T(8,128)(2,1)} %get-tuple-element.90.k_ref, bf16[2048,768]{1,0:T(8,128)(2,1)} %get-tuple-element.91.v_ref), custom_call_target="tpu_custom_call" | custom-call | flops 9663676416 | bytes 33554432 | tf_op jit(solution)/shard_map/attn_fwd/pallas_call | solution.py:508
  159.4 21.8 %all-gather.7.cloned.1.call-done = bf16[6144,384]{1,0:T(8,128)(2,1)} async-done(((bf16[192,384]{1,0:T(8,128)(2,1)}), bf16[6144,384]{1,0:T(8,128)(2,1)}) %all-gather.7.cloned.1.call-update) | async-done | bytes 4718608 | tf_op jit(solution)/shard_map/gather_late_weights/all_gather | solution.py:1137
  181.2 25.7 %feed_forward.1 = (bf16[512,768]{1,0:T(8,128)(2,1)}, f32[512,768]{1,0:T(8,128)}, bf16[512,768]{1,0:T(8,128)(2,1)}, bf16[768,768]{1,0:T(8,128)(2,1)}, f32[8,768]{...) custom-call(bf16[512,768]{1,0:T(8,128)(2,1)} %tokens_ref.5, ...), custom_call_target="tpu_custom_call" | custom-call | flops 14495514624 | bytes 25165824 | tf_op jit(solution)/shard_map/feed_forward/pallas_call | solution.py:891
  206.9 22.9 %attn_bwd.1 = (bf16[512,768]{1,0:T(8,128)(2,1)}, bf16[2048,768]{1,0:T(8,128)(2,1)}, bf16[2048,768]{1,0:T(8,128)(2,1)}) custom-call(bf16[512,768]{1,0:T(8,128)(2,1)} %get-tuple-element.89.q_ref, bf16[2048,768]{1,0:T(8,128)(2,1)} %get-tuple-element.90.k_ref, bf16[2048,768]{1,0:T(8,128)(2,1)} %get-tuple-element.91.v_ref, ...), custom_call_target="tpu_custom_call" | custom-call | flops 19327352832 | bytes 41943040 | tf_op jit(solution)/shard_map/attn_bwd/pallas_call | solution.py:508
  230.4 10.4 %unproject.1 = (bf16[1536,768]{1,0:T(8,128)(2,1)}, f32[8,768]{1,0:T(8,128)}) custom-call(bf16[512,768]{1,0:T(8,128)(2,1)} %get-tuple-element.183.a_ref, bf16[512,768]{1,0:T(8,128)(2,1)} %copy-done.6, bf16[512,768]{1,0:T(8,128)(2,1)} %pad_maximum_fusion.1.c_ref, bf16[2048,768]{1,0:T(8,128)(2,1)} %get-tuple-element.110.dk_ref, ...), custom_call_target="tpu_custom_call" | custom-call | flops 3623878656 | bytes 16777216 | tf_op jit(solution)/shard_map/unproject/pallas_call | solution.py:508
  240.8 1.4 select_add_fusion.4
  244.1 1.5 collective-permute-start.8
  245.6 18.2 %weigh.1 = (bf16[16,192,384]{2,1,0:T(8,128)(2,1)}, bf16[16,192,384]{2,1,0:T(8,128)(2,1)}, f32[512,768]{1,0:T(8,128)}, f32[8,768]{1,0:T(8,128)}) custom-call(s32[3]{0:T(128)} %pad_add_fusion.2.me, bf16[512,768]{1,0:T(8,128)(2,1)} %get-tuple-element.109.dq_ref, bf16[2048,768]{1,0:T(8,128)(2,1)} %get-tuple-element.110.dk_ref, ...), custom_call_target="tpu_custom_call" | custom-call | flops 7247757312 | bytes 16777216 | tf_op jit(solution)/shard_map/sum_gradients/weigh/pallas_call | solution.py:508
  263.9 0.9 add.161
  265.7 0.7 collective-permute-start.10
  268.1 2.7 collective-permute-done.13
  270.8 15.7 %collective-permute-done.11 = bf16[512,768]{1,0:T(8,128)(2,1)S(1)} collective-permute-done((bf16[512,768]{1,0:T(8,128)(2,1)S(1)}, bf16[512,768]{1,0:T(8,128)(2,1)S(1)}, u32[]{:S(2)}, u32[]{:S(2)}) %collective-permute-start.11) | collective-permute-done | bytes 786464 | tf_op jit(solution)/shard_map/sum_gradients/ppermute | solution.py:915
  287.0 1.4 copy-done.3
  289.8 0.7 collective-permute-start.14
  290.5 1.0 collective-permute-start.15
  291.5 1.3 collective-permute-start.16
  292.8 1.5 collective-permute-start.18
  294.2 19.1 %collective-permute-done.18 = f32[20,768]{1,0:T(8,128)S(1)} collective-permute-done((f32[20,768]{1,0:T(8,128)S(1)}, f32[20,768]{1,0:T(8,128)S(1)}, u32[]{:S(2)}, u32[]{:S(2)}) %collective-permute-start.18) | collective-permute-done | bytes 61472 | tf_op jit(solution)/shard_map/sum_gradients/ppermute | solution.py:915
  313.3 32.6 %collective-permute-done.16 = bf16[512,768]{1,0:T(8,128)(2,1)S(1)} collective-permute-done((bf16[512,768]{1,0:T(8,128)(2,1)S(1)}, bf16[512,768]{1,0:T(8,128)(2,1)S(1)}, u32[]{:S(2)}, u32[]{:S(2)}) %collective-permute-start.16) | collective-permute-done | bytes 786464 | tf_op jit(solution)/shard_map/sum_gradients/ppermute | solution.py:969
  347.4 1.3 collective-permute-start.19
  348.7 1.5 collective-permute-start.20
  350.8 1.5 collective-permute-start.22
  352.3 27.5 %collective-permute-done.22 = f32[20,768]{1,0:T(8,128)} collective-permute-done((f32[20,768]{1,0:T(8,128)}, f32[20,768]{1,0:T(8,128)}, u32[]{:S(2)}, u32[]{:S(2)}) %collective-permute-start.22) | collective-permute-done | bytes 61472 | tf_op jit(solution)/shard_map/sum_gradients/ppermute | solution.py:915
  379.8 2.7 collective-permute-done.19
  382.4 0.9 add.181
  383.4 1.3 fusion.11
  386.2 2.0 collective-permute-start.24
  388.2 2.0 collective-permute-start.25
  390.2 2.6 collective-permute-done.26
  392.9 1.1 add_convert_fusion.2.trunk_ref
  394.0 5.1 %finish.1 = bf16[512,768]{1,0:T(8,128)(2,1)} custom-call(s32[3]{0:T(128)} %pad_add_fusion.1.meta, bf16[512,768]{1,0:T(8,128)(2,1)} %add_convert_fusion.2.trunk_ref, bf16[512,768]{1,0:T(8,128)(2,1)} %copy-done.1, bf16[512,768]{1,0:T(8,128)(2,1)} %collective-permute-done.20.far_ref, f32[512,768]{1,0:T(8,128)} %get-tuple-element.145.own_ref, ...), custom_call_target="tpu_custom_call" | custom-call | bytes 16777216 | tf_op jit(solution)/shard_map/finish/pallas_call | solution.py:508
  399.1 3.7 collective-permute-done.27
  405.6 1.1 fusion.8
  406.8 0.8 slice.205
  407.5 1.0 convert_element_type.301
  408.5 0.7 slice_bitcast_fusion
  409.3 0.7 maximum_bitcast_fusion
  (99 shorter events, 18.0 us)
Async XLA Ops:
  7.2 5.4 %copy-start.11 = (s32[1,16]{1,0:T(1,128)S(1)}, s32[1,16]{1,0:T(1,128)}, u32[]{:S(2)}) copy-start(s32[1,16]{1,0:T(1,128)} %param.12) | copy-start | bytes 196
  7.2 10.7 %copy-start = (bf16[512,768]{1,0:T(8,128)(2,1)S(1)}, bf16[512,768]{1,0:T(8,128)(2,1)}, u32[]{:S(2)}) copy-start(bf16[512,768]{1,0:T(8,128)(2,1)} %tokens_ref.5) | copy-start | bytes 2359300
  7.2 105.2 %all-gather.5.cloned.1.call-start = ((), (), s32[]{:S(2)}) async-start(), calls=%async_computation.2 | async-start | bytes 10137600 | tf_op jit(solution)/shard_map/gather_early_weights/all_gather | solution.py:1116
  10.8 170.3 %all-gather.7.cloned.1.call-start = ((), (), s32[]{:S(2)}) async-start(), calls=%async_computation.3 | async-start | bytes 4866048 | tf_op jit(solution)/shard_map/gather_late_weights/all_gather | solution.py:1137
  12.5 395.0 %reduce-scatter.2.cloned.1.call-start = ((), (), s32[]{:S(2)}) async-start(), calls=%async_computation.1 | async-start | bytes 9732096 | tf_op jit(solution)/shard_map/scatter_late_weights/reduce_scatter | solution.py:1152
  19.0 22.9 %collective-permute-start = (bf16[512,768]{1,0:T(8,128)(2,1)}, bf16[512,768]{1,0:T(8,128)(2,1)S(1)}, u32[]{:S(2)}, u32[]{:S(2)}) collective-permute-start(bf16[512,768]{1,0:T(8,128)(2,1)} %pad_maximum_fusion), channel_id=1, source_target_pairs={{0,1},{1,0},{2,3},{3,2},{4,5},{5,4},{6,7},{7,6},{8,9},{9,8},{10,11... | collective-permute-start | bytes 2359304 | tf_op jit(solution)/shard_map/gather_tokens/ppermute | solution.py:915
  22.0 29.8 %collective-permute-start.1 = (bf16[512,768]{1,0:T(8,128)(2,1)S(1)}, bf16[512,768]{1,0:T(8,128)(2,1)S(1)}, u32[]{:S(2)}, u32[]{:S(2)}) collective-permute-start(bf16[512,768]{1,0:T(8,128)(2,1)S(1)} %copy-done), channel_id=1, source_target_pairs={{0,4},{1,5},{8,12},{9,13},{16,20},{17,21},{24,28},{25,29}} | collective-permute-start | bytes 2359304 | tf_op jit(solution)/shard_map/gather_tokens/ppermute | solution.py:969
  41.9 12.2 %copy-start.5 = (bf16[512,768]{1,0:T(8,128)(2,1)}, bf16[512,768]{1,0:T(8,128)(2,1)S(1)}, u32[]{:S(2)}) copy-start(bf16[512,768]{1,0:T(8,128)(2,1)S(1)} %collective-permute-done) | copy-start | bytes 2359300
  56.6 29.3 %collective-permute-start.2 = (bf16[512,768]{1,0:T(8,128)(2,1)}, bf16[512,768]{1,0:T(8,128)(2,1)}, u32[]{:S(2)}, u32[]{:S(2)}) collective-permute-start(bf16[512,768]{1,0:T(8,128)(2,1)} %get-tuple-element.162), channel_id=1, source_target_pairs={{0,2},{1,3},{2,4},{3,5},{4,6},{5,7},{8,10},{9,11},{10,12},{11,13},... | collective-permute-start | bytes 2359304 | tf_op jit(solution)/shard_map/gather_tokens/ppermute | solution.py:969
  58.8 27.1 %collective-permute-start.4 = (bf16[512,768]{1,0:T(8,128)(2,1)S(1)}, bf16[512,768]{1,0:T(8,128)(2,1)S(1)}, u32[]{:S(2)}, u32[]{:S(2)}) collective-permute-start(bf16[512,768]{1,0:T(8,128)(2,1)S(1)} %get-tuple-element.163), channel_id=1, source_target_pairs={{6,4},{7,5},{14,12},{15,13},{22,20},{23,21},{30,28},{31,29}} | collective-permute-start | bytes 2359304 | tf_op jit(solution)/shard_map/gather_tokens/ppermute | solution.py:969
  88.1 1.6 collective-permute-start.5
  88.8 4.0 copy-start.2
  88.8 0.9 collective-permute-start.6
  89.8 20.5 %collective-permute-start.7 = (bf16[512,768]{1,0:T(8,128)(2,1)S(1)}, bf16[512,768]{1,0:T(8,128)(2,1)S(1)}, u32[]{:S(2)}, u32[]{:S(2)}) collective-permute-start(bf16[512,768]{1,0:T(8,128)(2,1)S(1)} %add_add_fusion), channel_id=1, source_target_pairs={{0,1},{1,0},{2,3},{3,2},{4,5},{5,4},{6,7},{7,6},{8,9},{9,8},{10,11... | collective-permute-start | bytes 2359304 | tf_op jit(solution)/shard_map/gather_tokens/ppermute | solution.py:915
  92.8 31.1 %collective-permute-start.3 = (bf16[512,768]{1,0:T(8,128)(2,1)S(1)}, bf16[512,768]{1,0:T(8,128)(2,1)S(1)}, u32[]{:S(2)}, u32[]{:S(2)}) collective-permute-start(bf16[512,768]{1,0:T(8,128)(2,1)S(1)} %copy-done.2), channel_id=1, source_target_pairs={{0,1},{1,0},{2,3},{3,2},{4,5},{5,4},{6,7},{7,6},{8,9},{9,8},{10,11... | collective-permute-start | bytes 2359304 | tf_op jit(solution)/shard_map/gather_tokens/ppermute | solution.py:915
  123.9 0.9 copy-start.6
  240.8 1.9 copy-start.4
  242.7 0.7 copy-start.10
  244.1 20.7 %collective-permute-start.8 = (bf16[512,768]{1,0:T(8,128)(2,1)S(1)}, bf16[512,768]{1,0:T(8,128)(2,1)S(1)}, u32[]{:S(2)}, u32[]{:S(2)}) collective-permute-start(bf16[512,768]{1,0:T(8,128)(2,1)S(1)} %get-tuple-element.105), channel_id=1, source_target_pairs={{0,1},{1,0},{2,3},{3,2},{4,5},{5,4},{6,7},{7,6},{8,9},{9,8},{10,11... | collective-permute-start | bytes 2359304 | tf_op jit(solution)/shard_map/sum_gradients/ppermute | solution.py:915
  245.6 18.3 %copy-start.8 = (f32[8,768]{1,0:T(8,128)S(1)}, f32[8,768]{1,0:T(8,128)}, u32[]{:S(2)}) copy-start(f32[8,768]{1,0:T(8,128)} %get-tuple-element.115) | copy-start | bytes 73732
  245.6 19.2 %copy-start.9 = (f32[8,768]{1,0:T(8,128)S(1)}, f32[8,768]{1,0:T(8,128)}, u32[]{:S(2)}) copy-start(f32[8,768]{1,0:T(8,128)} %get-tuple-element.117) | copy-start | bytes 73732
  263.9 1.8 copy-start.12
  265.7 20.7 %collective-permute-start.12 = (bf16[16,192,384]{2,1,0:T(8,128)(2,1)S(1)}, bf16[16,192,384]{2,1,0:T(8,128)(2,1)S(1)}, u32[]{:S(2)}, u32[]{:S(2)}) collective-permute-start(bf16[16,192,384]{2,1,0:T(8,128)(2,1)S(1)} %copy-done.12), channel_id=1, source_target_pairs={{0,8},{8,0},{16,24},{24,16},{1,9},{9,1},{17,25},{25,17},{2,10},{10... | collective-permute-start | bytes 7077896 | tf_op jit(solution)/shard_map/sum_gradients/ppermute | solution.py:915
  265.7 5.1 %collective-permute-start.10 = (bf16[512,768]{1,0:T(8,128)(2,1)S(1)}, bf16[512,768]{1,0:T(8,128)(2,1)S(1)}, u32[]{:S(2)}, u32[]{:S(2)}) collective-permute-start(bf16[512,768]{1,0:T(8,128)(2,1)S(1)} %add_convert_fusion.5), channel_id=1, source_target_pairs={{6,4},{7,5},{14,12},{15,13},{22,20},{23,21},{30,28},{31,29}} | collective-permute-start | bytes 2359304 | tf_op jit(solution)/shard_map/sum_gradients/ppermute | solution.py:969
  266.4 20.0 %collective-permute-start.11 = (bf16[512,768]{1,0:T(8,128)(2,1)S(1)}, bf16[512,768]{1,0:T(8,128)(2,1)S(1)}, u32[]{:S(2)}, u32[]{:S(2)}) collective-permute-start(bf16[512,768]{1,0:T(8,128)(2,1)S(1)} %get-tuple-element.120), channel_id=1, source_target_pairs={{0,1},{1,0},{2,3},{3,2},{4,5},{5,4},{6,7},{7,6},{8,9},{9,8},{10,11... | collective-permute-start | bytes 2359304 | tf_op jit(solution)/shard_map/sum_gradients/ppermute | solution.py:915
  267.1 19.4 %collective-permute-start.9 = (bf16[512,768]{1,0:T(8,128)(2,1)S(1)}, bf16[512,768]{1,0:T(8,128)(2,1)S(1)}, u32[]{:S(2)}, u32[]{:S(2)}) collective-permute-start(bf16[512,768]{1,0:T(8,128)(2,1)S(1)} %add_convert_fusion.5), channel_id=1, source_target_pairs={{2,4},{3,5},{10,12},{11,13},{18,20},{19,21},{26,28},{27,29}} | collective-permute-start | bytes 2359304 | tf_op jit(solution)/shard_map/sum_gradients/ppermute | solution.py:969
  267.8 3.0 collective-permute-start.13
  286.6 1.8 copy-start.3
  289.1 56.8 %collective-permute-start.17 = (bf16[8,192,384]{2,1,0:T(8,128)(2,1)S(1)}, bf16[8,192,384]{2,1,0:T(8,128)(2,1)S(1)}, u32[]{:S(2)}, u32[]{:S(2)}) collective-permute-start(bf16[8,192,384]{2,1,0:T(8,128)(2,1)S(1)} %get-tuple-element.132), channel_id=1, source_target_pairs={{0,16},{1,17},{2,18},{3,19},{4,20},{5,21},{6,22},{7,23},{8,9},{9,8... | collective-permute-start | bytes 3538952 | tf_op jit(solution)/shard_map/sum_gradients/ppermute | solution.py:926
  289.8 23.5 %collective-permute-start.14 = (bf16[512,768]{1,0:T(8,128)(2,1)S(1)}, bf16[512,768]{1,0:T(8,128)(2,1)S(1)}, u32[]{:S(2)}, u32[]{:S(2)}) collective-permute-start(bf16[512,768]{1,0:T(8,128)(2,1)S(1)} %get-tuple-element.129), channel_id=1, source_target_pairs={{4,6},{5,7},{12,14},{13,15},{20,22},{21,23},{28,30},{29,31}} | collective-permute-start | bytes 2359304 | tf_op jit(solution)/shard_map/sum_gradients/ppermute | solution.py:969
  290.5 22.8 %collective-permute-start.15 = (bf16[512,768]{1,0:T(8,128)(2,1)S(1)}, bf16[512,768]{1,0:T(8,128)(2,1)S(1)}, u32[]{:S(2)}, u32[]{:S(2)}) collective-permute-start(bf16[512,768]{1,0:T(8,128)(2,1)S(1)} %get-tuple-element.130), channel_id=1, source_target_pairs={{4,2},{5,3},{12,10},{13,11},{20,18},{21,19},{28,26},{29,27}} | collective-permute-start | bytes 2359304 | tf_op jit(solution)/shard_map/sum_gradients/ppermute | solution.py:969
  291.5 54.4 %collective-permute-start.16 = (bf16[512,768]{1,0:T(8,128)(2,1)S(1)}, bf16[512,768]{1,0:T(8,128)(2,1)S(1)}, u32[]{:S(2)}, u32[]{:S(2)}) collective-permute-start(bf16[512,768]{1,0:T(8,128)(2,1)S(1)} %add_convert_fusion.4), channel_id=1, source_target_pairs={{2,0},{3,1},{6,4},{7,5},{10,8},{11,9},{14,12},{15,13},{18,16},{19,... | collective-permute-start | bytes 2359304 | tf_op jit(solution)/shard_map/sum_gradients/ppermute | solution.py:969
  292.8 20.5 %collective-permute-start.18 = (f32[20,768]{1,0:T(8,128)S(1)}, f32[20,768]{1,0:T(8,128)S(1)}, u32[]{:S(2)}, u32[]{:S(2)}) collective-permute-start(f32[20,768]{1,0:T(8,128)S(1)} %add.166), channel_id=1, source_target_pairs={{0,16},{8,24},{16,0},{24,8},{1,17},{9,25},{17,1},{25,9},{2,18},{10... | collective-permute-start | bytes 184328 | tf_op jit(solution)/shard_map/sum_gradients/ppermute | solution.py:915
  347.4 46.6 %copy-start.1 = (bf16[512,768]{1,0:T(8,128)(2,1)}, bf16[512,768]{1,0:T(8,128)(2,1)S(1)}, u32[]{:S(2)}) copy-start(bf16[512,768]{1,0:T(8,128)(2,1)S(1)} %fusion.4.near_ref) | copy-start | bytes 2359300
  347.4 35.0 %collective-permute-start.19 = (bf16[512,768]{1,0:T(8,128)(2,1)S(1)}, bf16[512,768]{1,0:T(8,128)(2,1)S(1)}, u32[]{:S(2)}, u32[]{:S(2)}) collective-permute-start(bf16[512,768]{1,0:T(8,128)(2,1)S(1)} %add_convert_fusion.3), channel_id=1, source_target_pairs={{4,0},{5,1},{12,8},{13,9},{20,16},{21,17},{28,24},{29,25}} | collective-permute-start | bytes 2359304 | tf_op jit(solution)/shard_map/sum_gradients/ppermute | solution.py:969
  348.7 33.7 %collective-permute-start.20 = (bf16[512,768]{1,0:T(8,128)(2,1)S(1)}, bf16[512,768]{1,0:T(8,128)(2,1)}, u32[]{:S(2)}, u32[]{:S(2)}) collective-permute-start(bf16[512,768]{1,0:T(8,128)(2,1)S(1)} %fusion.4.near_ref), channel_id=1, source_target_pairs={{0,1},{1,0},{2,3},{3,2},{4,5},{5,4},{6,7},{7,6},{8,9},{9,8},{10,11... | collective-permute-start | bytes 2359304 | tf_op jit(solution)/shard_map/sum_gradients/ppermute | solution.py:915
  350.3 29.5 %collective-permute-start.21 = (bf16[4,192,384]{2,1,0:T(8,128)(2,1)S(1)}, bf16[4,192,384]{2,1,0:T(8,128)(2,1)}, u32[]{:S(2)}, u32[]{:S(2)}) collective-permute-start(bf16[4,192,384]{2,1,0:T(8,128)(2,1)S(1)} %get-tuple-element.141), channel_id=1, source_target_pairs={{0,1},{1,0},{2,3},{3,2},{4,5},{5,4},{6,7},{7,6},{8,24},{9,25},{10,... | collective-permute-start | bytes 1769480 | tf_op jit(solution)/shard_map/sum_gradients/ppermute | solution.py:926
  350.8 29.0 %collective-permute-start.22 = (f32[20,768]{1,0:T(8,128)}, f32[20,768]{1,0:T(8,128)}, u32[]{:S(2)}, u32[]{:S(2)}) collective-permute-start(f32[20,768]{1,0:T(8,128)} %add.173), channel_id=1, source_target_pairs={{0,1},{1,0},{2,3},{3,2},{4,5},{5,4},{6,7},{7,6},{8,9},{9,8},{10,11... | collective-permute-start | bytes 184328 | tf_op jit(solution)/shard_map/sum_gradients/ppermute | solution.py:915
  384.6 8.2 %collective-permute-start.26 = (f32[20,768]{1,0:T(8,128)S(1)}, f32[20,768]{1,0:T(8,128)S(1)}, u32[]{:S(2)}, u32[]{:S(2)}) collective-permute-start(f32[20,768]{1,0:T(8,128)S(1)} %add.181), channel_id=1, source_target_pairs={{0,4},{1,5},{2,6},{3,7},{4,0},{5,1},{6,2},{7,3},{8,12},{9,13},{10,... | collective-permute-start | bytes 184328 | tf_op jit(solution)/shard_map/sum_gradients/ppermute | solution.py:915
  385.8 19.5 %collective-permute-start.23 = (bf16[192,384]{1,0:T(8,128)(2,1)S(1)}, bf16[192,384]{1,0:T(8,128)(2,1)S(1)}, u32[]{:S(2)}, u32[]{:S(2)}) collective-permute-start(bf16[192,384]{1,0:T(8,128)(2,1)S(1)} %get-tuple-element.149), channel_id=1, source_target_pairs={{0,2},{1,3},{2,0},{3,1},{4,6},{5,7},{6,4},{7,5},{8,10},{9,11},{10,... | collective-permute-start | bytes 442376 | tf_op jit(solution)/shard_map/sum_gradients/ppermute | solution.py:915
  386.2 19.4 %collective-permute-start.24 = (bf16[192,384]{1,0:T(8,128)(2,1)S(1)}, bf16[192,384]{1,0:T(8,128)(2,1)}, u32[]{:S(2)}, u32[]{:S(2)}) collective-permute-start(bf16[192,384]{1,0:T(8,128)(2,1)S(1)} %get-tuple-element.150), channel_id=1, source_target_pairs={{0,4},{1,5},{2,6},{3,7},{4,0},{5,1},{6,2},{7,3},{8,12},{9,13},{10,... | collective-permute-start | bytes 442376 | tf_op jit(solution)/shard_map/sum_gradients/ppermute | solution.py:915
  388.2 17.4 %collective-permute-start.25 = (bf16[192,384]{1,0:T(8,128)(2,1)S(1)}, bf16[192,384]{1,0:T(8,128)(2,1)}, u32[]{:S(2)}, u32[]{:S(2)}) collective-permute-start(bf16[192,384]{1,0:T(8,128)(2,1)S(1)} %get-tuple-element.151), channel_id=1, source_target_pairs={{0,6},{1,7},{2,4},{3,5},{4,2},{5,3},{6,0},{7,1},{8,14},{9,15},{10,... | collective-permute-start | bytes 442376 | tf_op jit(solution)/shard_map/sum_gradients/ppermute | solution.py:915
  392.8 9.9 %collective-permute-start.27 = (f32[20,768]{1,0:T(8,128)S(1)}, f32[20,768]{1,0:T(8,128)S(1)}, u32[]{:S(2)}, u32[]{:S(2)}) collective-permute-start(f32[20,768]{1,0:T(8,128)S(1)} %add.185), channel_id=1, source_target_pairs={{0,2},{1,3},{2,0},{3,1},{4,6},{5,7},{6,4},{7,5},{8,10},{9,11},{10,... | collective-permute-start | bytes 184328 | tf_op jit(solution)/shard_map/sum_gradients/ppermute | solution.py:915
  406.7 3.3 copy-start.7
Sparse Core Ops, SparseCore 0:
  11.6 95.5 all-gather.4
  110.7 70.4 all-gather.6
  229.9 174.2 reduce-scatter.1
